TPU v7x, 32 devices: a whole 2x2x4 slice. The times are simulated.
32 devices in a mesh: fsdp: 2 (over x), context: 4 (over y, core), tensor: 4 (over z).
Axes of the slice: x: 2, y: 2, z: 4, core: 2. Of those that a mesh axis runs over, the one named last changes fastest.
Arguments:
- tokens: bfloat16 [4, 2560, 1024], P('fsdp', 'context'), may hold values from -6 to 6
- state: bfloat16 [4, 512, 1024], P('fsdp', 'context'), may hold values from -6 to 6
- parent: int32 [4, 20], P('fsdp'), may hold values from -1 to 11, as said below
- seg_length: int32 [4, 20], P('fsdp', 'context'), may hold values from 64 to 128, as said below
- cell_gate: float32 [1024], replicated, may hold values from 0.7 to 1
- norm1_gain: float32 [1024], replicated, may hold values from 0.5 to 1.5
- norm1_shift: float32 [1024], replicated, may hold values from -1.5 to 1.5
- w_query: bfloat16 [1024, 1024], P('fsdp', 'tensor'), may hold values from -0.1875 to 0.1875
- w_key: bfloat16 [1024, 1024], P('fsdp', 'tensor'), may hold values from -0.1875 to 0.1875
- w_value: bfloat16 [1024, 1024], P('fsdp', 'tensor'), may hold values from -0.1875 to 0.1875
- w_attn_out: bfloat16 [1024, 1024], P('tensor', 'fsdp'), may hold values from -0.75 to 0.75
- rel_bias: float32 [8, 32], P('tensor'), may hold values from -4 to 4
- norm2_gain: float32 [1024], replicated, may hold values from 0.5 to 1.5
- norm2_shift: float32 [1024], replicated, may hold values from -1.5 to 1.5
- w_in: bfloat16 [1024, 4096], P('fsdp', 'tensor'), may hold values from -0.1875 to 0.1875
- w_out: bfloat16 [4096, 1024], P('tensor', 'fsdp'), may hold values from -0.125 to 0.125
- cotangent: bfloat16 [4, 2560, 1024], P('fsdp', 'context'), may hold values from -6 to 6
Outputs:
- output: bfloat16 [4, 2560, 1024], P('fsdp', 'context')
- tokens_grad: bfloat16 [4, 2560, 1024], P('fsdp', 'context')
- state_grad: bfloat16 [4, 512, 1024], P('fsdp', 'context')
- grad_query: float32 [1024, 1024], P('fsdp', 'tensor')
- grad_key: float32 [1024, 1024], P('fsdp', 'tensor')
- grad_value: float32 [1024, 1024], P('fsdp', 'tensor')
- grad_attn_out: float32 [1024, 1024], P('tensor', 'fsdp')
- grad_rel_bias: float32 [8, 32], P('tensor')
- grad_norm1_gain: float32 [1024], replicated
- grad_norm1_shift: float32 [1024], replicated
- grad_norm2_gain: float32 [1024], replicated
- grad_norm2_shift: float32 [1024], replicated
- grad_in: float32 [1024, 4096], P('fsdp', 'tensor')
- grad_out: float32 [4096, 1024], P('tensor', 'fsdp')
- norms: float32 [3], replicated
Inputs may be any that keep to these rules, and one draw needn't show every extreme that they name: Segments 0 to 7 form a trunk, each the child of the one before, segment 0 with parent -1; the next 4 segments are each a child of a trunk segment; each remaining segment is a child of one of those branches, 2 to each branch. `seg_length`: A segment's valid tokens are its first ones; every trunk and branch segment has 128; leaves have 128 // 2 or more.
All inputs are finite; a program needn't handle non-finite values.
Results may differ from a plain program's by a relative error of at most 0.022.
Values may be sent and summed in bfloat16 or wider, within the bound.
No kernel may reach another device: no remote copies, remote signals or barrier semaphores. Data moves between devices by JAX's collectives and lax.ppermute only.
A program may use at most 192 MiB of HBM per device.

v0:
```python
import math

import jax
import jax.numpy as jnp
from jax import lax
from jax.sharding import PartitionSpec as P

WINDOW = 512
BUCKETS = 32
REACH = 128


TOP_PRECISION = lax.Precision.HIGHEST
norm_epsilon = 1e-05
masked_score = -1e30
gelu_coeff = 0.7978845608028654


def bucket_edges(bucket_total, far_reach, window):
    exact_count = bucket_total // 2
    boundaries = []
    current = 0
    for distance in range(window):
        if distance < exact_count:
            bucket = distance
        else:
            bucket = exact_count + int(
                math.log(distance / exact_count)
                / math.log(far_reach / exact_count)
                * (bucket_total - exact_count)
            )
            bucket = min(bucket, bucket_total - 1)
        while current < bucket:
            current = current + 1
            boundaries.append(distance)
    return boundaries


def level_tables(levels, segment, window, bucket_total, far_reach):
    boundaries = bucket_edges(bucket_total, far_reach, window)
    lev_index = jnp.arange(levels, dtype=jnp.int32)[:, None, None]
    query_pos = jnp.arange(segment, dtype=jnp.int32)[None, :, None]
    key_pos = jnp.arange(segment, dtype=jnp.int32)[None, None, :]
    distance = lev_index * segment + query_pos - key_pos
    inside = (distance >= 0) & (distance < window)
    bucket = jnp.zeros(distance.shape, jnp.int32)
    for boundary in boundaries:
        bucket = bucket + (distance >= boundary).astype(jnp.int32)
    one_hot = (
        bucket[None] == jnp.arange(bucket_total, dtype=jnp.int32)[:, None, None, None]
    ).astype(jnp.float32)
    return (inside, one_hot)


def ancestor_table(parents, segments, levels):
    hop_table = (parents[:, None] == jnp.arange(segments, dtype=jnp.int32)[None, :]).astype(
        jnp.float32
    )
    current = jnp.eye(segments, dtype=jnp.float32)
    tables = [current]
    for _unused in range(levels - 1):
        current = jnp.dot(current, hop_table, precision=TOP_PRECISION)
        tables.append(current)
    return jnp.stack(tables, axis=1)


def layer_norm(values, norm_gain, norm_shift):
    row_mean = jnp.mean(values, axis=-1, keepdims=True)
    centered = values - row_mean
    variance = jnp.mean(centered * centered, axis=-1, keepdims=True)
    return centered * lax.rsqrt(variance + norm_epsilon) * norm_gain + norm_shift


def gelu_tanh(values):
    return (
        0.5 * values * (1.0 + jnp.tanh(gelu_coeff * (values + 0.044715 * values * values * values)))
    )


def matrix_product(form, left, right):
    return jnp.einsum(form, left, right, preferred_element_type=jnp.float32)


def on_device(
    tokens,
    state,
    parent,
    seg_length,
    cell_gate,
    norm1_gain,
    norm1_shift,
    w_query,
    w_key,
    w_value,
    w_attn_out,
    rel_bias,
    norm2_gain,
    norm2_shift,
    w_in,
    w_out,
    cotangent,
):
    trees_here, rows_here, model_width = tokens.shape
    local_segs = seg_length.shape[1]
    segment = rows_here // local_segs
    all_segs = parent.shape[1]
    heads_here = rel_bias.shape[0]
    head_dim = w_query.shape[1] // heads_here
    levels = WINDOW // segment + 1
    score_factor = head_dim ** (-0.5)
    position = lax.axis_index("context")
    row_weights = (
        lax.all_gather(w_query, "fsdp", axis=0, tiled=True),
        lax.all_gather(w_key, "fsdp", axis=0, tiled=True),
        lax.all_gather(w_value, "fsdp", axis=0, tiled=True),
        lax.all_gather(w_in, "fsdp", axis=0, tiled=True),
    )
    col_weights = (
        lax.all_gather(w_attn_out, "fsdp", axis=1, tiled=True),
        lax.all_gather(w_out, "fsdp", axis=1, tiled=True),
    )
    query_w, key_matrix, value_w, in_w = row_weights
    attn_w, out_w = col_weights
    inputs = tokens.astype(jnp.float32)
    states = state.astype(jnp.float32)
    normed_full, norm_one_back = jax.vjp(layer_norm, inputs, norm1_gain, norm1_shift)
    normed = normed_full.astype(jnp.bfloat16)
    state_full, state_norm_back = jax.vjp(layer_norm, states, norm1_gain, norm1_shift)
    state_normalized = state_full.astype(jnp.bfloat16)
    queries = matrix_product("tnd,de->tne", normed, query_w).astype(jnp.bfloat16)
    key_rows = matrix_product("tnd,de->tne", normed, key_matrix).astype(jnp.bfloat16)
    value_rows = matrix_product("tnd,de->tne", normed, value_w).astype(jnp.bfloat16)
    state_keys = matrix_product("tmd,de->tme", state_normalized, key_matrix).astype(jnp.bfloat16)
    state_values = matrix_product("tmd,de->tme", state_normalized, value_w).astype(jnp.bfloat16)
    gathered = (
        lax.all_gather(key_rows, "context", axis=1, tiled=True),
        lax.all_gather(value_rows, "context", axis=1, tiled=True),
        lax.all_gather(state_keys, "context", axis=1, tiled=True),
        lax.all_gather(state_values, "context", axis=1, tiled=True),
    )
    keys_all, values_all, state_keys_all, state_values_all = gathered
    inside, one_hot = level_tables(levels, segment, WINDOW, BUCKETS, REACH)
    ancestors_all = jax.vmap(lambda parent_row: ancestor_table(parent_row, all_segs, levels))(
        parent
    )
    ancestors = lax.dynamic_slice_in_dim(ancestors_all, position * local_segs, local_segs, 1)
    exists = jnp.sum(ancestors, axis=3) > 0.5
    lev_index = jnp.arange(levels, dtype=jnp.int32)[None, None, :]
    limits = jnp.where(lev_index == 0, seg_length[:, :, None], jnp.where(exists, segment, 0))
    key_pos = jnp.arange(segment, dtype=jnp.int32)
    allowed = inside.transpose(1, 0, 2)[None, None, None] & (
        key_pos[None, None, None, None, None, :] < limits[:, :, None, None, :, None]
    )
    anc_low = ancestors.astype(jnp.bfloat16)
    key_anc = (
        matrix_product(
            "tslj,tjke->tslke", anc_low, keys_all.reshape(trees_here, all_segs, segment, -1)
        )
        .astype(jnp.bfloat16)
        .reshape(trees_here, local_segs, levels, segment, heads_here, head_dim)
    )
    value_ancestor = (
        matrix_product(
            "tslj,tjke->tslke", anc_low, values_all.reshape(trees_here, all_segs, segment, -1)
        )
        .astype(jnp.bfloat16)
        .reshape(trees_here, local_segs, levels, segment, heads_here, head_dim)
    )
    query_per_head = queries.reshape(trees_here, local_segs, segment, heads_here, head_dim)
    state_key_per_head = state_keys_all.reshape(trees_here, -1, heads_here, head_dim)
    state_value_per_head = state_values_all.reshape(trees_here, -1, heads_here, head_dim)
    bias_blocks = jnp.einsum("hb,blqk->hlqk", rel_bias, one_hot, precision=TOP_PRECISION)
    bias_view = bias_blocks.transpose(0, 2, 1, 3)[None, None]

    def score_blocks():
        raw_win = (
            matrix_product("tsqhd,tslkhd->tshqlk", query_per_head, key_anc) * score_factor
            + bias_view
        )
        raw_win = jnp.where(allowed, raw_win, masked_score)
        state_logits = (
            matrix_product("tsqhd,tmhd->tshqm", query_per_head, state_key_per_head) * score_factor
        )
        return (raw_win, state_logits)

    raw_win, state_logits = score_blocks()
    row_top = jnp.maximum(jnp.max(raw_win, axis=(4, 5)), jnp.max(state_logits, axis=4))
    row_total = jnp.sum(jnp.exp(raw_win - row_top[..., None, None]), axis=(4, 5)) + jnp.sum(
        jnp.exp(state_logits - row_top[..., None]), axis=4
    )
    log_total = row_top + jnp.log(row_total)
    window_probability = jnp.exp(raw_win - log_total[..., None, None]).astype(jnp.bfloat16)
    state_probability = jnp.exp(state_logits - log_total[..., None]).astype(jnp.bfloat16)
    attention_result = matrix_product(
        "tshqlk,tslkhd->tsqhd", window_probability, value_ancestor
    ) + matrix_product("tshqm,tmhd->tsqhd", state_probability, state_value_per_head)
    attention_result = attention_result.reshape(trees_here, rows_here, -1).astype(jnp.bfloat16)
    branch = lax.psum(
        matrix_product("tne,ed->tnd", attention_result, attn_w).astype(jnp.bfloat16), "tensor"
    ).astype(jnp.float32)
    gated_branch = cell_gate * branch
    hidden = inputs + gated_branch
    normed_two_full, norm_two_back = jax.vjp(layer_norm, hidden, norm2_gain, norm2_shift)
    normed_two = normed_two_full.astype(jnp.bfloat16)
    up_proj = matrix_product("tnd,df->tnf", normed_two, in_w)
    activ_full, gelu_back = jax.vjp(gelu_tanh, up_proj)
    activated = activ_full.astype(jnp.bfloat16)
    mlp_out = lax.psum(
        matrix_product("tnf,fd->tnd", activated, out_w).astype(jnp.bfloat16), "tensor"
    ).astype(jnp.float32)
    result = hidden + mlp_out
    squares = jnp.stack(
        [jnp.sum(inputs * inputs), jnp.sum(gated_branch * gated_branch), jnp.sum(mlp_out * mlp_out)]
    )
    row_back = (
        lax.all_gather(w_query, "fsdp", axis=0, tiled=True),
        lax.all_gather(w_key, "fsdp", axis=0, tiled=True),
        lax.all_gather(w_value, "fsdp", axis=0, tiled=True),
        lax.all_gather(w_in, "fsdp", axis=0, tiled=True),
    )
    col_back = (
        lax.all_gather(w_attn_out, "fsdp", axis=1, tiled=True),
        lax.all_gather(w_out, "fsdp", axis=1, tiled=True),
    )
    query_w, key_matrix, value_w, in_w = row_back
    attn_w, out_w = col_back
    grad_result = cotangent.astype(jnp.float32)
    grad_mlp = grad_result.astype(jnp.bfloat16)
    local_out = matrix_product("tnf,tnd->fd", activated, grad_mlp)
    grad_act = matrix_product("tnd,fd->tnf", grad_mlp, out_w)
    grad_up = gelu_back(grad_act)[0].astype(jnp.bfloat16)
    local_in = matrix_product("tnd,tnf->df", normed_two, grad_up)
    grad_normed_two = lax.psum(
        matrix_product("tnf,df->tnd", grad_up, in_w).astype(jnp.bfloat16), "tensor"
    ).astype(jnp.float32)
    grad_hidden_norm, grad_gain_two, grad_shift_two = norm_two_back(grad_normed_two)
    grad_hidden = grad_result + grad_hidden_norm
    grad_branch = (cell_gate * grad_hidden).astype(jnp.bfloat16)
    local_attn = matrix_product("tne,tnd->ed", attention_result, grad_branch)
    grad_attended = matrix_product("tnd,ed->tne", grad_branch, attn_w).astype(jnp.bfloat16)
    grad_heads = grad_attended.reshape(trees_here, local_segs, segment, heads_here, head_dim)
    raw_win, state_logits = score_blocks()
    prob_win_full = jnp.exp(raw_win - log_total[..., None, None])
    prob_state_full = jnp.exp(state_logits - log_total[..., None])
    window_probability = prob_win_full.astype(jnp.bfloat16)
    state_probability = prob_state_full.astype(jnp.bfloat16)
    grad_prob_win = matrix_product("tsqhd,tslkhd->tshqlk", grad_heads, value_ancestor)
    grad_prob_state = matrix_product("tsqhd,tmhd->tshqm", grad_heads, state_value_per_head)
    weighted = jnp.sum(prob_win_full * grad_prob_win, axis=(4, 5)) + jnp.sum(
        prob_state_full * grad_prob_state, axis=4
    )
    grad_win = (prob_win_full * (grad_prob_win - weighted[..., None, None])).astype(jnp.bfloat16)
    grad_state_score = (prob_state_full * (grad_prob_state - weighted[..., None])).astype(
        jnp.bfloat16
    )
    grad_blocks = jnp.sum(grad_win.astype(jnp.float32), axis=(0, 1))
    local_bias = jnp.einsum("hqlk,blqk->hb", grad_blocks, one_hot, precision=TOP_PRECISION)
    grad_query_heads = (
        matrix_product("tshqlk,tslkhd->tsqhd", grad_win, key_anc)
        + matrix_product("tshqm,tmhd->tsqhd", grad_state_score, state_key_per_head)
    ) * score_factor
    grad_key_anc = matrix_product("tshqlk,tsqhd->tslkhd", grad_win, query_per_head) * score_factor
    grad_value_anc = matrix_product("tshqlk,tsqhd->tslkhd", window_probability, grad_heads)
    grad_state_keys = (
        matrix_product("tshqm,tsqhd->tmhd", grad_state_score, query_per_head) * score_factor
    ).reshape(trees_here, -1, heads_here * head_dim)
    grad_state_values = matrix_product("tshqm,tsqhd->tmhd", state_probability, grad_heads).reshape(
        trees_here, -1, heads_here * head_dim
    )
    grad_keys_tree = jnp.einsum(
        "tslj,tslke->tjke",
        ancestors,
        grad_key_anc.reshape(trees_here, local_segs, levels, segment, -1),
        precision=TOP_PRECISION,
    ).reshape(trees_here, all_segs * segment, -1)
    grad_values_tree = jnp.einsum(
        "tslj,tslke->tjke",
        ancestors,
        grad_value_anc.reshape(trees_here, local_segs, levels, segment, -1),
        precision=TOP_PRECISION,
    ).reshape(trees_here, all_segs * segment, -1)
    portion_values = (
        lax.psum_scatter(
            grad_keys_tree.astype(jnp.bfloat16), "context", scatter_dimension=1, tiled=True
        ).astype(jnp.float32),
        lax.psum_scatter(
            grad_values_tree.astype(jnp.bfloat16), "context", scatter_dimension=1, tiled=True
        ).astype(jnp.float32),
        lax.psum_scatter(
            grad_state_keys.astype(jnp.bfloat16), "context", scatter_dimension=1, tiled=True
        ).astype(jnp.float32),
        lax.psum_scatter(
            grad_state_values.astype(jnp.bfloat16), "context", scatter_dimension=1, tiled=True
        ).astype(jnp.float32),
    )
    key_totals, value_totals, state_key_totals, state_value_totals = portion_values
    grad_keys_low = key_totals.astype(jnp.bfloat16)
    grad_values_low = value_totals.astype(jnp.bfloat16)
    grad_state_keys_reduced = state_key_totals.astype(jnp.bfloat16)
    grad_svalues_low = state_value_totals.astype(jnp.bfloat16)
    grad_queries_low = grad_query_heads.reshape(trees_here, rows_here, -1).astype(jnp.bfloat16)
    local_query = matrix_product("tnd,tne->de", normed, grad_queries_low)
    local_key = matrix_product("tnd,tne->de", normed, grad_keys_low) + matrix_product(
        "fkn,fkb->nb", state_normalized, grad_state_keys_reduced
    )
    local_value = matrix_product("tnd,tne->de", normed, grad_values_low) + matrix_product(
        "fkn,fkb->nb", state_normalized, grad_svalues_low
    )
    normed_part = (
        matrix_product("tne,de->tnd", grad_queries_low, query_w)
        + matrix_product("tne,de->tnd", grad_keys_low, key_matrix)
        + matrix_product("tne,de->tnd", grad_values_low, value_w)
    )
    state_portion = matrix_product(
        "iqw,lw->iql", grad_state_keys_reduced, key_matrix
    ) + matrix_product("iqw,lw->iql", grad_svalues_low, value_w)
    grad_normed, grad_state_normed = (
        lax.psum(normed_part.astype(jnp.bfloat16), "tensor").astype(jnp.float32),
        lax.psum(state_portion.astype(jnp.bfloat16), "tensor").astype(jnp.float32),
    )
    grad_inputs_norm, gain_first, shift_first = norm_one_back(grad_normed)
    grad_states, gain_second, shift_second = state_norm_back(grad_state_normed)
    tokens_grad = (grad_hidden + grad_inputs_norm).astype(jnp.bfloat16)
    state_grad = grad_states.astype(jnp.bfloat16)
    row_grads = (
        lax.psum_scatter(
            local_query.astype(jnp.bfloat16), "fsdp", scatter_dimension=0, tiled=True
        ).astype(jnp.float32),
        lax.psum_scatter(
            local_key.astype(jnp.bfloat16), "fsdp", scatter_dimension=0, tiled=True
        ).astype(jnp.float32),
        lax.psum_scatter(
            local_value.astype(jnp.bfloat16), "fsdp", scatter_dimension=0, tiled=True
        ).astype(jnp.float32),
        lax.psum_scatter(
            local_in.astype(jnp.bfloat16), "fsdp", scatter_dimension=0, tiled=True
        ).astype(jnp.float32),
    )
    col_grads = (
        lax.psum_scatter(
            local_attn.astype(jnp.bfloat16), "fsdp", scatter_dimension=1, tiled=True
        ).astype(jnp.float32),
        lax.psum_scatter(
            local_out.astype(jnp.bfloat16), "fsdp", scatter_dimension=1, tiled=True
        ).astype(jnp.float32),
    )
    weight_grads = (
        lax.psum(row_grads[0].astype(jnp.bfloat16), "context").astype(jnp.float32),
        lax.psum(row_grads[1].astype(jnp.bfloat16), "context").astype(jnp.float32),
        lax.psum(row_grads[2].astype(jnp.bfloat16), "context").astype(jnp.float32),
        lax.psum(row_grads[3].astype(jnp.bfloat16), "context").astype(jnp.float32),
        lax.psum(col_grads[0].astype(jnp.bfloat16), "context").astype(jnp.float32),
        lax.psum(col_grads[1].astype(jnp.bfloat16), "context").astype(jnp.float32),
    )
    small = lax.psum(
        (
            gain_first + gain_second,
            shift_first + shift_second,
            grad_gain_two,
            grad_shift_two,
            local_bias,
            squares,
        ),
        ("fsdp", "context"),
    )
    cell_count = (
        trees_here * rows_here * model_width * lax.axis_size("fsdp") * lax.axis_size("context")
    )
    norms = jnp.sqrt(small[5] / cell_count)
    return (
        result.astype(jnp.bfloat16),
        tokens_grad,
        state_grad,
        weight_grads[0],
        weight_grads[1],
        weight_grads[2],
        weight_grads[4],
        small[4],
        small[0],
        small[1],
        small[2],
        small[3],
        weight_grads[3],
        weight_grads[5],
        norms,
    )


def solution(mesh):
    return jax.shard_map(
        on_device,
        mesh=mesh,
        in_specs=(
            P("fsdp", "context", None),
            P("fsdp", "context", None),
            P("fsdp", None),
            P("fsdp", "context"),
            P(),
            P(),
            P(),
            P("fsdp", "tensor"),
            P("fsdp", "tensor"),
            P("fsdp", "tensor"),
            P("tensor", "fsdp"),
            P("tensor", None),
            P(),
            P(),
            P("fsdp", "tensor"),
            P("tensor", "fsdp"),
            P("fsdp", "context", None),
        ),
        out_specs=(
            P("fsdp", "context", None),
            P("fsdp", "context", None),
            P("fsdp", "context", None),
            P("fsdp", "tensor"),
            P("fsdp", "tensor"),
            P("fsdp", "tensor"),
            P("tensor", "fsdp"),
            P("tensor", None),
            P(),
            P(),
            P(),
            P(),
            P("fsdp", "tensor"),
            P("tensor", "fsdp"),
            P(),
        ),
        check_vma=False,
    )
```

profile of v0, /device:TPU:0, one launch (start us, length us, event | category | flops | bytes accessed | tf_op | source)
XLA Modules:
  0.0 1052.3 jit_solution(727202221016412516)
XLA Ops:
  13.0 9.9 all_gather.39
  25.9 8.2 all_gather.36
  44.3 10.4 all_gather.41
  54.8 10.1 all_gather.38
  71.9 10.7 %all_gather.42 = bf16[2,512,256]{2,1,0:T(8,128)(2,1)} all-gather(bf16[2,128,256]{2,1,0:T(8,128)(2,1)S(1)} %convolution_convert_fusion.5), channel_id=1, replica_groups=mesh['fsdp'=2,'context'=4,'tensor'=4] {'context'}, dimensions={1}, use_global_device_ids=true | all-gather | bytes 655360 | tf_op jit(solution)/shard_map/all_gather | solution.py:139
  93.9 11.2 %all_gather.43 = bf16[256,1024]{1,0:T(8,128)(2,1)} all-gather(bf16[256,512]{1,0:T(8,128)(2,1)} %param.27), channel_id=1, replica_groups=mesh['fsdp'=2,'context'=4,'tensor'=4] {'fsdp'}, dimensions={1}, use_global_device_ids=true | all-gather | bytes 786432 | tf_op jit(solution)/shard_map/all_gather | solution.py:119
  183.2 102.3 %all-reduce.8.cloned.1.call-done = bf16[2,640,1024]{2,1,0:T(8,128)(2,1)} async-done(((bf16[2,640,1024]{2,1,0:T(8,128)(2,1)}), bf16[2,640,1024]{2,1,0:T(8,128)(2,1)}) %all-reduce.8.cloned.1.call-update) | async-done | bytes 2621456 | tf_op jit(solution)/shard_map/psum | solution.py:198
  297.8 9.9 fusion.18
  313.6 103.1 %all-reduce.10.cloned.1.call-done = bf16[2,640,1024]{2,1,0:T(8,128)(2,1)} async-done(((bf16[2,640,1024]{2,1,0:T(8,128)(2,1)}), bf16[2,640,1024]{2,1,0:T(8,128)(2,1)}) %all-reduce.10.cloned.1.call-update) | async-done | bytes 2621456 | tf_op jit(solution)/shard_map/psum | solution.py:233
  453.7 10.0 copy.307
  463.7 12.4 %bitcast_convert_fusion = bf16[2,20,128,256]{3,1,2,0:T(8,128)(2,1)S(1)} fusion(f32[2,5,5,128,256]{4,1,2,3,0:T(8,128)} %copy.307, f32[2,5,5,20,1]{3,0,2,1,4:T(2,128)S(1)} %get-tuple-element.49), kind=kOutput, calls=%fused_computation.32 | convolution fusion | flops 394526720 | bytes 9179040 | tf_op jit(solution)/shard_map/tslj,tslke->tjke/dot_general | solution.py:276
  498.2 8.5 convert_reduce_fusion.3
  513.2 8.1 copy.299
  521.3 9.9 copy.301
  531.3 12.3 %bitcast_convert_fusion.1 = bf16[2,20,128,256]{3,1,2,0:T(8,128)(2,1)S(1)} fusion(f32[2,5,5,128,256]{4,1,2,3,0:T(8,128)} %copy.301, f32[2,5,5,20,1]{3,0,2,1,4:T(2,128)S(1)} %get-tuple-element.49), kind=kOutput, calls=%fused_computation.33 | convolution fusion | flops 394526720 | bytes 9179040 | tf_op jit(solution)/shard_map/tslj,tslke->tjke/dot_general | solution.py:270
  563.4 8.1 bitcast_convert_fusion.2
  600.1 14.0 %reduce-scatter.19.cloned.1.call-done = bf16[512,256]{1,0:T(8,128)(2,1)} async-done(((bf16[1024,256]{1,0:T(8,128)(2,1)}), bf16[512,256]{1,0:T(8,128)(2,1)}) %reduce-scatter.19.cloned.1.call-update) | async-done | bytes 262160 | tf_op jit(solution)/shard_map/reduce_scatter | solution.py:326
  614.1 34.7 %reduce-scatter.29.cloned.1.call-done = bf16[1024,512]{1,0:T(8,128)(2,1)} async-done(((bf16[1024,1024]{1,0:T(8,128)(2,1)}), bf16[1024,512]{1,0:T(8,128)(2,1)}) %reduce-scatter.29.cloned.1.call-update) | async-done | bytes 1048592 | tf_op jit(solution)/shard_map/reduce_scatter | solution.py:343
  648.8 34.6 %reduce-scatter.27.cloned.1.call-done = bf16[512,1024]{1,0:T(8,128)(2,1)} async-done(((bf16[1024,1024]{1,0:T(8,128)(2,1)}), bf16[512,1024]{1,0:T(8,128)(2,1)}) %reduce-scatter.27.cloned.1.call-update) | async-done | bytes 1048592 | tf_op jit(solution)/shard_map/reduce_scatter | solution.py:335
  683.5 16.8 %reduce-scatter.23.cloned.1.call-done = bf16[512,256]{1,0:T(8,128)(2,1)} async-done(((bf16[1024,256]{1,0:T(8,128)(2,1)}), bf16[512,256]{1,0:T(8,128)(2,1)}) %reduce-scatter.23.cloned.1.call-update) | async-done | bytes 262160 | tf_op jit(solution)/shard_map/reduce_scatter | solution.py:332
  700.3 17.3 %reduce-scatter.21.cloned.1.call-done = bf16[512,256]{1,0:T(8,128)(2,1)} async-done(((bf16[1024,256]{1,0:T(8,128)(2,1)}), bf16[512,256]{1,0:T(8,128)(2,1)}) %reduce-scatter.21.cloned.1.call-update) | async-done | bytes 262160 | tf_op jit(solution)/shard_map/reduce_scatter | solution.py:329
  731.9 57.8 %all-reduce.14.cloned.1.call-done = (bf16[512,256]{1,0:T(8,128)(2,1)}, bf16[512,256]{1,0:T(8,128)(2,1)}, bf16[512,256]{1,0:T(8,128)(2,1)}, bf16[256,512]{1,0:T(8...) async-done(((bf16[512,256]{1,0:T(8,128)(2,1)}, bf16[512,256]{1,0:T(8,128)(2,1)}, bf16[512,256]{1,0:T(8,128)(2,1)}, bf16[256,512]{1,0:T(8,128)(2,1)}, ...) | async-done | bytes 3145744 | tf_op jit(solution)/shard_map/psum | solution.py:348
  801.3 198.1 %all-reduce.12.cloned.1.call-done = (bf16[2,640,1024]{2,1,0:T(8,128)(2,1)}, bf16[2,640,1024]{2,1,0:T(8,128)(2,1)}, bf16[2,128,1024]{2,1,0:T(8,128)(2,1)}) async-done(((bf16[2,640,1024]{2,1,0:T(8,128)(2,1)}, bf16[2,640,1024]{2,1,0:T(8,128)(2,1)}, bf16[2,128,1024]{2,1,0:T(8,128)(2,1)}), (bf16[2,640,1024]{2,1,0:T(8,128)(2,1)}, bf16[2,640,1024]{2,1,0:T(8,128)(2,1)}, ...) | async-done | bytes 5767184 | tf_op jit(solution)/shard_map/psum | solution.py:208
  1019.8 24.6 %all-reduce = (f32[2,32]{1,0:T(2,128)}, f32[1024]{0:T(1024)}, f32[1024]{0:T(1024)}, f32[1024]{0:T(1024)}, f32[1024]{0:T(1024)}, /*index=5*/f32[3]{0:T(128)S(1)}) all-reduce(f32[2,32]{1,0:T(2,128)S(1)} %convolution_bitcast_fusion.11, f32[1024]{0:T(1024)S(1)} %add.571, ...), channel_id=1, replica_groups=mesh['fsdp'=2,'context'=4,'tensor'=4] {'fsdp','context'}, use_global_device_ids=true, to_apply=%region_37.38 | all-reduce | flops 4163 | bytes 33304 | tf_op jit(solution)/shard_map/psum | solution.py:355
  (314 shorter events, 292.7 us)
Async XLA Ops:
  8.1 104.4 %all-gather.7.cloned.1.call-start = ((), (), s32[]{:S(2)}) async-start(), calls=%async_computation.11 | async-start | bytes 3276800 | tf_op jit(solution)/shard_map/all_gather | solution.py:136
  25.9 114.2 %all-gather.5.cloned.1.call-start = ((), (), s32[]{:S(2)}) async-start(), calls=%async_computation.10 | async-start | bytes 3276800 | tf_op jit(solution)/shard_map/all_gather | solution.py:137
  37.0 248.5 %all-reduce.8.cloned.1.call-start = ((), (), s32[]{:S(2)}) async-start(), calls=%async_computation.12 | async-start | bytes 5242880 | tf_op jit(solution)/shard_map/psum | solution.py:198
  175.1 110.4 %copy-start.45 = (f32[1024]{0:T(1024)S(1)}, f32[1024]{0:T(1024)}, u32[]{:S(2)}) copy-start(f32[1024]{0:T(1024)} %param.21) | copy-start | bytes 12292
  181.6 108.1 %all-gather.9.cloned.1.call-start = ((), (), s32[]{:S(2)}) async-start(), calls=%async_computation.13 | async-start | bytes 3145728 | tf_op jit(solution)/shard_map/all_gather | solution.py:116
  182.2 115.6 %all-gather.11.cloned.1.call-start = ((), (), s32[]{:S(2)}) async-start(), calls=%async_computation.14 | async-start | bytes 3145728 | tf_op jit(solution)/shard_map/all_gather | solution.py:120
  182.8 106.9 %copy-start.48 = (f32[1024]{0:T(1024)S(1)}, f32[1024]{0:T(1024)}, u32[]{:S(2)}) copy-start(f32[1024]{0:T(1024)} %param.29) | copy-start | bytes 12292
  182.8 106.9 %copy-start.60 = (f32[1024]{0:T(1024)S(1)}, f32[1024]{0:T(1024)}, u32[]{:S(2)}) copy-start(f32[1024]{0:T(1024)} %param.30) | copy-start | bytes 12292
  182.8 233.9 %all-reduce.10.cloned.1.call-start = ((), (), s32[]{:S(2)}) async-start(), calls=%async_computation.15 | async-start | bytes 5242880 | tf_op jit(solution)/shard_map/psum | solution.py:233
  313.4 266.0 %reduce-scatter.17.cloned.1.call-start = ((), (), s32[]{:S(2)}) async-start(), calls=%async_computation.19 | async-start | bytes 655360 | tf_op jit(solution)/shard_map/reduce_scatter | solution.py:292
  444.6 137.2 %reduce-scatter.13.cloned.1.call-start = ((), (), s32[]{:S(2)}) async-start(), calls=%async_computation.17 | async-start | bytes 3276800 | tf_op jit(solution)/shard_map/reduce_scatter | solution.py:286
  478.2 107.6 %reduce-scatter.15.cloned.1.call-start = ((), (), s32[]{:S(2)}) async-start(), calls=%async_computation.18 | async-start | bytes 655360 | tf_op jit(solution)/shard_map/reduce_scatter | solution.py:289
  506.7 81.4 %reduce-scatter.11.cloned.1.call-start = ((), (), s32[]{:S(2)}) async-start(), calls=%async_computation.16 | async-start | bytes 3276800 | tf_op jit(solution)/shard_map/reduce_scatter | solution.py:283
  545.8 54.4 %reduce-scatter.25.cloned.1.call-start = ((), (), s32[]{:S(2)}) async-start(), calls=%async_computation.23 | async-start | bytes 786432 | tf_op jit(solution)/shard_map/reduce_scatter | solution.py:340
  549.3 64.9 %reduce-scatter.19.cloned.1.call-start = ((), (), s32[]{:S(2)}) async-start(), calls=%async_computation.20 | async-start | bytes 786432 | tf_op jit(solution)/shard_map/reduce_scatter | solution.py:326
  563.2 85.6 %reduce-scatter.29.cloned.1.call-start = ((), (), s32[]{:S(2)}) async-start(), calls=%async_computation.25 | async-start | bytes 3145728 | tf_op jit(solution)/shard_map/reduce_scatter | solution.py:343
  571.6 111.8 %reduce-scatter.27.cloned.1.call-start = ((), (), s32[]{:S(2)}) async-start(), calls=%async_computation.24 | async-start | bytes 3145728 | tf_op jit(solution)/shard_map/reduce_scatter | solution.py:335
  579.3 121.0 %reduce-scatter.23.cloned.1.call-start = ((), (), s32[]{:S(2)}) async-start(), calls=%async_computation.22 | async-start | bytes 786432 | tf_op jit(solution)/shard_map/reduce_scatter | solution.py:332
  585.7 131.9 %reduce-scatter.21.cloned.1.call-start = ((), (), s32[]{:S(2)}) async-start(), calls=%async_computation.21 | async-start | bytes 786432 | tf_op jit(solution)/shard_map/reduce_scatter | solution.py:329
  592.1 197.6 %all-reduce.14.cloned.1.call-start = ((), (), s32[]{:S(2)}) async-start(), calls=%async_computation.27 | async-start | bytes 6291456 | tf_op jit(solution)/shard_map/psum | solution.py:348
  600.1 120.0 %copy-start.47 = (bf16[2,128,256]{2,1,0:T(8,128)(2,1)S(1)}, bf16[2,128,256]{2,1,0:T(8,128)(2,1)}, u32[]{:S(2)}) copy-start(bf16[2,128,256]{2,1,0:T(8,128)(2,1)} %reduce-scatter.15.cloned.1.call-done) | copy-start | bytes 393220
  717.7 281.8 %all-reduce.12.cloned.1.call-start = ((), (), s32[]{:S(2)}) async-start(), calls=%async_computation.26 | async-start | bytes 11534336 | tf_op jit(solution)/shard_map/psum | solution.py:208
  789.7 211.3 %copy-start.55 = (f32[2,128]{1,0:T(2,128)S(1)}, f32[2,128]{1,0:T(2,128)}, u32[]{:S(2)}) copy-start(f32[2,128]{1,0:T(2,128)} %copy-done.54) | copy-start | bytes 3076
  801.3 205.5 %copy-start.50 = (f32[2,640]{1,0:T(2,128)S(1)}, f32[2,640]{1,0:T(2,128)}, u32[]{:S(2)}) copy-start(f32[2,640]{1,0:T(2,128)} %copy-done.49) | copy-start | bytes 15364
  (62 other events, 432.9 us)
Sparse Core Ops, SparseCore 0:
  26.0 29.8 all-gather.6
  58.0 28.3 all-gather.4
  181.7 103.7 all-reduce.7
  313.5 103.1 all-reduce.9
  444.7 20.6 reduce-scatter.16
  478.3 33.6 reduce-scatter.12
  514.5 21.6 reduce-scatter.14
  545.9 34.0 reduce-scatter.10
  582.2 14.5 reduce-scatter.24
  599.6 14.5 reduce-scatter.18
  617.0 31.8 reduce-scatter.28
  651.6 31.8 reduce-scatter.26
  685.7 14.5 reduce-scatter.22
  703.0 14.5 reduce-scatter.20
  720.3 69.3 all-reduce.13
  792.7 206.7 all-reduce.11
Sparse Core Ops, SparseCore 1:
  183.6 32.6 all-gather.8
  217.6 32.9 all-gather.10
where the time goes:
time: 1060 us; the launch traced here: 1050 us
  waiting for transfers between devices  580 us (55%)
  matrix products  185 us (17%)
  local copies, waits for them, and re-layouts  106 us (10%)
  blocking collectives  85 us (8%)
  other arithmetic  77.2 us (7%)
  between operations  16.8 us (2%)
    psum x1, waiting for transfers between devices, on_device(): lax.psum(matrix_product('tnf,fd->tnd', activated, out_w).astype(jnp.bfloa...  198 us
    dot_general x36, matrix products, matrix_product(): return jnp.einsum(form, left, right, preferred_element_type=jnp.float32)  142 us
    psum x1, waiting for transfers between devices, on_device(): lax.psum(matrix_product('tnf,df->tnd', grad_up, in_w).astype(jnp.bfloat16...  103 us
    psum x1, waiting for transfers between devices, on_device(): lax.psum(matrix_product('tne,ed->tnd', attention_result, attn_w).astype(j...  102 us
    psum x1, waiting for transfers between devices, on_device(): lax.psum(row_grads[0].astype(jnp.bfloat16), 'context').astype(jnp.float32)  57.8 us
    reduce_scatter x1, waiting for transfers between devices, on_device(): lax.psum_scatter(local_out.astype(jnp.bfloat16), 'fsdp', scatter_dimensio...  34.7 us
    reduce_scatter x1, waiting for transfers between devices, on_device(): lax.psum_scatter(local_in.astype(jnp.bfloat16), 'fsdp', scatter_dimension...  34.6 us
    psum x1, blocking collectives, on_device(): lax.psum((gain_first + gain_second, shift_first + shift_second, grad_gain...  24.6 us
  transfers between devices with their start and end apart: 18, of which 9 were waited for; matrix products, arithmetic and copies ran while one was open for 24% of the time, Pallas kernels for 0%

commit v1 on v0

v1 whole, which is shorter than its diff:
```python
import functools
import math

import jax
import jax.numpy as jnp
from jax import lax
from jax.experimental import pallas as pl
from jax.experimental.pallas import tpu as pltpu
from jax.sharding import PartitionSpec as P

WINDOW = 512
BUCKETS = 32
REACH = 128
EPSILON = 1e-05
MASKED = -1e30
GELU_C = 0.7978845608028654
GELU_A = 0.044715
BF = jnp.bfloat16
F32 = jnp.float32


def bucket_edges(bucket_total, far_reach, window):
    exact_count = bucket_total // 2
    boundaries = []
    current = 0
    for distance in range(window):
        if distance < exact_count:
            bucket = distance
        else:
            bucket = exact_count + int(
                math.log(distance / exact_count)
                / math.log(far_reach / exact_count)
                * (bucket_total - exact_count)
            )
            bucket = min(bucket, bucket_total - 1)
        while current < bucket:
            current = current + 1
            boundaries.append(distance)
    return boundaries


EDGES = bucket_edges(BUCKETS, REACH, WINDOW)


def mm(left, right):
    return lax.dot_general(left, right, (((1,), (0,)), ((), ())), preferred_element_type=F32)


def mm_nt(left, right):
    return lax.dot_general(left, right, (((1,), (1,)), ((), ())), preferred_element_type=F32)


def mm_tn(left, right):
    return lax.dot_general(left, right, (((0,), (0,)), ((), ())), preferred_element_type=F32)


def bias_tables(rb_ref, h, levels, seg, bm_ref):
    row = lax.broadcasted_iota(jnp.int32, (seg, seg), 0)
    col = lax.broadcasted_iota(jnp.int32, (seg, seg), 1)
    for lev in range(levels):
        dist = lev * seg + row - col
        low, high = lev * seg - (seg - 1), lev * seg + seg - 1
        if low >= EDGES[-1]:
            val = jnp.full((seg, seg), rb_ref[h, BUCKETS - 1], F32)
        else:
            val = jnp.full((seg, seg), rb_ref[h, 0], F32)
            for i, edge in enumerate(EDGES):
                if edge <= high:
                    val = jnp.where(dist >= edge, rb_ref[h, i + 1], val)
        if low < 0:
            val = jnp.where(dist >= 0, val, MASKED)
        if high >= WINDOW:
            val = jnp.where(dist < WINDOW, val, MASKED)
        bm_ref[:, lev * seg : (lev + 1) * seg] = val


def chain(par_ref, t, first, levels, all_segs, local_segs, ctx):
    out = []
    anc = first
    for lev in range(levels):
        if lev > 0:
            up = par_ref[t, jnp.maximum(anc, 0)]
            anc = jnp.where(anc >= 0, up, -1)
        safe = jnp.maximum(anc, 0)
        owner = lax.div(safe, local_segs)
        out.append((anc >= 0, jnp.bitwise_xor(owner, ctx), safe - owner * local_segs))
    return out


def scores_of(q, kw_ref, bm_ref, line, length, levels, seg, factor):
    win = levels * seg
    col = lax.broadcasted_iota(jnp.int32, (1, seg), 1)
    raw = mm_nt(q, kw_ref[...]) * factor
    parts = []
    for lev in range(levels):
        part = raw[:, lev * seg : (lev + 1) * seg] + bm_ref[:, lev * seg : (lev + 1) * seg]
        if lev == 0:
            part = part + jnp.where(col < length, 0.0, MASKED)
        else:
            part = part + jnp.where(line[lev][0], 0.0, MASKED)
        parts.append(part)
    parts.append(raw[:, win:])
    return jnp.concatenate(parts, axis=1)


def fill_sources(parts_k, parts_v, kall, vall, kw, vw, rows, win):
    for b in range(len(parts_k)):
        for src, dst, wide in ((parts_k[b], kall, kw), (parts_v[b], vall, vw)):
            dst[b] = src[0, :rows, :]
            n = src.shape[1] - rows
            wide[win + b * n : win + (b + 1) * n, :] = src[0, rows:, :]


def fetch_window(line, kall, vall, kw, vw, seg):
    for lev, (_, part, block) in enumerate(line):
        start = pl.multiple_of(block * seg, seg)
        kw[lev * seg : (lev + 1) * seg, :] = kall[part, pl.ds(start, seg), :]
        vw[lev * seg : (lev + 1) * seg, :] = vall[part, pl.ds(start, seg), :]


def attend_kernel(dims, par_ref, len_ref, ctx_ref, rb_ref, q_ref, *refs):
    levels, seg, local_segs, all_segs, factor = dims
    parts_k, parts_v = refs[0:4], refs[4:8]
    att_ref, lse_ref, kall, vall, kw, vw, bm = refs[8:]
    t, h = pl.program_id(0), pl.program_id(1)
    ctx = ctx_ref[0]
    rows, win = local_segs * seg, levels * seg
    bias_tables(rb_ref, h, levels, seg, bm)
    fill_sources(parts_k, parts_v, kall, vall, kw, vw, rows, win)

    def one(s, carry):
        line = chain(par_ref, t, ctx * local_segs + s, levels, all_segs, local_segs, ctx)
        fetch_window(line, kall, vall, kw, vw, seg)
        at = pl.ds(pl.multiple_of(s * seg, seg), seg)
        score = scores_of(q_ref[0, at, :], kw, bm, line, len_ref[t, s], levels, seg, factor)
        top = jnp.max(score, axis=1, keepdims=True)
        prob = jnp.exp(score - top)
        total = jnp.sum(prob, axis=1, keepdims=True)
        lse_ref[0, 0, at, :] = jnp.broadcast_to(top + jnp.log(total), (seg, 128))
        att = mm(prob.astype(BF), vw[...]) / total
        att_ref[0, at, :] = att.astype(BF)
        return carry

    lax.fori_loop(0, local_segs, one, 0)


def attend_back_kernel(dims, par_ref, len_ref, ctx_ref, rb_ref, q_ref, *refs):
    levels, seg, local_segs, all_segs, factor = dims
    parts_k, parts_v = refs[0:4], refs[4:8]
    do_ref, lse_ref, dq_ref, dkv_ref, db_ref = refs[8:13]
    kall, vall, kw, vw, bm, dk, dv, near, far = refs[13:]
    h, t = pl.program_id(0), pl.program_id(1)
    ctx = ctx_ref[0]
    rows, win = local_segs * seg, levels * seg
    states = kw.shape[0] - win
    each = states // 4
    bias_tables(rb_ref, h, levels, seg, bm)
    fill_sources(parts_k, parts_v, kall, vall, kw, vw, rows, win)
    dk[...] = jnp.zeros(dk.shape, F32)
    dv[...] = jnp.zeros(dv.shape, F32)

    @pl.when(t == 0)
    def _():
        near[...] = jnp.zeros(near.shape, F32)
        far[...] = jnp.zeros(far.shape, F32)

    def one(s, carry):
        line = chain(par_ref, t, ctx * local_segs + s, levels, all_segs, local_segs, ctx)
        fetch_window(line, kall, vall, kw, vw, seg)
        at = pl.ds(pl.multiple_of(s * seg, seg), seg)
        q = q_ref[0, at, :]
        do = do_ref[0, at, :]
        score = scores_of(q, kw, bm, line, len_ref[t, s], levels, seg, factor)
        prob = jnp.exp(score - lse_ref[0, 0, at, :][:, 0:1])
        dprob = mm_nt(do, vw[...])
        delta = jnp.sum(prob * dprob, axis=1, keepdims=True)
        dscore = (prob * (dprob - delta)).astype(BF)
        dq_ref[0, at, :] = (mm(dscore, kw[...]) * factor).astype(BF)
        near[...] += dscore[:, : 2 * seg].astype(F32)
        tail = dscore[:, 2 * seg : 3 * seg].astype(F32)
        for lev in range(3, levels):
            tail = tail + dscore[:, lev * seg : (lev + 1) * seg].astype(F32)
        far[...] += tail
        gk = mm_tn(dscore, q) * factor
        gv = mm_tn(prob.astype(BF), do)
        for lev, (_, part, block) in enumerate(line):
            start = pl.ds(pl.multiple_of(block * seg, seg), seg)
            dk[part, start, :] += gk[lev * seg : (lev + 1) * seg]
            dv[part, start, :] += gv[lev * seg : (lev + 1) * seg]
        for b in range(4):
            dk[b, rows:, :] += gk[win + b * each : win + (b + 1) * each]
            dv[b, rows:, :] += gv[win + b * each : win + (b + 1) * each]
        return carry

    lax.fori_loop(0, local_segs, one, 0)
    for place, b in enumerate((0, 2, 1, 3)):
        dkv_ref[place, 0, 0] = dk[b].astype(BF)
        dkv_ref[place, 1, 0] = dv[b].astype(BF)

    @pl.when(t == pl.num_programs(1) - 1)
    def _():
        row = lax.broadcasted_iota(jnp.int32, (seg, seg), 0)
        col = lax.broadcasted_iota(jnp.int32, (seg, seg), 1)
        edges = [-(10**6)] + list(EDGES) + [10**6]
        for b in range(BUCKETS):
            total = far[...] if b == BUCKETS - 1 else jnp.zeros((seg, seg), F32)
            for lev in range(2):
                dist = lev * seg + row - col
                inside = (dist >= edges[b]) & (dist < edges[b + 1])
                total = total + jnp.where(inside, near[:, lev * seg : (lev + 1) * seg], 0.0)
            db_ref[0, b : b + 1, :] = jnp.sum(total, axis=0, keepdims=True)


def attention_calls(trees, heads, local_segs, all_segs, seg, each, head_dim):
    levels = WINDOW // seg + 1
    rows = local_segs * seg
    tall = rows + each
    win = levels * seg
    wide = win + 4 * each
    factor = head_dim ** (-0.5)
    dims = (levels, seg, local_segs, all_segs, factor)
    assert EDGES[-1] <= 2 * seg - (seg - 1)
    flops = 2 * trees * heads * rows * wide * head_dim
    base_scratch = [
        pltpu.VMEM((4, rows, head_dim), BF),
        pltpu.VMEM((4, rows, head_dim), BF),
        pltpu.VMEM((wide, head_dim), BF),
        pltpu.VMEM((wide, head_dim), BF),
        pltpu.VMEM((seg, win), F32),
    ]

    def specs(order):
        def at(col):
            return pl.BlockSpec((1, tall, head_dim), lambda a, b, *_: (order(a, b)[0], 0, col(order(a, b)[1])))

        q_spec = at(lambda h: h)
        own_k, own_v = at(lambda h: heads + h), at(lambda h: 2 * heads + h)
        oth_k, oth_v = at(lambda h: h), at(lambda h: heads + h)
        return [q_spec, own_k, oth_k, oth_k, oth_k, own_v, oth_v, oth_v, oth_v]

    th = lambda a, b: (a, b)
    ht = lambda a, b: (b, a)
    forward = pl.pallas_call(
        functools.partial(attend_kernel, dims),
        out_shape=(
            jax.ShapeDtypeStruct((trees, rows, heads * head_dim), BF),
            jax.ShapeDtypeStruct((trees, heads, rows, 128), F32),
        ),
        grid_spec=pltpu.PrefetchScalarGridSpec(
            num_scalar_prefetch=4,
            grid=(trees, heads),
            in_specs=specs(th),
            out_specs=(
                pl.BlockSpec((1, rows, head_dim), lambda t, h, *_: (t, 0, h)),
                pl.BlockSpec((1, 1, rows, 128), lambda t, h, *_: (t, h, 0, 0)),
            ),
            scratch_shapes=base_scratch,
        ),
        compiler_params=pltpu.CompilerParams(vmem_limit_bytes=32 << 20),
        cost_estimate=pl.CostEstimate(
            flops=2 * flops, transcendentals=trees * heads * rows * wide, bytes_accessed=8 << 20
        ),
        name="attend",
    )
    backward = pl.pallas_call(
        functools.partial(attend_back_kernel, dims),
        out_shape=(
            jax.ShapeDtypeStruct((trees, rows, heads * head_dim), BF),
            jax.ShapeDtypeStruct((4, 2, trees, tall, heads * head_dim), BF),
            jax.ShapeDtypeStruct((heads, BUCKETS, 128), F32),
        ),
        grid_spec=pltpu.PrefetchScalarGridSpec(
            num_scalar_prefetch=4,
            grid=(heads, trees),
            in_specs=specs(ht)
            + [
                pl.BlockSpec((1, rows, head_dim), lambda h, t, *_: (t, 0, h)),
                pl.BlockSpec((1, 1, rows, 128), lambda h, t, *_: (t, h, 0, 0)),
            ],
            out_specs=(
                pl.BlockSpec((1, rows, head_dim), lambda h, t, *_: (t, 0, h)),
                pl.BlockSpec((4, 2, 1, tall, head_dim), lambda h, t, *_: (0, 0, t, 0, h)),
                pl.BlockSpec((1, BUCKETS, 128), lambda h, t, *_: (h, 0, 0)),
            ),
            scratch_shapes=base_scratch
            + [
                pltpu.VMEM((4, tall, head_dim), F32),
                pltpu.VMEM((4, tall, head_dim), F32),
                pltpu.VMEM((seg, 2 * seg), F32),
                pltpu.VMEM((seg, seg), F32),
            ],
        ),
        compiler_params=pltpu.CompilerParams(vmem_limit_bytes=40 << 20),
        cost_estimate=pl.CostEstimate(
            flops=5 * flops, transcendentals=trees * heads * rows * wide, bytes_accessed=16 << 20
        ),
        name="attend_back",
    )
    return forward, backward


def norm_stats(values):
    mean = jnp.mean(values, axis=-1, keepdims=True)
    centered = values - mean
    scale = lax.rsqrt(jnp.mean(centered * centered, axis=-1, keepdims=True) + EPSILON)
    return centered * scale, scale


def norm_back(grad, xhat, scale, gain):
    scaled = grad * gain
    first = jnp.mean(scaled, axis=-1, keepdims=True)
    second = jnp.mean(scaled * xhat, axis=-1, keepdims=True)
    return scale * (scaled - first - xhat * second)


def gelu_parts(u):
    inner = GELU_C * (u + GELU_A * u * u * u)
    th = jnp.tanh(inner)
    value = 0.5 * u * (1.0 + th)
    slope = 0.5 * (1.0 + th) + 0.5 * u * (1.0 - th * th) * GELU_C * (1.0 + 3.0 * GELU_A * u * u)
    return value, slope


def build(mesh):
    nf, nc, nt = mesh.shape["fsdp"], mesh.shape["context"], mesh.shape["tensor"]
    assert nc == 4

    def px(x):
        return lax.ppermute(x, "fsdp", [(0, 1), (1, 0)])

    def pc(x, k):
        return lax.ppermute(x, "context", [(a, a ^ k) for a in range(nc)])

    def pz(x, j):
        return lax.ppermute(x, "tensor", [(a, (a - j) % nt) for a in range(nt)])

    def on_device(
        tokens,
        state,
        parent,
        seg_length,
        cell_gate,
        norm1_gain,
        norm1_shift,
        w_query,
        w_key,
        w_value,
        w_attn_out,
        rel_bias,
        norm2_gain,
        norm2_shift,
        w_in,
        w_out,
        cotangent,
    ):
        trees, rows, width = tokens.shape
        local_segs = seg_length.shape[1]
        seg = rows // local_segs
        all_segs = parent.shape[1]
        heads = rel_bias.shape[0]
        cols = w_query.shape[1]
        head_dim = cols // heads
        each = state.shape[1]
        fi, ci, zi = lax.axis_index("fsdp"), lax.axis_index("context"), lax.axis_index("tensor")
        core = ci & 1
        zr, zs = rows // nt, each // nt

        def zpart(x, k, axis=1):
            n = x.shape[axis] // nt
            return lax.dynamic_slice_in_dim(x, k * n, n, axis)

        def place(blocks, starts, axis, total):
            shape = list(blocks[0].shape)
            shape[axis] = total
            out = jnp.zeros(shape, blocks[0].dtype)
            for block, start in zip(blocks, starts):
                out = lax.dynamic_update_slice_in_dim(out, block, start, axis)
            return out

        def gather_f(x, axis):
            n = x.shape[axis]
            if nf == 2:
                return place([x, px(x)], [fi * n, (1 - fi) * n], axis, 2 * n)
            return lax.all_gather(x, "fsdp", axis=axis, tiled=True)

        def scatter_f(x, axis):
            n = x.shape[axis] // nf
            if nf == 2:
                sent = lax.dynamic_slice_in_dim(x, (1 - fi) * n, n, axis).astype(BF)
                return lax.dynamic_slice_in_dim(x, fi * n, n, axis) + px(sent).astype(F32)
            return lax.psum_scatter(
                x.astype(BF), "fsdp", scatter_dimension=axis, tiled=True
            ).astype(F32)

        def gather_c(x, axis):
            n = x.shape[axis]
            y = pc(x, 2)
            return place(
                [x, y, pc(x, 1), pc(y, 1)],
                [ci * n, (ci ^ 2) * n, (ci ^ 1) * n, (ci ^ 3) * n],
                axis,
                nc * n,
            )

        def cpart(x, k, axis):
            n = x.shape[axis] // nc
            return lax.dynamic_slice_in_dim(x, k * n, n, axis)

        def scatter_c(x, axis):
            sent = jnp.stack([cpart(x, ci ^ 1, axis), cpart(x, ci ^ 3, axis)]).astype(BF)
            got = pc(sent, 1).astype(F32)
            far = (cpart(x, ci ^ 2, axis) + got[1]).astype(BF)
            return cpart(x, ci, axis) + got[0] + pc(far, 2).astype(F32)

        w_qkv = jnp.concatenate([w_query, w_key, w_value], axis=1)
        depth = w_qkv.shape[0]
        if nf == 2:
            half = depth // 2
            near = px(lax.dynamic_slice_in_dim(w_qkv, core * half, half, 0))
            over = pc(near, 1)
            base = (1 - fi) * depth
            qkv_w = place(
                [w_qkv, near, over],
                [fi * depth, base + core * half, base + (1 - core) * half],
                0,
                2 * depth,
            )
        else:
            qkv_w = lax.all_gather(w_qkv, "fsdp", axis=0, tiled=True)

        both = jnp.concatenate([tokens, state], axis=1).astype(F32)
        xhat_one, _ = norm_stats(both)
        normed = (xhat_one * norm1_gain + norm1_shift).astype(BF).reshape(-1, width)
        qkv = mm(normed, qkv_w).astype(BF).reshape(trees, rows + each, 3 * cols)
        kv = qkv[:, :, cols:]
        kv_y = pc(kv, 2)
        kv_c = pc(kv, 1)
        kv_cy = pc(kv_y, 1)

        fc = w_in.shape[1] // nc
        in_z = lax.dynamic_slice_in_dim(w_in, ci * fc, fc, 1)
        out_z = lax.dynamic_slice_in_dim(w_out, ci * fc, fc, 0)
        o_rows = w_attn_out.shape[0] // nc
        o_z = lax.dynamic_slice_in_dim(w_attn_out, ci * o_rows, o_rows, 0)
        in_blocks = [in_z] + [pz(in_z, j) for j in range(1, nt)]
        out_blocks = [out_z] + [pz(out_z, j) for j in range(1, nt)]
        o_blocks = [o_z] + [pz(o_z, j) for j in range(1, nt)]
        in_c = gather_f(jnp.concatenate(in_blocks, axis=1), 0)
        out_c = gather_f(jnp.concatenate(out_blocks, axis=0), 1)
        o_w = gather_c(gather_f(jnp.stack(o_blocks), 2), 1).reshape(nt * nc * o_rows, width)

        forward, backward = attention_calls(
            trees, heads, local_segs, all_segs, seg, each, head_dim
        )
        tables = (parent, seg_length, ci.reshape(1).astype(jnp.int32), rel_bias)
        sources = (qkv, qkv, kv_c, kv_y, kv_cy, qkv, kv_c, kv_y, kv_cy)
        attended, log_total = forward(*tables, *sources)

        att_blocks = [zpart(attended, zi)]
        for j in range(1, nt):
            att_blocks.append(pz(zpart(attended, (zi - j) % nt), j))
        att = jnp.concatenate(att_blocks, axis=2).reshape(trees * zr, nt * cols)
        inputs = zpart(tokens, zi).astype(F32).reshape(trees * zr, width)
        branch = mm(att, o_w)
        gated = cell_gate * branch
        hidden = inputs + gated
        xhat_two, scale_two = norm_stats(hidden)
        normed_two = (xhat_two * norm2_gain + norm2_shift).astype(BF)

        def spread(x):
            y = pc(x, 2)
            return jnp.concatenate([x, y, pc(x, 1), pc(y, 1)], axis=0)

        grad_low = zpart(cotangent, zi).reshape(trees * zr, width)
        grad_rows = spread(grad_low)
        ff_rows = spread(normed_two)
        up_proj = mm(ff_rows, in_c)
        active, slope = gelu_parts(up_proj)
        active = active.astype(BF)
        grad_up = (mm_nt(grad_rows, out_c) * slope).astype(BF)

        def collect(part):
            part = part.reshape(4, trees * zr, width)
            got = pc(part[2:].astype(BF), 1).astype(F32)
            far = (part[1] + got[1]).astype(BF)
            return part[0] + got[0] + pc(far, 2).astype(F32)

        grad_normed_two = collect(mm_nt(grad_up, in_c))
        mlp_out = collect(mm(active, out_c))
        part_in = mm_tn(ff_rows, grad_up)
        part_out = mm_tn(active, grad_rows)

        def broadcast_z(x):
            n = x.shape[1]
            blocks = [x] + [pz(x, j) for j in range(1, nt)]
            return place(blocks, [((zi + j) % nt) * n for j in range(nt)], 1, nt * n)

        result = (hidden + mlp_out).astype(BF).reshape(trees, zr, width)
        output = broadcast_z(result)

        grad_result = grad_low.astype(F32)
        gain_two = jnp.sum(grad_normed_two * xhat_two, axis=0)
        shift_two = jnp.sum(grad_normed_two, axis=0)
        grad_hidden = grad_result + norm_back(grad_normed_two, xhat_two, scale_two, norm2_gain)
        grad_branch = (cell_gate * grad_hidden).astype(BF)
        grad_att = mm_nt(grad_branch, o_w).astype(BF).reshape(trees, zr, nt, cols)
        part_attn = mm_tn(att, grad_branch)
        heads_blocks = [grad_att[:, :, 0]]
        heads_at = [zi * zr]
        for j in range(1, nt):
            heads_blocks.append(
                lax.ppermute(grad_att[:, :, j], "tensor", [(a, (a + j) % nt) for a in range(nt)])
            )
            heads_at.append(((zi - j) % nt) * zr)
        grad_heads = place(heads_blocks, heads_at, 1, rows)

        grad_q, parts, bias_rows = backward(*tables, *sources, grad_heads, log_total)
        got = pc(parts[2:], 1).astype(F32)
        far = (parts[1].astype(F32) + got[1]).astype(BF)
        grad_kv = (
            parts[0].astype(F32) + got[0] + pc(far, 2).astype(F32)
        ).astype(BF)

        o_depth = qkv_w.shape[0] // nc
        slab = lax.dynamic_slice_in_dim(qkv_w, ci * o_depth, o_depth, 0)
        all_w = gather_c(
            jnp.concatenate([slab] + [pz(slab, j) for j in range(1, nt)], axis=1), 0
        )
        q_blocks, kv_blocks = [], []
        for j in range(nt):
            k = (zi - j) % nt
            q_piece = zpart(grad_q, k)
            kv_piece = jnp.concatenate(
                [zpart(grad_kv[:, :, :rows], k, 2), zpart(grad_kv[:, :, rows:], k, 2)], axis=2
            )
            q_blocks.append(pz(q_piece, j) if j else q_piece)
            kv_blocks.append(pz(kv_piece, j) if j else kv_piece)
        line = []
        for j in range(nt):
            line.append(jnp.pad(q_blocks[j], ((0, 0), (0, zs), (0, 0))))
            line.append(kv_blocks[j][0])
            line.append(kv_blocks[j][1])
        line = jnp.concatenate(line, axis=2).reshape(trees * (zr + zs), nt * 3 * cols)
        grad_normed = mm_nt(line, all_w).reshape(trees, zr + zs, width)
        own = jnp.concatenate([zpart(tokens, zi), zpart(state, zi)], axis=1).astype(F32)
        xhat_own, scale_own = norm_stats(own)
        gain_one = jnp.sum(grad_normed * xhat_own, axis=(0, 1))
        shift_one = jnp.sum(grad_normed, axis=(0, 1))
        grad_own = norm_back(grad_normed, xhat_own, scale_own, norm1_gain)
        grad_tokens_own = (grad_hidden.reshape(trees, zr, width) + grad_own[:, :zr]).astype(BF)
        tokens_grad = broadcast_z(grad_tokens_own)
        state_grad = broadcast_z(grad_own[:, zr:].astype(BF))

        def sum_z(blocks):
            total = blocks[0]
            for j in range(1, nt):
                total = total + lax.ppermute(
                    blocks[j].astype(BF), "tensor", [(a, (a + j) % nt) for a in range(nt)]
                ).astype(F32)
            return total

        in_sum = scatter_f(part_in, 0)
        in_own = sum_z([in_sum[:, j * fc : (j + 1) * fc] for j in range(nt)])
        grad_in = gather_c(in_own.astype(BF), 1).astype(F32)
        out_sum = scatter_f(part_out, 1)
        out_own = sum_z([out_sum[j * fc : (j + 1) * fc] for j in range(nt)])
        grad_out = gather_c(out_own.astype(BF), 0).astype(F32)
        attn_sum = scatter_f(
            scatter_c(part_attn.reshape(nt, nc * o_rows, width), 1), 2
        )
        attn_own = sum_z([attn_sum[j] for j in range(nt)])
        grad_attn_out = gather_c(attn_own.astype(BF), 0).astype(F32)

        normed3 = normed.reshape(trees, rows + each, width)
        part_q = mm_tn(
            normed3[:, :rows].reshape(-1, width), grad_q.reshape(-1, cols)
        )
        part_k = mm_tn(normed, grad_kv[0].reshape(-1, cols))
        part_v = mm_tn(normed, grad_kv[1].reshape(-1, cols))
        part_qkv = jnp.concatenate([part_q, part_k, part_v], axis=1)
        part_qkv = part_qkv.reshape(nf, depth, 3 * cols)
        qkv_sum = scatter_f(scatter_c(part_qkv, 1), 0)[0]
        grad_qkv = gather_c(qkv_sum.astype(BF), 0).astype(F32)

        def total(x):
            if nf == 2:
                x = x + px(x)
            else:
                x = lax.psum(x, "fsdp")
            x = x + pc(x, 1)
            x = x + pc(x, 2)
            if nt & (nt - 1) == 0:
                k = 1
                while k < nt:
                    x = x + lax.ppermute(x, "tensor", [(a, a ^ k) for a in range(nt)])
                    k = 2 * k
                return x
            return lax.psum(x, "tensor")

        bias_own = jnp.sum(bias_rows, axis=2)
        bias_all = lax.dynamic_update_slice(
            jnp.zeros((heads * nt, BUCKETS), F32), bias_own, (zi * heads, 0)
        )
        squares = jnp.stack(
            [jnp.sum(inputs * inputs), jnp.sum(gated * gated), jnp.sum(mlp_out * mlp_out)]
        )
        early = total(
            jnp.concatenate([gain_two, shift_two, bias_all.reshape(-1), squares])
        )
        late = total(jnp.concatenate([gain_one, shift_one]))
        at = 2 * width + bias_all.size
        bias_sum = early[2 * width : at].reshape(bias_all.shape)
        grad_bias = lax.dynamic_slice_in_dim(bias_sum, zi * heads, heads, 0)
        cell_count = trees * rows * width * nf * nc
        norms = jnp.sqrt(early[at : at + 3] / cell_count)
        return (
            output,
            tokens_grad,
            state_grad,
            grad_qkv[:, :cols],
            grad_qkv[:, cols : 2 * cols],
            grad_qkv[:, 2 * cols :],
            grad_attn_out,
            grad_bias,
            late[:width],
            late[width:],
            early[:width],
            early[width : 2 * width],
            grad_in,
            grad_out,
            norms,
        )

    return on_device


def solution(mesh):
    return jax.shard_map(
        build(mesh),
        mesh=mesh,
        in_specs=(
            P("fsdp", "context", None),
            P("fsdp", "context", None),
            P("fsdp", None),
            P("fsdp", "context"),
            P(),
            P(),
            P(),
            P("fsdp", "tensor"),
            P("fsdp", "tensor"),
            P("fsdp", "tensor"),
            P("tensor", "fsdp"),
            P("tensor", None),
            P(),
            P(),
            P("fsdp", "tensor"),
            P("tensor", "fsdp"),
            P("fsdp", "context", None),
        ),
        out_specs=(
            P("fsdp", "context", None),
            P("fsdp", "context", None),
            P("fsdp", "context", None),
            P("fsdp", "tensor"),
            P("fsdp", "tensor"),
            P("fsdp", "tensor"),
            P("tensor", "fsdp"),
            P("tensor", None),
            P(),
            P(),
            P(),
            P(),
            P("fsdp", "tensor"),
            P("tensor", "fsdp"),
            P(),
        ),
        check_vma=False,
    )
```

time: 1060 us -> 639 us (0.60)
  waiting for transfers between devices: 580 us -> 315 us
  matrix products: 185 us -> 44.6 us
  starting transfers between devices: 2.64 us -> 97.7 us
  blocking collectives: 85 us -> 0 us
  Pallas kernels: 0 us -> 39.1 us
  other arithmetic: 77.2 us -> 50.2 us
  local copies, waits for them, and re-layouts: 106 us -> 81.8 us
  between operations: 16.8 us -> 2.64 us
    psum x4 -> x0, waiting for transfers between devices: 461 us -> none  [the longest x1 198 us: on_device(): lax.psum(matrix_product('tnf,fd->tnd', activated, out_w).astype(jnp.bfloa...]
    ppermute x0 -> x98, waiting for transfers between devices: none -> 315 us  [the longest x30 92.3 us: pz(): return lax.ppermute(x, 'tensor', [(a, (a - j) % nt) for a in range(nt)])]
    dot_general x44 -> x14, matrix products: 179 us -> 44.6 us  [the longest x4 20.3 us: mm_nt(): lax.dot_general(left, right, (((1,), (1,)), ((), ())), preferred_element_...]
    reduce_scatter x10 -> x0, waiting for transfers between devices: 118 us -> none  [the longest x1 34.7 us: on_device(): lax.psum_scatter(local_out.astype(jnp.bfloat16), 'fsdp', scatter_dimensio...]
    ppermute x0 -> x98, starting transfers between devices: none -> 97.7 us  [the longest x30 38.5 us: pz(): return lax.ppermute(x, 'tensor', [(a, (a - j) % nt) for a in range(nt)])]
    all_gather x6 -> x0, blocking collectives: 60.4 us -> none  [the longest x1 11.2 us: on_device(): lax.all_gather(w_attn_out, 'fsdp', axis=1, tiled=True)]
    reshape x11 -> x4, local copies, waits for them, and re-layouts: 45.3 us -> 5.53 us  [the longest x1 3.57 us: on_device(): part_qkv = part_qkv.reshape(nf, depth, 3 * cols)]
    pallas_call x0 -> x2, Pallas kernels: none -> 39.1 us  [the longest x1 22.9 us: on_device(): backward(*tables, *sources, grad_heads, log_total)]
  transfers between devices with their start and end apart: 18 -> 98, of which waited for: 9 -> 37; matrix products, arithmetic and copies ran while one was open for 24% -> 25% of each run, Pallas kernels for 0% -> 6%
where the time goes in v1:
time: 639 us; the launch traced here: 631 us
  waiting for transfers between devices  315 us (49%)
  starting transfers between devices  97.7 us (15%)
  local copies, waits for them, and re-layouts  81.8 us (13%)
  other arithmetic  50.2 us (8%)
  matrix products  44.6 us (7%)
  Pallas kernels  39.1 us (6%)
    ppermute x30, waiting for transfers between devices, pz(): return lax.ppermute(x, 'tensor', [(a, (a - j) % nt) for a in range(nt)])  92.3 us
    ppermute x42, waiting for transfers between devices, pc(): return lax.ppermute(x, 'context', [(a, a ^ k) for a in range(nc)])  73 us
    ppermute x10, waiting for transfers between devices, px(): return lax.ppermute(x, 'fsdp', [(0, 1), (1, 0)])  67.4 us
    ppermute x4, waiting for transfers between devices, total(): x = x + lax.ppermute(x, 'tensor', [(a, a ^ k) for a in range(nt)])  40.7 us
    ppermute x30, starting transfers between devices, pz(): return lax.ppermute(x, 'tensor', [(a, (a - j) % nt) for a in range(nt)])  38.5 us
    ppermute x9, waiting for transfers between devices, sum_z(): lax.ppermute(blocks[j].astype(BF), 'tensor', [(a, (a + j) % nt) for a in...  30.6 us
    ppermute x42, starting transfers between devices, pc(): return lax.ppermute(x, 'context', [(a, a ^ k) for a in range(nc)])  26.5 us
    pallas_call x1, Pallas kernels, on_device(): backward(*tables, *sources, grad_heads, log_total)  22.9 us
  transfers between devices with their start and end apart: 98, of which 37 were waited for; matrix products, arithmetic and copies ran while one was open for 25% of the time, Pallas kernels for 6%

profile of v1, /device:TPU:0, one launch (start us, length us, event | category | flops | bytes accessed | tf_op | source)
XLA Modules:
  0.0 631.5 jit_solution(14547125300002927087)
XLA Ops:
  45.5 23.6 %collective-permute-done.3.refs_2_.refs_6_ = bf16[2,768,512]{2,1,0:T(8,128)(2,1)} collective-permute-done((bf16[2,768,512]{2,1,0:T(8,128)(2,1)}, bf16[2,768,512]{2,1,0:T(8,128)(2,1)}, u32[]{:S(2)}, u32[]{:S(2)}) %collective-permute-start.3) | collective-permute-done | bytes 1572896 | tf_op jit(solution)/shard_map/ppermute | solution.py:332
  96.4 13.6 %collective-permute-done.23 = bf16[256,512]{1,0:T(8,128)(2,1)S(1)} collective-permute-done((bf16[256,512]{1,0:T(8,128)(2,1)}, bf16[256,512]{1,0:T(8,128)(2,1)S(1)}, u32[]{:S(2)}, u32[]{:S(2)}) %collective-permute-start.23) | collective-permute-done | bytes 262176 | tf_op jit(solution)/shard_map/ppermute | solution.py:335
  117.9 16.3 %attend.1 = (bf16[2,640,256]{2,1,0:T(8,128)(2,1)S(1)}, f32[2,2,640,128]{3,2,1,0:T(8,128)S(1)}) custom-call(s32[2,20]{1,0:T(2,128)S(1)} %copy-done.6, s32[2,5]{1,0:T(2,128)S(1)} %copy-done.7, s32[1]{0:T(128)} %bitcast.1.ctx_ref, f32[2,32]{1,0:T(2,128)S(1)} %copy-done.8, bf16[2,768,768]{2,1,0:T(8,128)(2,1)S(1)} %bitcast.202, ...), custom_call_target="tpu_custom_call" | custom-call | flops 1509949440 | bytes 8388608 | tf_op jit(solution)/shard_map/attend/pallas_call | solution.py:457
  137.7 14.9 %collective-permute-done.48 = bf16[256,768]{1,0:T(8,128)(2,1)S(1)} collective-permute-done((bf16[256,768]{1,0:T(8,128)(2,1)S(1)}, bf16[256,768]{1,0:T(8,128)(2,1)S(1)}, u32[]{:S(2)}, u32[]{:S(2)}) %collective-permute-start.48) | collective-permute-done | bytes 393248 | tf_op jit(solution)/shard_map/ppermute | solution.py:335
  166.7 18.4 %collective-permute-done.21 = bf16[512,1024]{1,0:T(8,128)(2,1)S(1)} collective-permute-done((bf16[512,1024]{1,0:T(8,128)(2,1)S(1)}, bf16[512,1024]{1,0:T(8,128)(2,1)S(1)}, u32[]{:S(2)}, u32[]{:S(2)}) %collective-permute-start.21) | collective-permute-done | bytes 1048608 | tf_op jit(solution)/shard_map/ppermute | solution.py:329
  189.2 17.1 %collective-permute-done.25 = bf16[1024,512]{1,0:T(8,128)(2,1)S(1)} collective-permute-done((bf16[1024,512]{1,0:T(8,128)(2,1)S(1)}, bf16[1024,512]{1,0:T(8,128)(2,1)S(1)}, u32[]{:S(2)}, u32[]{:S(2)}) %collective-permute-start.25) | collective-permute-done | bytes 1048608 | tf_op jit(solution)/shard_map/ppermute | solution.py:329
  207.1 5.2 collective-permute-done.15
  224.8 9.6 %fusion.12 = bf16[1280,1024]{1,0:T(8,128)(2,1)S(1)} fusion(f32[1280,1024]{1,0:T(8,128)S(1)} %fusion.64, bf16[1024,1024]{1,0:T(8,128)(2,1)S(1)} %constant_dynamic-update-slice_fusion.39, bf16[320,1024]{1,0:T(8,128)(2,1)S(1)} %collective-permute-done.33, bf16[320,1024]{1,0:T(8,128)(2,1)S(1)} %collective-permute-done.32, ...), kind=kOutput, calls=%fused_computation.18 | convolution fusion | flops 2719744000 | bytes 12582912 | tf_op jit(solution)/shard_map/dot_general | solution.py:50
  241.5 5.2 fusion.90
  250.9 20.1 %collective-permute-done.84 = bf16[512,1024]{1,0:T(8,128)(2,1)S(1)} collective-permute-done((bf16[512,1024]{1,0:T(8,128)(2,1)S(1)}, bf16[512,1024]{1,0:T(8,128)(2,1)S(1)}, u32[]{:S(2)}, u32[]{:S(2)}) %collective-permute-start.84) | collective-permute-done | bytes 1048608 | tf_op jit(solution)/shard_map/ppermute | solution.py:329
  277.7 13.4 %collective-permute-done.93 = bf16[256,512]{1,0:T(8,128)(2,1)S(1)} collective-permute-done((bf16[256,512]{1,0:T(8,128)(2,1)S(1)}, bf16[256,512]{1,0:T(8,128)(2,1)S(1)}, u32[]{:S(2)}, u32[]{:S(2)}) %collective-permute-start.93) | collective-permute-done | bytes 262176 | tf_op jit(solution)/shard_map/ppermute | solution.py:557
  296.6 11.4 %collective-permute-done.86 = bf16[512,256]{1,0:T(8,128)(2,1)S(1)} collective-permute-done((bf16[512,256]{1,0:T(8,128)(2,1)S(1)}, bf16[512,256]{1,0:T(8,128)(2,1)S(1)}, u32[]{:S(2)}, u32[]{:S(2)}) %collective-permute-start.86) | collective-permute-done | bytes 262176 | tf_op jit(solution)/shard_map/ppermute | solution.py:557
  317.2 12.5 %collective-permute-done.27 = bf16[320,1024]{1,0:T(8,128)(2,1)S(1)} collective-permute-done((bf16[320,1024]{1,0:T(8,128)(2,1)S(1)}, bf16[320,1024]{1,0:T(8,128)(2,1)S(1)}, u32[]{:S(2)}, u32[]{:S(2)}) %collective-permute-start.27) | collective-permute-done | bytes 655392 | tf_op jit(solution)/shard_map/ppermute | solution.py:332
  340.7 6.2 collective-permute-done.36
  346.9 5.2 collective-permute-done.37
  353.5 22.9 %attend_back.1 = (bf16[2,640,256]{2,1,0:T(8,128)(2,1)S(1)}, bf16[4,2,2,768,256]{4,3,2,1,0:T(8,128)(2,1)}, f32[2,32,128]{2,1,0:T(8,128)S(1)}) custom-call(s32[2,20]{1,0:T(2,128)S(1)} %copy-done.6, s32[2,5]{1,0:T(2,128)S(1)} %copy-done.7, s32[1]{0:T(128)} %bitcast.1.ctx_ref, f32[2,32]{1,0:T(2,128)S(1)} %copy-done.8, bf16[2,768,768]{2,1,0:T(8,128)(2,1)S(1)} %bitcast.205, ...), custom_call_target="tpu_custom_call" | custom-call | flops 3774873600 | bytes 16777216 | tf_op jit(solution)/shard_map/attend_back/pallas_call | solution.py:517
  411.9 19.3 %collective-permute-done.77 = f32[2307]{0:T(1024)S(1)} collective-permute-done((f32[2307]{0:T(1024)S(1)}, f32[2307]{0:T(1024)S(1)}, u32[]{:S(2)}, u32[]{:S(2)}) %collective-permute-start.77) | collective-permute-done | bytes 9260 | tf_op jit(solution)/shard_map/ppermute | solution.py:595
  433.2 12.6 %collective-permute-done.78 = f32[2307]{0:T(1024)S(1)} collective-permute-done((f32[2307]{0:T(1024)S(1)}, f32[2307]{0:T(1024)S(1)}, u32[]{:S(2)}, u32[]{:S(2)}) %collective-permute-start.78) | collective-permute-done | bytes 9260 | tf_op jit(solution)/shard_map/ppermute | solution.py:595
  472.8 17.7 %collective-permute-done.71 = bf16[64,512]{1,0:T(8,128)(2,1)S(1)} collective-permute-done((bf16[64,512]{1,0:T(8,128)(2,1)S(1)}, bf16[64,512]{1,0:T(8,128)(2,1)S(1)}, u32[]{:S(2)}, u32[]{:S(2)}) %collective-permute-start.71) | collective-permute-done | bytes 65568 | tf_op jit(solution)/shard_map/ppermute | solution.py:332
  524.0 11.9 %collective-permute-done.44 = bf16[2,2,192,256]{3,2,1,0:T(8,128)(2,1)S(1)} collective-permute-done((bf16[2,2,192,256]{3,2,1,0:T(8,128)(2,1)S(1)}, bf16[2,2,192,256]{3,2,1,0:T(8,128)(2,1)S(1)}, u32[]{:S(2)}, u32[]{:S(2)}) %collective-permute-start.44) | collective-permute-done | bytes 393248 | tf_op jit(solution)/shard_map/ppermute | solution.py:335
  540.3 6.0 fusion.27
  561.1 8.8 %collective-permute-done.83 = f32[2048]{0:T(1024)S(1)} collective-permute-done((f32[2048]{0:T(1024)S(1)}, f32[2048]{0:T(1024)S(1)}, u32[]{:S(2)}, u32[]{:S(2)}) %collective-permute-start.83) | collective-permute-done | bytes 8224 | tf_op jit(solution)/shard_map/ppermute | solution.py:595
  575.7 7.6 %collective-permute-done.60 = bf16[2,128,768]{2,1,0:T(8,128)(2,1)S(1)} collective-permute-done((bf16[2,128,768]{2,1,0:T(8,128)(2,1)S(1)}, bf16[2,128,768]{2,1,0:T(8,128)(2,1)S(1)}, u32[]{:S(2)}, u32[]{:S(2)}) %collective-permute-start.60) | collective-permute-done | bytes 393248 | tf_op jit(solution)/shard_map/ppermute | solution.py:332
  591.0 37.0 %collective-permute-done.54 = bf16[2,160,1024]{2,1,0:T(8,128)(2,1)S(1)} collective-permute-done((bf16[2,160,1024]{2,1,0:T(8,128)(2,1)S(1)}, bf16[2,160,1024]{2,1,0:T(8,128)(2,1)S(1)}, u32[]{:S(2)}, u32[]{:S(2)}) %collective-permute-start.54) | collective-permute-done | bytes 655392 | tf_op jit(solution)/shard_map/ppermute | solution.py:335
  (468 shorter events, 292.5 us)
Async XLA Ops:
  39.9 40.0 %collective-permute-start.18 = (bf16[512,256]{1,0:T(8,128)(2,1)}, bf16[512,256]{1,0:T(8,128)(2,1)}, u32[]{:S(2)}, u32[]{:S(2)}) collective-permute-start(bf16[512,256]{1,0:T(8,128)(2,1)} %constant_dynamic-slice_fusion.17), channel_id=1, source_target_pairs={{0,3},{1,0},{2,1},{3,2},{4,7},{5,4},{6,5},{7,6},{8,11},{9,8},{10,9... | collective-permute-start | bytes 786440 | tf_op jit(solution)/shard_map/ppermute | solution.py:335
  40.7 43.1 %collective-permute-start.19 = (bf16[512,256]{1,0:T(8,128)(2,1)}, bf16[512,256]{1,0:T(8,128)(2,1)}, u32[]{:S(2)}, u32[]{:S(2)}) collective-permute-start(bf16[512,256]{1,0:T(8,128)(2,1)} %constant_dynamic-slice_fusion.17), channel_id=1, source_target_pairs={{0,2},{1,3},{2,0},{3,1},{4,6},{5,7},{6,4},{7,5},{8,10},{9,11},{10,... | collective-permute-start | bytes 786440 | tf_op jit(solution)/shard_map/ppermute | solution.py:335
  45.4 71.0 %collective-permute-start.2 = (bf16[2,768,512]{2,1,0:T(8,128)(2,1)}, bf16[2,768,512]{2,1,0:T(8,128)(2,1)}, u32[]{:S(2)}, u32[]{:S(2)}) collective-permute-start(bf16[2,768,512]{2,1,0:T(8,128)(2,1)} %slice.264), channel_id=1, source_target_pairs={{0,4},{4,0},{8,12},{12,8},{1,5},{5,1},{9,13},{13,9},{2,6},{6,2},{1... | collective-permute-start | bytes 4718600 | tf_op jit(solution)/shard_map/ppermute | solution.py:332
  69.1 48.7 %collective-permute-start.4 = (bf16[2,768,512]{2,1,0:T(8,128)(2,1)}, bf16[2,768,512]{2,1,0:T(8,128)(2,1)}, u32[]{:S(2)}, u32[]{:S(2)}) collective-permute-start(bf16[2,768,512]{2,1,0:T(8,128)(2,1)} %collective-permute-done.3.refs_2_.refs_6_), channel_id=1, source_target_pairs={{0,4},{4,0},{8,12},{12,8},{1,5},{5,1},{9,13},{13,9},{2,6},{6,2},{1... | collective-permute-start | bytes 4718600 | tf_op jit(solution)/shard_map/ppermute | solution.py:332
  116.4 72.7 %collective-permute-start.31 = (bf16[320,1024]{1,0:T(8,128)(2,1)S(1)}, bf16[320,1024]{1,0:T(8,128)(2,1)S(1)}, u32[]{:S(2)}, u32[]{:S(2)}) collective-permute-start(bf16[320,1024]{1,0:T(8,128)(2,1)S(1)} %bitcast.219), channel_id=1, source_target_pairs={{0,8},{4,12},{8,0},{12,4},{1,9},{5,13},{9,1},{13,5},{2,10},{6,14},... | collective-permute-start | bytes 1966088 | tf_op jit(solution)/shard_map/ppermute | solution.py:332
  117.8 41.2 %collective-permute-start.14 = (bf16[4,64,1024]{2,1,0:T(8,128)(2,1)S(1)}, bf16[4,64,1024]{2,1,0:T(8,128)(2,1)S(1)}, u32[]{:S(2)}, u32[]{:S(2)}) collective-permute-start(bf16[4,64,1024]{2,1,0:T(8,128)(2,1)S(1)} %collective-permute-done.12), channel_id=1, source_target_pairs={{0,4},{4,0},{8,12},{12,8},{1,5},{5,1},{9,13},{13,9},{2,6},{6,2},{1... | collective-permute-start | bytes 1572872 | tf_op jit(solution)/shard_map/ppermute | solution.py:332
  160.5 45.8 %collective-permute-start.25 = (bf16[1024,512]{1,0:T(8,128)(2,1)S(1)}, bf16[1024,512]{1,0:T(8,128)(2,1)S(1)}, u32[]{:S(2)}, u32[]{:S(2)}) collective-permute-start(bf16[1024,512]{1,0:T(8,128)(2,1)S(1)} %get-tuple-element.80), channel_id=1, source_target_pairs={{0,16},{16,0},{1,17},{17,1},{2,18},{18,2},{3,19},{19,3},{4,20},{20... | collective-permute-start | bytes 3145736 | tf_op jit(solution)/shard_map/ppermute | solution.py:329
  163.0 43.5 %collective-permute-start.50 = (bf16[256,3072]{1,0:T(8,128)(2,1)S(1)}, bf16[256,3072]{1,0:T(8,128)(2,1)}, u32[]{:S(2)}, u32[]{:S(2)}) collective-permute-start(bf16[256,3072]{1,0:T(8,128)(2,1)S(1)} %get-tuple-element.64), channel_id=1, source_target_pairs={{0,8},{4,12},{8,0},{12,4},{1,9},{5,13},{9,1},{13,5},{2,10},{6,14},... | collective-permute-start | bytes 4718600 | tf_op jit(solution)/shard_map/ppermute | solution.py:332
  164.4 50.6 %collective-permute-start.51 = (bf16[256,3072]{1,0:T(8,128)(2,1)S(1)}, bf16[256,3072]{1,0:T(8,128)(2,1)S(1)}, u32[]{:S(2)}, u32[]{:S(2)}) collective-permute-start(bf16[256,3072]{1,0:T(8,128)(2,1)S(1)} %get-tuple-element.64), channel_id=1, source_target_pairs={{0,4},{4,0},{8,12},{12,8},{1,5},{5,1},{9,13},{13,9},{2,6},{6,2},{1... | collective-permute-start | bytes 4718600 | tf_op jit(solution)/shard_map/ppermute | solution.py:332
  215.0 169.9 %collective-permute-start.52 = (bf16[256,3072]{1,0:T(8,128)(2,1)}, bf16[256,3072]{1,0:T(8,128)(2,1)}, u32[]{:S(2)}, u32[]{:S(2)}) collective-permute-start(bf16[256,3072]{1,0:T(8,128)(2,1)} %collective-permute-done.50), channel_id=1, source_target_pairs={{0,4},{4,0},{8,12},{12,8},{1,5},{5,1},{9,13},{13,9},{2,6},{6,2},{1... | collective-permute-start | bytes 4718600 | tf_op jit(solution)/shard_map/ppermute | solution.py:332
  275.6 40.8 %collective-permute-start.35 = (bf16[320,1024]{1,0:T(8,128)(2,1)S(1)}, bf16[320,1024]{1,0:T(8,128)(2,1)S(1)}, u32[]{:S(2)}, u32[]{:S(2)}) collective-permute-start(bf16[320,1024]{1,0:T(8,128)(2,1)S(1)} %fusion.35), channel_id=1, source_target_pairs={{0,8},{4,12},{8,0},{12,4},{1,9},{5,13},{9,1},{13,5},{2,10},{6,14},... | collective-permute-start | bytes 1966088 | tf_op jit(solution)/shard_map/ppermute | solution.py:332
  295.2 92.8 %collective-permute-start.95 = (bf16[256,512]{1,0:T(8,128)(2,1)}, bf16[256,512]{1,0:T(8,128)(2,1)}, u32[]{:S(2)}, u32[]{:S(2)}) collective-permute-start(bf16[256,512]{1,0:T(8,128)(2,1)} %get-tuple-element.34), channel_id=1, source_target_pairs={{0,8},{4,12},{8,0},{12,4},{1,9},{5,13},{9,1},{13,5},{2,10},{6,14},... | collective-permute-start | bytes 786440 | tf_op jit(solution)/shard_map/ppermute | solution.py:332
  308.0 82.6 %collective-permute-start.96 = (bf16[256,512]{1,0:T(8,128)(2,1)}, bf16[256,512]{1,0:T(8,128)(2,1)}, u32[]{:S(2)}, u32[]{:S(2)}) collective-permute-start(bf16[256,512]{1,0:T(8,128)(2,1)} %get-tuple-element.34), channel_id=1, source_target_pairs={{0,4},{4,0},{8,12},{12,8},{1,5},{5,1},{9,13},{13,9},{2,6},{6,2},{1... | collective-permute-start | bytes 786440 | tf_op jit(solution)/shard_map/ppermute | solution.py:332
  380.3 68.2 %collective-permute-start.39 = (bf16[2,2,2,768,256]{4,3,2,1,0:T(8,128)(2,1)}, bf16[2,2,2,768,256]{4,3,2,1,0:T(8,128)(2,1)}, u32[]{:S(2)}, u32[]{:S(2)}) collective-permute-start(bf16[2,2,2,768,256]{4,3,2,1,0:T(8,128)(2,1)} %slice.220), channel_id=1, source_target_pairs={{0,4},{4,0},{8,12},{12,8},{1,5},{5,1},{9,13},{13,9},{2,6},{6,2},{1... | collective-permute-start | bytes 9437192 | tf_op jit(solution)/shard_map/ppermute | solution.py:332
  398.8 57.6 %collective-permute-start.28 = (bf16[2,160,1024]{2,1,0:T(8,128)(2,1)}, bf16[2,160,1024]{2,1,0:T(8,128)(2,1)}, u32[]{:S(2)}, u32[]{:S(2)}) collective-permute-start(bf16[2,160,1024]{2,1,0:T(8,128)(2,1)} %bitcast.13), channel_id=1, source_target_pairs={{0,3},{1,0},{2,1},{3,2},{4,7},{5,4},{6,5},{7,6},{8,11},{9,8},{10,9... | collective-permute-start | bytes 1966088 | tf_op jit(solution)/shard_map/ppermute | solution.py:335
  402.4 61.6 %collective-permute-start.29 = (bf16[2,160,1024]{2,1,0:T(8,128)(2,1)}, bf16[2,160,1024]{2,1,0:T(8,128)(2,1)}, u32[]{:S(2)}, u32[]{:S(2)}) collective-permute-start(bf16[2,160,1024]{2,1,0:T(8,128)(2,1)} %bitcast.13), channel_id=1, source_target_pairs={{0,2},{1,3},{2,0},{3,1},{4,6},{5,7},{6,4},{7,5},{8,10},{9,11},{10,... | collective-permute-start | bytes 1966088 | tf_op jit(solution)/shard_map/ppermute | solution.py:335
  454.0 39.9 %collective-permute-start.40 = (bf16[2,2,768,256]{3,2,1,0:T(8,128)(2,1)S(1)}, bf16[2,2,768,256]{3,2,1,0:T(8,128)(2,1)}, u32[]{:S(2)}, u32[]{:S(2)}) collective-permute-start(bf16[2,2,768,256]{3,2,1,0:T(8,128)(2,1)S(1)} %fusion.29), channel_id=1, source_target_pairs={{0,8},{4,12},{8,0},{12,4},{1,9},{5,13},{9,1},{13,5},{2,10},{6,14},... | collective-permute-start | bytes 4718600 | tf_op jit(solution)/shard_map/ppermute | solution.py:332
  467.8 43.5 %collective-permute-start.41 = (bf16[2,160,256]{2,1,0:T(8,128)(2,1)}, bf16[2,160,256]{2,1,0:T(8,128)(2,1)}, u32[]{:S(2)}, u32[]{:S(2)}) collective-permute-start(bf16[2,160,256]{2,1,0:T(8,128)(2,1)} %get-tuple-element.87), channel_id=1, source_target_pairs={{0,3},{1,0},{2,1},{3,2},{4,7},{5,4},{6,5},{7,6},{8,11},{9,8},{10,9... | collective-permute-start | bytes 491528 | tf_op jit(solution)/shard_map/ppermute | solution.py:335
  468.5 53.9 %collective-permute-start.43 = (bf16[2,160,256]{2,1,0:T(8,128)(2,1)}, bf16[2,160,256]{2,1,0:T(8,128)(2,1)}, u32[]{:S(2)}, u32[]{:S(2)}) collective-permute-start(bf16[2,160,256]{2,1,0:T(8,128)(2,1)} %get-tuple-element.86), channel_id=1, source_target_pairs={{0,2},{1,3},{2,0},{3,1},{4,6},{5,7},{6,4},{7,5},{8,10},{9,11},{10,... | collective-permute-start | bytes 491528 | tf_op jit(solution)/shard_map/ppermute | solution.py:335
  469.5 67.8 %collective-permute-start.45 = (bf16[2,160,256]{2,1,0:T(8,128)(2,1)}, bf16[2,160,256]{2,1,0:T(8,128)(2,1)}, u32[]{:S(2)}, u32[]{:S(2)}) collective-permute-start(bf16[2,160,256]{2,1,0:T(8,128)(2,1)} %get-tuple-element.85), channel_id=1, source_target_pairs={{0,1},{1,2},{2,3},{3,0},{4,5},{5,6},{6,7},{7,4},{8,9},{9,10},{10,1... | collective-permute-start | bytes 491528 | tf_op jit(solution)/shard_map/ppermute | solution.py:335
  497.4 41.5 %collective-permute-start.46 = (bf16[2,2,192,256]{3,2,1,0:T(8,128)(2,1)}, bf16[2,2,192,256]{3,2,1,0:T(8,128)(2,1)S(1)}, u32[]{:S(2)}, u32[]{:S(2)}) collective-permute-start(bf16[2,2,192,256]{3,2,1,0:T(8,128)(2,1)} %pad_maximum_fusion.17), channel_id=1, source_target_pairs={{0,1},{1,2},{2,3},{3,0},{4,5},{5,6},{6,7},{7,4},{8,9},{9,10},{10,1... | collective-permute-start | bytes 1179656 | tf_op jit(solution)/shard_map/ppermute | solution.py:335
  519.2 53.4 %collective-permute-start.59 = (bf16[2,2,128,768]{3,2,1,0:T(8,128)(2,1)S(1)}, bf16[2,2,128,768]{3,2,1,0:T(8,128)(2,1)S(1)}, u32[]{:S(2)}, u32[]{:S(2)}) collective-permute-start(bf16[2,2,128,768]{3,2,1,0:T(8,128)(2,1)S(1)} %pad_maximum_fusion.9), channel_id=1, source_target_pairs={{0,4},{4,0},{8,12},{12,8},{1,5},{5,1},{9,13},{13,9},{2,6},{6,2},{1... | collective-permute-start | bytes 2359304 | tf_op jit(solution)/shard_map/ppermute | solution.py:332
  575.0 52.9 %collective-permute-start.54 = (bf16[2,160,1024]{2,1,0:T(8,128)(2,1)S(1)}, bf16[2,160,1024]{2,1,0:T(8,128)(2,1)S(1)}, u32[]{:S(2)}, u32[]{:S(2)}) collective-permute-start(bf16[2,160,1024]{2,1,0:T(8,128)(2,1)S(1)} %get-tuple-element.52), channel_id=1, source_target_pairs={{0,2},{1,3},{2,0},{3,1},{4,6},{5,7},{6,4},{7,5},{8,10},{9,11},{10,... | collective-permute-start | bytes 1966088 | tf_op jit(solution)/shard_map/ppermute | solution.py:335
  575.1 53.0 %collective-permute-start.55 = (bf16[2,160,1024]{2,1,0:T(8,128)(2,1)S(1)}, bf16[2,160,1024]{2,1,0:T(8,128)(2,1)S(1)}, u32[]{:S(2)}, u32[]{:S(2)}) collective-permute-start(bf16[2,160,1024]{2,1,0:T(8,128)(2,1)S(1)} %get-tuple-element.52), channel_id=1, source_target_pairs={{0,1},{1,2},{2,3},{3,0},{4,5},{5,6},{6,7},{7,4},{8,9},{9,10},{10,1... | collective-permute-start | bytes 1966088 | tf_op jit(solution)/shard_map/ppermute | solution.py:335
  (122 other events, 1841.6 us)

commit v2 on v1

v2 whole, which is shorter than its diff:
```python
import functools
import math

import jax
import jax.numpy as jnp
from jax import lax
from jax.experimental import pallas as pl
from jax.experimental.pallas import tpu as pltpu
from jax.sharding import PartitionSpec as P

WINDOW = 512
BUCKETS = 32
REACH = 128
EPSILON = 1e-05
MASKED = -1e30
GELU_C = 0.7978845608028654
GELU_A = 0.044715
BF = jnp.bfloat16
F32 = jnp.float32


def cost(us):
    return pl.CostEstimate(
        flops=int(us * 1e9), transcendentals=0, bytes_accessed=int(us * 3e6)
    )


def bucket_edges(bucket_total, far_reach, window):
    exact_count = bucket_total // 2
    boundaries = []
    current = 0
    for distance in range(window):
        if distance < exact_count:
            bucket = distance
        else:
            bucket = exact_count + int(
                math.log(distance / exact_count)
                / math.log(far_reach / exact_count)
                * (bucket_total - exact_count)
            )
            bucket = min(bucket, bucket_total - 1)
        while current < bucket:
            current = current + 1
            boundaries.append(distance)
    return boundaries


EDGES = bucket_edges(BUCKETS, REACH, WINDOW)


def mm(left, right):
    return lax.dot_general(left, right, (((1,), (0,)), ((), ())), preferred_element_type=F32)


def mm_nt(left, right):
    return lax.dot_general(left, right, (((1,), (1,)), ((), ())), preferred_element_type=F32)


def mm_tn(left, right):
    return lax.dot_general(left, right, (((0,), (0,)), ((), ())), preferred_element_type=F32)


def bias_tables(rb_ref, h, levels, seg, bm_ref):
    row = lax.broadcasted_iota(jnp.int32, (seg, seg), 0)
    col = lax.broadcasted_iota(jnp.int32, (seg, seg), 1)
    for lev in range(levels):
        dist = lev * seg + row - col
        low, high = lev * seg - (seg - 1), lev * seg + seg - 1
        if low >= EDGES[-1]:
            val = jnp.full((seg, seg), rb_ref[h, BUCKETS - 1], F32)
        else:
            val = jnp.full((seg, seg), rb_ref[h, 0], F32)
            for i, edge in enumerate(EDGES):
                if edge <= high:
                    val = jnp.where(dist >= edge, rb_ref[h, i + 1], val)
        if low < 0:
            val = jnp.where(dist >= 0, val, MASKED)
        if high >= WINDOW:
            val = jnp.where(dist < WINDOW, val, MASKED)
        bm_ref[:, lev * seg : (lev + 1) * seg] = val


def chain(par_ref, t, first, levels, all_segs, local_segs, ctx):
    out = []
    anc = first
    for lev in range(levels):
        if lev > 0:
            up = par_ref[t, jnp.maximum(anc, 0)]
            anc = jnp.where(anc >= 0, up, -1)
        safe = jnp.maximum(anc, 0)
        owner = lax.div(safe, local_segs)
        out.append((anc >= 0, jnp.bitwise_xor(owner, ctx), safe - owner * local_segs))
    return out


def scores_of(q, kw_ref, bm_ref, line, length, levels, seg, factor):
    win = levels * seg
    col = lax.broadcasted_iota(jnp.int32, (1, seg), 1)
    raw = mm_nt(q, kw_ref[...]) * factor
    parts = []
    for lev in range(levels):
        part = raw[:, lev * seg : (lev + 1) * seg] + bm_ref[:, lev * seg : (lev + 1) * seg]
        if lev == 0:
            part = part + jnp.where(col < length, 0.0, MASKED)
        else:
            part = part + jnp.where(line[lev][0], 0.0, MASKED)
        parts.append(part)
    parts.append(raw[:, win:])
    return jnp.concatenate(parts, axis=1)


def fill_sources(parts_k, parts_v, kall, vall, kw, vw, rows, win):
    for b in range(len(parts_k)):
        for src, dst, wide in ((parts_k[b], kall, kw), (parts_v[b], vall, vw)):
            dst[b] = src[0, :rows, :]
            n = src.shape[1] - rows
            wide[win + b * n : win + (b + 1) * n, :] = src[0, rows:, :]


def fetch_window(line, kall, vall, kw, vw, seg):
    for lev, (_, part, block) in enumerate(line):
        start = pl.multiple_of(block * seg, seg)
        kw[lev * seg : (lev + 1) * seg, :] = kall[part, pl.ds(start, seg), :]
        vw[lev * seg : (lev + 1) * seg, :] = vall[part, pl.ds(start, seg), :]


def attend_kernel(dims, par_ref, len_ref, pos_ref, rb_ref, q_ref, *refs):
    levels, seg, local_segs, all_segs, factor, nt = dims
    parts_k, parts_v = refs[0:4], refs[4:8]
    att_refs, lse_ref = refs[8 : 8 + nt], refs[8 + nt]
    kall, vall, kw, vw, bm, whole = refs[9 + nt :]
    t, h = pl.program_id(0), pl.program_id(1)
    ctx, zi = pos_ref[0], pos_ref[1]
    rows, win = local_segs * seg, levels * seg
    bias_tables(rb_ref, h, levels, seg, bm)
    fill_sources(parts_k, parts_v, kall, vall, kw, vw, rows, win)

    def one(s, carry):
        line = chain(par_ref, t, ctx * local_segs + s, levels, all_segs, local_segs, ctx)
        fetch_window(line, kall, vall, kw, vw, seg)
        at = pl.ds(pl.multiple_of(s * seg, seg), seg)
        score = scores_of(q_ref[0, at, :], kw, bm, line, len_ref[t, s], levels, seg, factor)
        top = jnp.max(score, axis=1, keepdims=True)
        prob = jnp.exp(score - top)
        total = jnp.sum(prob, axis=1, keepdims=True)
        lse_ref[0, 0, at, :] = jnp.broadcast_to(top + jnp.log(total), (seg, 128))
        att = mm(prob.astype(BF), vw[...]) / total
        whole[at, :] = att.astype(BF)
        return carry

    lax.fori_loop(0, local_segs, one, 0)
    n = rows // nt
    for j in range(nt):
        k = lax.rem(zi - j + nt, nt)
        att_refs[j][0] = whole[pl.ds(pl.multiple_of(k * n, n), n), :]


def attend_back_kernel(dims, par_ref, len_ref, pos_ref, rb_ref, q_ref, *refs):
    levels, seg, local_segs, all_segs, factor, nt = dims
    parts_k, parts_v = refs[0:4], refs[4:8]
    do_refs, lse_ref = refs[8 : 8 + nt], refs[8 + nt]
    dq_refs = refs[9 + nt : 9 + 2 * nt]
    dq_ref, near_ref, far_ref, db_ref = refs[9 + 2 * nt : 13 + 2 * nt]
    kall, vall, kw, vw, bm, dk, dv, near, far, dos = refs[13 + 2 * nt :]
    h, t = pl.program_id(0), pl.program_id(1)
    ctx, zi = pos_ref[0], pos_ref[1]
    rows, win = local_segs * seg, levels * seg
    states = kw.shape[0] - win
    each = states // 4
    n = rows // nt
    bias_tables(rb_ref, h, levels, seg, bm)
    fill_sources(parts_k, parts_v, kall, vall, kw, vw, rows, win)
    dk[...] = jnp.zeros(dk.shape, F32)
    dv[...] = jnp.zeros(dv.shape, F32)
    for j in range(nt):
        k = lax.rem(zi - j + nt, nt)
        dos[pl.ds(pl.multiple_of(k * n, n), n), :] = do_refs[j][0]

    @pl.when(t == 0)
    def _():
        near[...] = jnp.zeros(near.shape, F32)
        far[...] = jnp.zeros(far.shape, F32)

    def one(s, carry):
        line = chain(par_ref, t, ctx * local_segs + s, levels, all_segs, local_segs, ctx)
        fetch_window(line, kall, vall, kw, vw, seg)
        at = pl.ds(pl.multiple_of(s * seg, seg), seg)
        q = q_ref[0, at, :]
        do = dos[at, :]
        score = scores_of(q, kw, bm, line, len_ref[t, s], levels, seg, factor)
        prob = jnp.exp(score - lse_ref[0, 0, at, :][:, 0:1])
        dprob = mm_nt(do, vw[...])
        delta = jnp.sum(prob * dprob, axis=1, keepdims=True)
        dscore = (prob * (dprob - delta)).astype(BF)
        dq_ref[0, at, :] = (mm(dscore, kw[...]) * factor).astype(BF)
        near[...] += dscore[:, : 2 * seg].astype(F32)
        tail = dscore[:, 2 * seg : 3 * seg].astype(F32)
        for lev in range(3, levels):
            tail = tail + dscore[:, lev * seg : (lev + 1) * seg].astype(F32)
        far[...] += tail
        gk = mm_tn(dscore, q) * factor
        gv = mm_tn(prob.astype(BF), do)
        for lev, (_, part, block) in enumerate(line):
            start = pl.ds(pl.multiple_of(block * seg, seg), seg)
            dk[part, start, :] += gk[lev * seg : (lev + 1) * seg]
            dv[part, start, :] += gv[lev * seg : (lev + 1) * seg]
        for b in range(4):
            dk[b, rows:, :] += gk[win + b * each : win + (b + 1) * each]
            dv[b, rows:, :] += gv[win + b * each : win + (b + 1) * each]
        return carry

    lax.fori_loop(0, local_segs, one, 0)
    for ref, pair in ((near_ref, (0, 2)), (far_ref, (1, 3))):
        for place, b in enumerate(pair):
            ref[place, 0, 0] = dk[b].astype(BF)
            ref[place, 1, 0] = dv[b].astype(BF)
    for j in range(nt):
        k = lax.rem(zi - j + nt, nt)
        dq_refs[j][0] = dq_ref[0, pl.ds(pl.multiple_of(k * n, n), n), :]

    @pl.when(t == pl.num_programs(1) - 1)
    def _():
        row = lax.broadcasted_iota(jnp.int32, (seg, seg), 0)
        col = lax.broadcasted_iota(jnp.int32, (seg, seg), 1)
        edges = [-(10**6)] + list(EDGES) + [10**6]
        for b in range(BUCKETS):
            total = far[...] if b == BUCKETS - 1 else jnp.zeros((seg, seg), F32)
            for lev in range(2):
                dist = lev * seg + row - col
                inside = (dist >= edges[b]) & (dist < edges[b + 1])
                total = total + jnp.where(inside, near[:, lev * seg : (lev + 1) * seg], 0.0)
            db_ref[0, b : b + 1, :] = jnp.sum(total, axis=0, keepdims=True)


def hbm_call(prefetch, body, out_shape, keep=False, **kw):
    if not keep:
        return pl.pallas_call(body, out_shape=out_shape, **kw)
    several = isinstance(out_shape, tuple)
    outs = tuple(
        pltpu.HBM(o.shape, o.dtype) for o in (out_shape if several else (out_shape,))
    )
    kernel = pl.pallas_call(body, out_shape=outs if several else outs[0], **kw)

    def run(*args):
        rest = [pltpu.with_memory_space_constraint(a, pltpu.HBM) for a in args[prefetch:]]
        return kernel(*args[:prefetch], *rest)

    return run


def attention_calls(trees, heads, local_segs, all_segs, seg, each, head_dim, nt):
    levels = WINDOW // seg + 1
    rows = local_segs * seg
    tall = rows + each
    win = levels * seg
    wide = win + 4 * each
    factor = head_dim ** (-0.5)
    dims = (levels, seg, local_segs, all_segs, factor, nt)
    assert EDGES[-1] <= 2 * seg - (seg - 1)
    base_scratch = [
        pltpu.VMEM((4, rows, head_dim), BF),
        pltpu.VMEM((4, rows, head_dim), BF),
        pltpu.VMEM((wide, head_dim), BF),
        pltpu.VMEM((wide, head_dim), BF),
        pltpu.VMEM((seg, win), F32),
    ]

    def specs(order):
        def at(col):
            return pl.BlockSpec(
                (1, tall, head_dim), lambda a, b, *_: (order(a, b)[0], 0, col(order(a, b)[1]))
            )

        k, v = at(lambda h: h), at(lambda h: heads + h)
        return [k, k, k, k, k, v, v, v, v]

    th = lambda a, b: (a, b)
    ht = lambda a, b: (b, a)
    chunk_shape = jax.ShapeDtypeStruct((trees, rows // nt, heads * head_dim), BF)

    def chunk_spec(order):
        return pl.BlockSpec(
            (1, rows // nt, head_dim), lambda a, b, *_: (order(a, b)[0], 0, order(a, b)[1])
        )

    forward = hbm_call(
        4,
        functools.partial(attend_kernel, dims),
        out_shape=(chunk_shape,) * nt + (jax.ShapeDtypeStruct((trees, heads, rows, 128), F32),),
        grid_spec=pltpu.PrefetchScalarGridSpec(
            num_scalar_prefetch=4,
            grid=(trees, heads),
            in_specs=specs(th),
            out_specs=(chunk_spec(th),) * nt
            + (pl.BlockSpec((1, 1, rows, 128), lambda t, h, *_: (t, h, 0, 0)),),
            scratch_shapes=base_scratch + [pltpu.VMEM((rows, head_dim), BF)],
        ),
        compiler_params=pltpu.CompilerParams(vmem_limit_bytes=24 << 20),
        cost_estimate=cost(16),
        keep=True,
        name="attend",
    )
    pair = jax.ShapeDtypeStruct((2, 2, trees, tall, heads * head_dim), BF)
    pair_spec = pl.BlockSpec((2, 2, 1, tall, head_dim), lambda h, t, *_: (0, 0, t, 0, h))
    backward = hbm_call(
        4,
        functools.partial(attend_back_kernel, dims),
        out_shape=(chunk_shape,) * nt
        + (
            jax.ShapeDtypeStruct((trees, rows, heads * head_dim), BF),
            pair,
            pair,
            jax.ShapeDtypeStruct((heads, BUCKETS, 128), F32),
        ),
        grid_spec=pltpu.PrefetchScalarGridSpec(
            num_scalar_prefetch=4,
            grid=(heads, trees),
            in_specs=specs(ht)
            + [chunk_spec(ht)] * nt
            + [pl.BlockSpec((1, 1, rows, 128), lambda h, t, *_: (t, h, 0, 0))],
            out_specs=(chunk_spec(ht),) * nt
            + (
                pl.BlockSpec((1, rows, head_dim), lambda h, t, *_: (t, 0, h)),
                pair_spec,
                pair_spec,
                pl.BlockSpec((1, BUCKETS, 128), lambda h, t, *_: (h, 0, 0)),
            ),
            scratch_shapes=base_scratch
            + [
                pltpu.VMEM((4, tall, head_dim), F32),
                pltpu.VMEM((4, tall, head_dim), F32),
                pltpu.VMEM((seg, 2 * seg), F32),
                pltpu.VMEM((seg, seg), F32),
                pltpu.VMEM((rows, head_dim), BF),
            ],
        ),
        compiler_params=pltpu.CompilerParams(vmem_limit_bytes=32 << 20),
        cost_estimate=cost(24),
        keep=True,
        name="attend_back",
    )
    return forward, backward


def norm_stats(values):
    mean = jnp.mean(values, axis=-1, keepdims=True)
    centered = values - mean
    scale = lax.rsqrt(jnp.mean(centered * centered, axis=-1, keepdims=True) + EPSILON)
    return centered * scale, scale


def norm_back(grad, xhat, scale, gain):
    scaled = grad * gain
    first = jnp.mean(scaled, axis=-1, keepdims=True)
    second = jnp.mean(scaled * xhat, axis=-1, keepdims=True)
    return scale * (scaled - first - xhat * second)


def gelu_parts(u):
    square = u * u
    th = jnp.tanh(u * (GELU_C + GELU_C * GELU_A * square))
    half = 0.5 * (1.0 + th)
    slope = half + (0.5 * u) * (1.0 - th * th) * (GELU_C + 3.0 * GELU_C * GELU_A * square)
    return u * half, slope


def norm_kernel(gain, shift, tok, st, out):
    each = st.shape[1]
    rows = tok.shape[1]
    for lo in range(0, rows + each, each):
        x = (tok[0, lo : lo + each, :] if lo < rows else st[0]).astype(F32)
        xhat, _ = norm_stats(x)
        out[0, lo : lo + each, :] = (xhat * gain[...] + shift[...]).astype(BF)


def project_kernel(pos, x, *refs):
    if len(refs) == 3:
        w = refs[0]
        q_ref, kv_ref = refs[1:]
    else:
        wq, wk, wv, near, over, q_ref, kv_ref, w = refs

        @pl.when((pl.program_id(0) == 0) & (pl.program_id(1) == 0))
        def _():
            fi, core = pos[2], pos[0] & 1
            depth, cols = wq.shape
            half = depth // 2
            for i, part in enumerate((wq, wk, wv)):
                w[pl.ds(pl.multiple_of(fi * depth, depth), depth), i * cols : (i + 1) * cols] = (
                    part[...]
                )
            base = (1 - fi) * depth
            w[pl.ds(pl.multiple_of(base + core * half, half), half), :] = near[...]
            w[pl.ds(pl.multiple_of(base + (1 - core) * half, half), half), :] = over[...]

    y = mm(x[0], w[...]).astype(BF)
    cols = q_ref.shape[2]
    q_ref[0] = y[:, :cols]
    kv_ref[0] = y[:, cols:]


def load_projection(pos, blocks, w):
    n = len(blocks) if blocks[0].shape[1] == w.shape[1] else len(blocks) // 2
    rows, depth = blocks[0].shape
    for j in range(n):
        at = slice(j * rows, (j + 1) * rows)
        if n == len(blocks):
            w[at, :] = blocks[j][...]
        else:
            fi = pos[2]
            w[at, pl.ds(pl.multiple_of(fi * depth, depth), depth)] = blocks[j][...]
            w[at, pl.ds(pl.multiple_of((1 - fi) * depth, depth), depth)] = blocks[n + j][...]


def mix_kernel(n, pos, *refs):
    att, blocks = refs[:n], refs[n:-8]
    tok, cell, gain, shift, hid_ref, n2_ref, stat_ref, w = refs[-8:]

    @pl.when(pl.program_id(0) == 0)
    def _():
        load_projection(pos, blocks, w)
        stat_ref[...] = jnp.zeros(stat_ref.shape, F32)

    cols = att[0].shape[2]
    branch = mm(att[0][0], w[:cols, :])
    for j in range(1, n):
        branch = branch + mm(att[j][0], w[j * cols : (j + 1) * cols, :])
    x = tok[0].astype(F32)
    gated = cell[...] * branch
    hidden = x + gated
    hid_ref[0] = hidden
    xhat, _ = norm_stats(hidden)
    n2_ref[0] = (xhat * gain[...] + shift[...]).astype(BF)
    stat_ref[0:1, :] += jnp.sum(x * x, axis=0, keepdims=True)
    stat_ref[1:2, :] += jnp.sum(gated * gated, axis=0, keepdims=True)


def ff_kernel(*refs):
    xs, gs = refs[0:4], refs[4:8]
    pack, near_ref, far_ref, act_ref, gup_ref, xall, gall, win, wout = refs[8:]
    nt, nf, _, depth, fc = pack.shape
    width = nf * depth
    for z in range(nt):
        for f in range(nf):
            win[z, f * depth : (f + 1) * depth, :] = pack[z, f, 0]
            wout[z, f * depth : (f + 1) * depth, :] = pack[z, f, 1]
    for p in range(4):
        xall[p] = xs[p][...]
        gall[p] = gs[p][...]
    step = 256

    def one(i, carry):
        p = lax.rem(i + 2, 4)
        x, g = xall[p], gall[p]
        for z in range(nt):
            value, slope = gelu_parts(mm(x, win[z]))
            act_ref[p, :, z * fc : (z + 1) * fc] = value.astype(BF)
            gup_ref[p, :, z * fc : (z + 1) * fc] = (mm(g, wout[z]) * slope).astype(BF)
        for n in range(0, width, step):
            part = mm_nt(gup_ref[p, :, :fc], win[0, n : n + step, :])
            for z in range(1, nt):
                part = part + mm_nt(
                    gup_ref[p, :, z * fc : (z + 1) * fc], win[z, n : n + step, :]
                )
            part = part.astype(BF)

            @pl.when(p < 2)
            def _():
                near_ref[p, :, n : n + step] = part

            @pl.when(p >= 2)
            def _():
                far_ref[p - 2, :, n : n + step] = part

        return carry

    lax.fori_loop(0, 4, one, 0)


def ff_grad_kernel(*refs):
    xs, gs = refs[0:4], refs[4:8]
    act, gup, pack, sent_ref, near_ref, far_ref, xall, gall, acc, wout = refs[8:]
    _, nf, _, depth, fc = pack.shape
    mine = xs[0].shape[0]

    @pl.when(pl.program_id(0) == 0)
    def _():
        for p in range(4):
            xall[p * mine : (p + 1) * mine, :] = xs[p][...]
            gall[p * mine : (p + 1) * mine, :] = gs[p][...]
        acc[...] = jnp.zeros(acc.shape, F32)

    for f in range(nf):
        wout[f * depth : (f + 1) * depth, :] = pack[0, f, 1]
    a = act[...].reshape(4 * mine, fc)
    acc[...] += mm_nt(a, wout[...])
    for i, part in ((0, mm_tn(xall[...], gup[...].reshape(4 * mine, fc))), (1, mm_tn(gall[...], a))):
        for f in range(nf):
            sent_ref[f, 0, i] = part[f * depth : (f + 1) * depth].astype(BF)

    @pl.when(pl.program_id(0) == pl.num_programs(0) - 1)
    def _():
        near_ref[...] = acc[: 2 * mine, :].reshape(near_ref.shape).astype(BF)
        far_ref[...] = acc[2 * mine :, :].reshape(far_ref.shape).astype(BF)


def branch_back_kernel(nt, pos, *refs):
    blocks, (own, got, far, hid, cot, cell, gain) = refs[: -(nt + 11)], refs[-(nt + 11) : -(nt + 4)]
    gh_ref, gb_ref = refs[-(nt + 4) : -(nt + 2)]
    ga_refs, stat_ref, w = refs[-(nt + 2) : -2], refs[-2], refs[-1]

    @pl.when(pl.program_id(0) == 0)
    def _():
        load_projection(pos, blocks, w)
        stat_ref[...] = jnp.zeros(stat_ref.shape, F32)

    grad = own[0, 0].astype(F32) + got[0, 0].astype(F32) + far[0].astype(F32)
    xhat, scale = norm_stats(hid[0])
    gh = cot[0].astype(F32) + norm_back(grad, xhat, scale, gain[...])
    gh_ref[0] = gh
    gb = (cell[...] * gh).astype(BF)
    gb_ref[0] = gb
    cols = ga_refs[0].shape[2]
    for j, ref in enumerate(ga_refs):
        ref[0] = mm_nt(gb, w[j * cols : (j + 1) * cols, :]).astype(BF)

    stat_ref[0:1, :] += jnp.sum(grad * xhat, axis=0, keepdims=True)
    stat_ref[1:2, :] += jnp.sum(grad, axis=0, keepdims=True)


def combine_kernel(rows, pos, own, got, far, *refs):
    nt = (len(refs) - 1) // 2
    dq, total_ref, send = refs[:nt], refs[nt], refs[nt + 1 :]
    total = (
        own[0, 0, 0].astype(F32) + got[0, 0, 0].astype(F32) + far[0, 0].astype(F32)
    ).astype(BF)
    total_ref[0, 0] = total
    n = rows // nt
    m = (total_ref.shape[2] - rows) // nt
    kv = pl.program_id(1)
    for j in range(nt):
        k = lax.rem(pos[1] - j + nt, nt)

        @pl.when(kv == 0)
        def _():
            send[j][0, 0, :n, :] = dq[j][0]
            send[j][0, 0, n:, :] = jnp.zeros((m, dq[j].shape[2]), BF)

        send[j][1 + kv, 0, :n, :] = total_ref[0, 0, pl.ds(pl.multiple_of(k * n, n), n), :]
        send[j][1 + kv, 0, n:, :] = total_ref[0, 0, pl.ds(pl.multiple_of(rows + k * m, m), m), :]


def input_back_kernel(nt, pos, *refs):
    blocks = refs[:nt]
    w, tok, st, gh, gain, out_ref, stat_ref = refs[nt:]
    cols = blocks[0].shape[3]
    n = tok.shape[1]
    every = None
    for j in range(nt):
        k = lax.rem(pos[1] + j, nt)
        for i in range(3):
            part = mm_nt(blocks[j][i, 0], w[k, :, i * cols : (i + 1) * cols])
            every = part if every is None else every + part

    @pl.when(pl.program_id(0) == 0)
    def _():
        stat_ref[...] = jnp.zeros(stat_ref.shape, F32)

    for x_ref, grad, lo, hi, extra in (
        (tok, every[:n], 0, n, gh),
        (st, every[n:], n, every.shape[0], None),
    ):
        xhat, scale = norm_stats(x_ref[0].astype(F32))
        back = norm_back(grad, xhat, scale, gain[...])
        if extra is not None:
            back = back + extra[0]
        out_ref[0, lo:hi, :] = back.astype(BF)
        stat_ref[0:1, :] += jnp.sum(grad * xhat, axis=0, keepdims=True)
        stat_ref[1:2, :] += jnp.sum(grad, axis=0, keepdims=True)


def qkv_grad_kernel(nf, pos, x, gq, gkv, far_ref, mid_ref, own_ref, acc, right):
    t = pl.program_id(0)
    rows, cols = gq.shape[1], gq.shape[2]
    tall = x.shape[1]
    right[:rows, :cols] = gq[0]
    right[rows:, :cols] = jnp.zeros((tall - rows, cols), BF)
    right[:, cols : 2 * cols] = gkv[0, 0]
    right[:, 2 * cols :] = gkv[1, 0]
    part = mm_tn(x[0], right[...])

    @pl.when(t == 0)
    def _():
        acc[...] = part

    @pl.when(t > 0)
    def _():
        acc[...] += part

    @pl.when(t == pl.num_programs(0) - 1)
    def _():
        n = own_ref.shape[1]
        for f in range(nf):
            for flip, ref in ((0, own_ref), (2, mid_ref), (1, far_ref), (3, far_ref)):
                k = jnp.bitwise_xor(pos[0], flip)
                start = pl.multiple_of(f * (acc.shape[0] // nf) + k * n, n)
                piece = acc[pl.ds(start, n), :]
                if flip & 1:
                    ref[flip // 2, f] = piece.astype(BF)
                else:
                    ref[f] = piece


def order_kernel(sizes, places, *refs):
    outs = refs[-len(sizes) :]
    for i, block in enumerate(refs[: -len(sizes)]):
        lo = 0
        for n, out in zip(sizes, outs):
            out[0, pl.ds(pl.multiple_of(places[i] * n, n), n), :] = block[0, lo : lo + n, :]
            lo = lo + n


def finish_ff_kernel(rows, pos, *refs):
    gin, gout, gatt = refs[4:]
    depth, fc = gin.shape[0], refs[0].shape[1]
    for flip, b in zip((0, 2, 1, 3), refs[:4]):
        k = jnp.bitwise_xor(pos[0], flip)
        at = pl.ds(pl.multiple_of(k * fc, fc), fc)
        gin[:, at] = b[:depth, :].astype(F32)
        gout[at, :] = b[depth : 2 * depth, :].astype(F32).T
        att = pl.ds(pl.multiple_of(k * rows, rows), rows)
        for i in range(depth // fc):
            lo = 2 * depth + i * rows
            gatt[att, i * fc : (i + 1) * fc] = b[lo : lo + rows, :].astype(F32)


def finish_qkv_kernel(pos, *refs):
    for flip, b in zip((0, 2, 1, 3), refs[:4]):
        n = b.shape[0]
        at = pl.ds(pl.multiple_of(jnp.bitwise_xor(pos[0], flip) * n, n), n)
        for i, out in enumerate(refs[4:]):
            cols = out.shape[1]
            out[at, :] = b[:, i * cols : (i + 1) * cols].astype(F32)


def build(mesh):
    nf, nc, nt = mesh.shape["fsdp"], mesh.shape["context"], mesh.shape["tensor"]
    assert nc == 4

    def px(x):
        return lax.ppermute(x, "fsdp", [(0, 1), (1, 0)])

    def pc(x, k):
        return lax.ppermute(x, "context", [(a, a ^ k) for a in range(nc)])

    def pz(x, j):
        return lax.ppermute(x, "tensor", [(a, (a - j) % nt) for a in range(nt)])

    def ps(x, j):
        return lax.ppermute(x, "tensor", [(a, (a + j) % nt) for a in range(nt)])

    def on_device(
        tokens,
        state,
        parent,
        seg_length,
        cell_gate,
        norm1_gain,
        norm1_shift,
        w_query,
        w_key,
        w_value,
        w_attn_out,
        rel_bias,
        norm2_gain,
        norm2_shift,
        w_in,
        w_out,
        cotangent,
    ):
        trees, rows, width = tokens.shape
        local_segs = seg_length.shape[1]
        seg = rows // local_segs
        all_segs = parent.shape[1]
        heads = rel_bias.shape[0]
        depth, cols = w_query.shape
        head_dim = cols // heads
        each = state.shape[1]
        tall = rows + each
        fi, ci, zi = lax.axis_index("fsdp"), lax.axis_index("context"), lax.axis_index("tensor")
        core = ci & 1
        zr, zs = rows // nt, each // nt
        mine = trees * zr
        pos = jnp.stack([ci, zi, fi]).astype(jnp.int32)
        cell, gain_1, shift_1, gain_2, shift_2 = (
            v.reshape(1, width)
            for v in (cell_gate, norm1_gain, norm1_shift, norm2_gain, norm2_shift)
        )
        sds = jax.ShapeDtypeStruct

        def gate(*xs):
            return lax.optimization_barrier(xs)

        stat = sds((8, width), F32)

        def call(body, grid, ins, outs, out_shape, scratch=(), prefetch=1, vmem=24, name="", us=4, keep=False):
            return hbm_call(
                prefetch,
                body,
                out_shape=out_shape,
                grid_spec=pltpu.PrefetchScalarGridSpec(
                    num_scalar_prefetch=prefetch,
                    grid=grid,
                    in_specs=ins,
                    out_specs=outs,
                    scratch_shapes=scratch,
                ),
                compiler_params=pltpu.CompilerParams(vmem_limit_bytes=vmem << 20),
                cost_estimate=cost(us),
                keep=keep,
                name=name,
            )

        def whole(shape):
            return pl.BlockSpec(shape, lambda *_: (0,) * len(shape))

        row_1 = whole((1, width))
        stat_spec = whole((8, width))

        def place(blocks, starts, axis, total):
            shape = list(blocks[0].shape)
            shape[axis] = total
            out = jnp.zeros(shape, blocks[0].dtype)
            for block, start in zip(blocks, starts):
                out = lax.dynamic_update_slice_in_dim(out, block, start, axis)
            return out

        def half_of(x, k, axis, parts):
            n = x.shape[axis] // parts
            return lax.dynamic_slice_in_dim(x, k * n, n, axis)

        def gather_f(x, axis):
            n = x.shape[axis]
            if nf == 2:
                return place([x, px(x)], [fi * n, (1 - fi) * n], axis, 2 * n)
            return lax.all_gather(x, "fsdp", axis=axis, tiled=True)

        def scatter_f(x, axis):
            if nf == 2:
                sent = half_of(x, 1 - fi, axis, 2).astype(BF)
                return half_of(x, fi, axis, 2) + px(sent).astype(F32)
            return lax.psum_scatter(
                x.astype(BF), "fsdp", scatter_dimension=axis, tiled=True
            ).astype(F32)

        def gather_c(x, axis):
            n = x.shape[axis]
            pair = jnp.stack([x, pc(x, 2)])
            over = pc(pair, 1)
            return place(
                [x, pair[1], over[0], over[1]],
                [ci * n, (ci ^ 2) * n, (ci ^ 1) * n, (ci ^ 3) * n],
                axis,
                nc * n,
            )

        def scatter_c(x, axis):
            cut = lambda k: half_of(x, k, axis, nc)
            sent = jnp.stack([cut(ci ^ 1), cut(ci ^ 3)]).astype(BF)
            got = pc(sent, 1).astype(F32)
            far = (cut(ci ^ 2) + got[1]).astype(BF)
            return cut(ci) + got[0] + pc(far, 2).astype(F32)

        if nf == 2:
            half = depth // 2
            near_send = jnp.concatenate(
                [half_of(w, core, 0, 2) for w in (w_query, w_key, w_value)], axis=1
            )
            near_send, w_in, w_out = gate(near_send, w_in, w_out)
            near_w = px(near_send)
            near_w, w_attn_out = gate(near_w, w_attn_out)
            over_w = pc(near_w, 1)
            weights = (w_query, w_key, w_value, near_w, over_w)
            weight_specs = [whole((depth, cols))] * 3 + [whole((half, 3 * cols))] * 2
            w_scratch = [pltpu.VMEM((2 * depth, 3 * cols), BF)]
        else:
            full_w = lax.all_gather(
                jnp.concatenate([w_query, w_key, w_value], axis=1), "fsdp", axis=0, tiled=True
            )
            weights = (full_w,)
            weight_specs = [whole(full_w.shape)]
            w_scratch = []

        fc = w_in.shape[1] // nc
        pack = jnp.stack([half_of(w_in, ci, 1, nc), half_of(w_out, ci, 0, nc).T])
        packs = lax.all_gather(pack, ("tensor", "fsdp"), axis=0, tiled=False)
        packs = packs.reshape(nt, nf, 2, depth, fc)

        o_blocks = [w_attn_out] + [pz(w_attn_out, j) for j in range(1, nt)]
        o_over = [px(w_attn_out)] if nf == 2 else []

        normed = call(
            norm_kernel,
            (trees,),
            [
                row_1,
                row_1,
                pl.BlockSpec((1, rows, width), lambda t: (t, 0, 0)),
                pl.BlockSpec((1, each, width), lambda t: (t, 0, 0)),
            ],
            pl.BlockSpec((1, tall, width), lambda t: (t, 0, 0)),
            sds((trees, tall, width), BF),
            prefetch=0,
            name="norm",
            us=5,
        )(gain_1, shift_1, tokens, state)
        tile = tall // 3
        queries, kv = call(
            project_kernel,
            (trees, 3),
            [pl.BlockSpec((1, tile, width), lambda t, i, *_: (t, i, 0))] + weight_specs,
            (
                pl.BlockSpec((1, tile, cols), lambda t, i, *_: (t, i, 0)),
                pl.BlockSpec((1, tile, 2 * cols), lambda t, i, *_: (t, i, 0)),
            ),
            (sds((trees, tall, cols), BF), sds((trees, tall, 2 * cols), BF)),
            w_scratch,
            name="project",
        )(pos, normed, *weights)
        kv_y = pc(kv, 2)
        kv_c = pc(kv, 1)
        grad_low = half_of(cotangent, zi, 1, nt).reshape(mine, width)
        kv_y, grad_low, *o_blocks = gate(kv_y, grad_low, *o_blocks)
        kv_cy = pc(kv_y, 1)
        if nf == 2:
            o_over += [px(b) for b in o_blocks[1:]]
        else:
            full = lax.all_gather(jnp.stack(o_blocks), "fsdp", axis=2, tiled=True)
            o_blocks = [full[j] for j in range(nt)]
        grad_y = pc(grad_low, 2)
        grad_c = pc(grad_low, 1)

        forward, backward = attention_calls(
            trees, heads, local_segs, all_segs, seg, each, head_dim, nt
        )
        tables = (parent, seg_length, pos, rel_bias)
        sources = (queries, kv, kv_c, kv_y, kv_cy, kv, kv_c, kv_y, kv_cy)
        *att_send, log_total = forward(*tables, *sources)
        quarter = jnp.concatenate(
            [half_of(w, ci, 0, nc) for w in (w_query, w_key, w_value)], axis=1
        )
        att_send[0], quarter, grad_y, *o_over = gate(att_send[0], quarter, grad_y, *o_over)
        all_w = lax.all_gather(quarter, ("tensor", "fsdp", "context"), axis=0, tiled=False)
        all_w = all_w.reshape(nt, nf * depth, 3 * cols)
        grad_rows = [grad_low, grad_y, grad_c, pc(grad_y, 1)]

        att = [att_send[0]] + [pz(att_send[j], j) for j in range(1, nt)]
        chunk = pl.BlockSpec((1, zr, width), lambda t, *_: (t, 0, 0))
        chunk_z = pl.BlockSpec((1, zr, width), lambda t, pos: (t, pos[1], 0))
        small = pl.BlockSpec((1, zr, cols), lambda t, *_: (t, 0, 0))
        o_all = tuple(o_blocks) + tuple(o_over)
        o_specs = [whole(o_all[0].shape)] * len(o_all)
        o_scratch = [pltpu.VMEM((nt * cols, width), BF)]
        hidden, normed_two, stat_a = call(
            functools.partial(mix_kernel, nt),
            (trees,),
            [small] * nt + o_specs + [chunk_z, row_1, row_1, row_1],
            (chunk, chunk, stat_spec),
            (sds((trees, zr, width), F32), sds((trees, zr, width), BF), stat),
            o_scratch,
            name="mix",
            keep=True,
        )(pos, *att, *o_all, tokens, cell, gain_2, shift_2)

        rows_two = normed_two.reshape(mine, width)
        rows_y = pc(rows_two, 2)
        ff_rows = [rows_two, rows_y, pc(rows_two, 1), pc(rows_y, 1)]
        block = whole((mine, width))
        units = nt * fc
        half_spec, full_spec = whole((2, mine, width)), whole((4, mine, units))
        half_sds, full_sds = sds((2, mine, width), BF), sds((4, mine, units), BF)
        gn_near, gn_far, active, grad_up = call(
            ff_kernel,
            (1,),
            [block] * 8 + [whole(packs.shape)],
            (half_spec, half_spec, full_spec, full_spec),
            (half_sds, half_sds, full_sds, full_sds),
            [pltpu.VMEM((4, mine, width), BF)] * 2 + [pltpu.VMEM((nt, width, fc), BF)] * 2,
            prefetch=0,
            vmem=48,
            name="feed",
            keep=True,
            us=20,
        )(*ff_rows, *grad_rows, packs)
        gn_got = pc(gn_far, 1)
        gn_mid = (gn_near[1].astype(F32) + gn_got[1].astype(F32)).astype(BF)
        gn_end = pc(gn_mid, 2)
        unit_spec = pl.BlockSpec((4, mine, fc), lambda z, *_: (0, 0, z))
        pack_spec = pl.BlockSpec((1,) + packs.shape[1:], lambda z, *_: (z, 0, 0, 0, 0))
        ff_sent, ff_near, ff_far = call(
            ff_grad_kernel,
            (nt,),
            [block] * 8 + [unit_spec, unit_spec, pack_spec],
            (
                pl.BlockSpec((nf, 1, 2, depth, fc), lambda z, *_: (0, z, 0, 0, 0)),
                half_spec,
                half_spec,
            ),
            (sds((nf, nt, 2, depth, fc), BF), half_sds, half_sds),
            [pltpu.VMEM((4 * mine, width), BF)] * 2
            + [pltpu.VMEM((4 * mine, width), F32), pltpu.VMEM((width, fc), BF)],
            prefetch=0,
            vmem=56,
            name="feed_grads",
            keep=True,
            us=16,
        )(*ff_rows, *grad_rows, active, grad_up, packs)
        gn_end, ff_sent, ff_near, ff_far = gate(gn_end, ff_sent, ff_near, ff_far)
        ff_got = pc(ff_far, 1)

        pair = pl.BlockSpec((1, 1, zr, width), lambda t, *_: (0, t, 0, 0))
        grad_hidden, grad_branch, *rest = call(
            functools.partial(branch_back_kernel, nt),
            (trees,),
            o_specs + [pair, pair, chunk, chunk, chunk_z, row_1, row_1],
            (chunk, chunk) + (small,) * nt + (stat_spec,),
            (sds((trees, zr, width), F32), sds((trees, zr, width), BF))
            + (sds((trees, zr, cols), BF),) * nt
            + (stat,),
            o_scratch,
            name="branch_back",
            keep=True,
        )(
            pos,
            *o_all,
            gn_near.reshape(2, trees, zr, width),
            gn_got.reshape(2, trees, zr, width),
            gn_end.reshape(trees, zr, width),
            hidden,
            cotangent,
            cell,
            gain_2,
        )
        stat_b = rest.pop()
        ff_got, grad_branch, *rest = gate(ff_got, grad_branch, *rest)
        grad_heads = [rest[0]] + [ps(rest[j], j) for j in range(1, nt)]
        ff_mid = (ff_near[1].astype(F32) + ff_got[1].astype(F32)).astype(BF)
        ff_end = pc(ff_mid, 2)
        part_attn = mm_tn(
            jnp.concatenate([a.reshape(mine, cols) for a in att], axis=1),
            grad_branch.reshape(mine, width),
        ).reshape(nt, cols, width)
        cut = lambda k: half_of(part_attn, k, 1, nc)
        attn_got = pc(jnp.stack([cut(ci ^ 1), cut(ci ^ 3)]).astype(BF), 1).astype(F32)
        attn_near = cut(ci) + attn_got[0]
        attn_mid = (cut(ci ^ 2) + attn_got[1]).astype(BF)

        mlp_out = ff_near[0].astype(F32) + ff_got[0].astype(F32) + ff_end.astype(F32)
        result = (hidden.reshape(mine, width) + mlp_out).astype(BF)
        result, attn_near, attn_mid, *grad_heads = gate(
            result, attn_near, attn_mid, *grad_heads
        )
        result = result.reshape(trees, zr, width)
        o_rows = cols // nc

        def spread_near(x):
            if nt == 4:
                return [
                    lax.ppermute(x, "tensor", [(0, 1), (1, 2), (2, 3)]),
                    lax.ppermute(x, "tensor", [(1, 0), (2, 1), (3, 2)]),
                ]
            return [pz(x, 1), pz(x, nt - 1)]

        def ordered(blocks, places, sizes):
            n = blocks[0].shape[1]
            return call(
                functools.partial(order_kernel, sizes),
                (trees,),
                [pl.BlockSpec((1, n, width), lambda t, *_: (t, 0, 0))] * len(blocks),
                tuple(
                    pl.BlockSpec((1, nt * m, width), lambda t, *_: (t, 0, 0)) for m in sizes
                ),
                tuple(sds((trees, nt * m, width), BF) for m in sizes),
                name="order",
                us=1,
            )(jnp.stack(places).astype(jnp.int32), *blocks)

        def swap(x, pairs):
            return lax.ppermute(x, "tensor", pairs + [(b, a) for a, b in pairs])

        first_at = [jnp.maximum(zi - 1, 0), jnp.minimum(zi + 1, nt - 1), zi]
        ends = (zi == 0) | (zi == 3)

        out_near = spread_near(result)
        attn_end = pc(attn_mid, 2)

        *dq_send, grad_q, kv_near, kv_far, bias_rows = backward(
            *tables, *sources, *grad_heads, log_total
        )
        ff_half = lax.psum_scatter(ff_sent, "fsdp", scatter_dimension=0, tiled=True)[0]
        ff_half = ff_half.reshape(nt, 2 * depth, fc)
        kv_far, kv_near, attn_end, *out_near = gate(kv_far, kv_near, attn_end, *out_near)
        kv_got = pc(kv_far, 1)
        kv_mid = (kv_near[1].astype(F32) + kv_got[1].astype(F32)).astype(BF)
        kv_mid, result, attn_end, ff_half = gate(kv_mid, result, attn_end, ff_half)
        kv_end = pc(kv_mid, 2)
        if nt == 4:
            out_far = [swap(result, [(0, 3)]), swap(result, [(0, 2), (1, 3)])]
        else:
            out_far = [pz(result, j) for j in range(2, nt - 1)]
        attn_sum = attn_near + attn_end.astype(F32)
        attn_sum = scatter_f(attn_sum, 2).astype(BF)
        attn_sum = lax.dynamic_slice_in_dim(
            jnp.concatenate([attn_sum, attn_sum], axis=0), nt - zi, nt, 0
        )
        if depth == 2 * fc:
            ff_half = jnp.concatenate(
                [ff_half, attn_sum[:, :, :fc], attn_sum[:, :, fc:]], axis=1
            )
        kv_end, ff_half, attn_sum, *out_far = gate(kv_end, ff_half, attn_sum, *out_far)
        own = lax.psum_scatter(ff_half, "tensor", scatter_dimension=0, tiled=True)[0]
        five = pl.BlockSpec((1, 1, 1, tall, cols), lambda t, k, *_: (0, k, t, 0, 0))
        four = pl.BlockSpec((1, 1, tall, cols), lambda t, k, *_: (k, t, 0, 0))
        send = pl.BlockSpec((3, 1, zr + zs, cols), lambda t, k, *_: (0, t, 0, 0))
        grad_kv, *kv_send = call(
            functools.partial(combine_kernel, rows),
            (trees, 2),
            [five, five, four]
            + [pl.BlockSpec((1, zr, cols), lambda t, k, *_: (t, 0, 0))] * nt,
            (four,) + (send,) * nt,
            (sds((2, trees, tall, cols), BF),) + (sds((3, trees, zr + zs, cols), BF),) * nt,
            name="combine",
            keep=True,
        )(pos, kv_near, kv_got, kv_end, *dq_send)
        dqkv = [kv_send[0]] + [pz(kv_send[j], j) for j in range(1, nt)]

        dq_rows = depth // nc
        cut_specs = (whole((2, nf, dq_rows, 3 * cols)),) + (whole((nf, dq_rows, 3 * cols)),) * 2
        qkv_far, qkv_mid, qkv_own = call(
            functools.partial(qkv_grad_kernel, nf),
            (trees,),
            [
                pl.BlockSpec((1, tall, width), lambda t, *_: (t, 0, 0)),
                pl.BlockSpec((1, rows, cols), lambda t, *_: (t, 0, 0)),
                pl.BlockSpec((2, 1, tall, cols), lambda t, *_: (0, t, 0, 0)),
            ],
            cut_specs,
            (
                sds((2, nf, dq_rows, 3 * cols), BF),
                sds((nf, dq_rows, 3 * cols), F32),
                sds((nf, dq_rows, 3 * cols), F32),
            ),
            [pltpu.VMEM((nf * depth, 3 * cols), F32), pltpu.VMEM((tall, 3 * cols), BF)],
            name="qkv_grads",
            keep=True,
            us=8,
        )(pos, normed, grad_q, grad_kv)
        if nt == 4:
            places = [first_at[0], first_at[1], jnp.where(ends, 3 - zi, zi), zi, zi ^ 2]
            blocks = [out_near[0], out_near[1], out_far[0], result, out_far[1]]
        else:
            blocks = [result, *out_near, *out_far]
            places = [zi, (zi + 1) % nt, (zi - 1) % nt] + [(zi + j) % nt for j in range(2, nt - 1)]
        (output,) = ordered(blocks, places, (zr,))
        qkv_far, qkv_mid, qkv_own, output, *dqkv = gate(
            qkv_far, qkv_mid, qkv_own, output, *dqkv
        )
        qkv_got = pc(qkv_far, 1).astype(F32)

        chunk_sz = pl.BlockSpec((1, zs, width), lambda t, pos: (t, pos[1], 0))
        grads_own, stat_c = call(
            functools.partial(input_back_kernel, nt),
            (trees,),
            [pl.BlockSpec((3, 1, zr + zs, cols), lambda t, *_: (0, t, 0, 0))] * nt
            + [whole(all_w.shape), chunk_z, chunk_sz, chunk, row_1],
            (pl.BlockSpec((1, zr + zs, width), lambda t, *_: (t, 0, 0)), stat_spec),
            (sds((trees, zr + zs, width), BF), stat),
            vmem=32,
            name="input_back",
            keep=True,
        )(pos, *dqkv, all_w, tokens, state, grad_hidden, gain_1)
        qkv_got, grads_own = gate(qkv_got, grads_own)

        bias_own = jnp.sum(bias_rows, axis=2)
        bias_all = lax.dynamic_update_slice(
            jnp.zeros((heads * nt, BUCKETS), F32), bias_own, (zi * heads, 0)
        )
        squares = jnp.stack([jnp.sum(stat_a[0]), jnp.sum(stat_a[1]), jnp.sum(mlp_out * mlp_out)])
        spare = jnp.zeros((2 * width - bias_all.size - 3,), F32)
        early = jnp.concatenate(
            [
                stat_b[:2],
                jnp.concatenate([bias_all.reshape(-1), squares, spare]).reshape(2, width),
            ],
            axis=0,
        )
        early, grads_own = gate(early, grads_own)
        sums = jnp.concatenate([stat_c[:2], early], axis=0)

        in_near = spread_near(grads_own)
        if nt == 4:
            in_far = [swap(grads_own, [(0, 2), (1, 3)])]
        else:
            in_far = [pz(grads_own, j) for j in range(2, nt - 1)]
        qkv_end = pc((qkv_mid + qkv_got[1]).astype(BF), 2)
        if depth == 2 * fc:
            parts = [own]
        else:
            parts = [own, lax.psum_scatter(attn_sum, "tensor", scatter_dimension=0, tiled=True)[0]]
        parts_y = [pc(p, 2) for p in parts]
        sums = sums + px(sums) if nf == 2 else lax.psum(sums, "fsdp")
        sums = sums + pc(sums, 1)
        sums = sums + pc(sums, 2)
        in_far[0], qkv_end, sums, *parts_y = gate(in_far[0], qkv_end, sums, *parts_y)
        if nt == 4:
            in_far.append(
                lax.ppermute(in_far[0], "tensor", [(2, 3), (1, 0), (3, 2), (0, 1)])
            )
            places = first_at + [zi ^ 2, 3 - zi]
            blocks = [in_near[0], in_near[1], grads_own, in_far[0], in_far[1]]
        else:
            blocks = [grads_own, *in_near, *in_far]
        tokens_grad, state_grad = ordered(blocks, places, (zr, zs))
        if nt & (nt - 1):
            sums = lax.psum(sums, "tensor")
        else:
            k = 1
            while k < nt:
                sums = sums + lax.ppermute(sums, "tensor", [(a, a ^ k) for a in range(nt)])
                k = 2 * k

        qkv_sum = scatter_f(qkv_own + qkv_got[0] + qkv_end.astype(F32), 0)[0].astype(BF)
        qkv_y = pc(qkv_sum, 2)
        qkv_blocks = (qkv_sum, qkv_y, pc(qkv_sum, 1), pc(qkv_y, 1))
        grad_qkv = call(
            finish_qkv_kernel,
            (1,),
            [whole((dq_rows, 3 * cols))] * 4,
            (whole((depth, cols)),) * 3,
            (sds((depth, cols), F32),) * 3,
            name="finish_qkv",
            us=1,
        )(pos, *qkv_blocks)
        over = [pc(p, 1) for p in parts] + [pc(p, 1) for p in parts_y]
        if depth == 2 * fc:
            grad_in, grad_out, grad_attn_out = call(
                functools.partial(finish_ff_kernel, o_rows),
                (1,),
                [whole(own.shape)] * 4,
                (whole((depth, nc * fc)), whole((nc * fc, depth)), whole((nc * o_rows, depth))),
                (
                    sds((depth, nc * fc), F32),
                    sds((nc * fc, depth), F32),
                    sds((nc * o_rows, depth), F32),
                ),
                name="finish_ff",
                us=1,
            )(pos, own, parts_y[0], over[0], over[1])
        else:
            flips = (ci, ci ^ 2, ci ^ 1, ci ^ 3)
            ff_blocks = [parts[0], parts_y[0], over[0], over[2]]
            at = [k * fc for k in flips]
            grad_in = place([b[:depth] for b in ff_blocks], at, 1, nc * fc).astype(F32)
            grad_out = place([b[depth:].T for b in ff_blocks], at, 0, nc * fc).astype(F32)
            grad_attn_out = place(
                [parts[1], parts_y[1], over[1], over[3]],
                [k * o_rows for k in flips],
                0,
                nc * o_rows,
            ).astype(F32)

        last = sums[4:].reshape(-1)
        bias_sum = last[: bias_all.size].reshape(bias_all.shape)
        grad_bias = lax.dynamic_slice_in_dim(bias_sum, zi * heads, heads, 0)
        cell_count = trees * rows * width * nf * nc
        norms = jnp.sqrt(last[bias_all.size : bias_all.size + 3] / cell_count)
        return (
            output,
            tokens_grad,
            state_grad,
            *grad_qkv,
            grad_attn_out,
            grad_bias,
            sums[0],
            sums[1],
            sums[2],
            sums[3],
            grad_in,
            grad_out,
            norms,
        )

    return on_device


def solution(mesh):
    return jax.shard_map(
        build(mesh),
        mesh=mesh,
        in_specs=(
            P("fsdp", "context", None),
            P("fsdp", "context", None),
            P("fsdp", None),
            P("fsdp", "context"),
            P(),
            P(),
            P(),
            P("fsdp", "tensor"),
            P("fsdp", "tensor"),
            P("fsdp", "tensor"),
            P("tensor", "fsdp"),
            P("tensor", None),
            P(),
            P(),
            P("fsdp", "tensor"),
            P("tensor", "fsdp"),
            P("fsdp", "context", None),
        ),
        out_specs=(
            P("fsdp", "context", None),
            P("fsdp", "context", None),
            P("fsdp", "context", None),
            P("fsdp", "tensor"),
            P("fsdp", "tensor"),
            P("fsdp", "tensor"),
            P("tensor", "fsdp"),
            P("tensor", None),
            P(),
            P(),
            P(),
            P(),
            P("fsdp", "tensor"),
            P("tensor", "fsdp"),
            P(),
        ),
        check_vma=False,
    )
```

time: 639 us -> 548 us (0.86); the launches traced: 631 us -> 547 us
  Pallas kernels: 39.1 us -> 131 us
  local copies, waits for them, and re-layouts: 81.8 us -> 20.5 us
  waiting for transfers between devices: 315 us -> 269 us
  matrix products: 44.6 us -> 2.87 us
  other arithmetic: 50.2 us -> 29.3 us
  starting transfers between devices: 97.7 us -> 77.8 us
  between operations: 2.64 us -> 16.1 us
    pallas_call x2 -> x15, Pallas kernels: 39.1 us -> 131 us  [the longest x9 113 us: run(): return kernel(*args[:prefetch], *rest)]
    ppermute x10 -> x8, waiting for transfers between devices: 67.4 us -> 28.5 us  [px(): return lax.ppermute(x, 'fsdp', [(0, 1), (1, 0)])]
    dot_general x8 -> x0, matrix products: 32.8 us -> none  [the longest x4 20.3 us: mm_nt(): lax.dot_general(left, right, (((1,), (1,)), ((), ())), preferred_element_...]
    ppermute x42 -> x28, waiting for transfers between devices: 73 us -> 46.9 us  [pc(): return lax.ppermute(x, 'context', [(a, a ^ k) for a in range(nc)])]
    ppermute x30 -> x9, starting transfers between devices: 38.5 us -> 15.7 us  [pz(): return lax.ppermute(x, 'tensor', [(a, (a - j) % nt) for a in range(nt)])]
    dynamic_update_slice x40 -> x0, local copies, waits for them, and re-layouts: 21.8 us -> none  [place(): out = lax.dynamic_update_slice_in_dim(out, block, start, axis)]
    ppermute x30 -> x9, waiting for transfers between devices: 92.3 us -> 112 us  [pz(): return lax.ppermute(x, 'tensor', [(a, (a - j) % nt) for a in range(nt)])]
    ppermute x16 -> x13, starting transfers between devices: 18.9 us -> 33.8 us  [the longest x3 11.7 us: ps(): return lax.ppermute(x, 'tensor', [(a, (a + j) % nt) for a in range(nt)])]
  transfers between devices with their start and end apart: 98 -> 62, of which waited for: 37 -> 29; matrix products, arithmetic and copies ran while one was open for 25% -> 7% of each run, Pallas kernels for 6% -> 19%
where the time goes in v2:
time: 548 us; the launch traced here: 547 us
  waiting for transfers between devices  269 us (49%)
  Pallas kernels  131 us (24%)
  starting transfers between devices  77.8 us (14%)
  other arithmetic  29.3 us (5%)
  local copies, waits for them, and re-layouts  20.5 us (4%)
  between operations  16.1 us (3%)
    pallas_call x9, Pallas kernels, run(): return kernel(*args[:prefetch], *rest)  113 us
    ppermute x9, waiting for transfers between devices, pz(): return lax.ppermute(x, 'tensor', [(a, (a - j) % nt) for a in range(nt)])  112 us
    ppermute x3, waiting for transfers between devices, swap(): return lax.ppermute(x, 'tensor', pairs + [(b, a) for a, b in pairs])  53.2 us
    ppermute x28, waiting for transfers between devices, pc(): return lax.ppermute(x, 'context', [(a, a ^ k) for a in range(nc)])  46.9 us
    ppermute x8, waiting for transfers between devices, px(): return lax.ppermute(x, 'fsdp', [(0, 1), (1, 0)])  28.5 us
    ppermute x28, starting transfers between devices, pc(): return lax.ppermute(x, 'context', [(a, a ^ k) for a in range(nc)])  17.3 us
    ppermute x9, starting transfers between devices, pz(): return lax.ppermute(x, 'tensor', [(a, (a - j) % nt) for a in range(nt)])  15.7 us
    ppermute x1, waiting for transfers between devices, on_device(): lax.ppermute(in_far[0], 'tensor', [(2, 3), (1, 0), (3, 2), (0, 1)])  13.2 us
  transfers between devices with their start and end apart: 62, of which 29 were waited for; matrix products, arithmetic and copies ran while one was open for 7% of the time, Pallas kernels for 19%

profile of v2, /device:TPU:0, one launch (start us, length us, event | category | flops | bytes accessed | tf_op | source)
XLA Modules:
  0.0 546.9 jit_solution(2913625526418412007)
XLA Ops:
  17.3 5.9 %collective-permute-done.refs_3_ = bf16[256,768]{1,0:T(8,128)(2,1)S(1)} collective-permute-done((bf16[256,768]{1,0:T(8,128)(2,1)}, bf16[256,768]{1,0:T(8,128)(2,1)S(1)}, u32[]{:S(2)}, u32[]{:S(2)}) %collective-permute-start) | collective-permute-done | bytes 393248 | tf_op jit(solution)/shard_map/ppermute | solution.py:651
  40.2 11.0 %collective-permute-done.4.refs_5_.refs_1_ = bf16[256,512]{1,0:T(8,128)(2,1)} collective-permute-done((bf16[256,512]{1,0:T(8,128)(2,1)S(1)}, bf16[256,512]{1,0:T(8,128)(2,1)}, u32[]{:S(2)}, u32[]{:S(2)}) %collective-permute-start.4) | collective-permute-done | bytes 262176 | tf_op jit(solution)/shard_map/ppermute | solution.py:657
  51.3 18.1 %collective-permute-done.5.refs_6_.refs_2_ = bf16[256,512]{1,0:T(8,128)(2,1)} collective-permute-done((bf16[256,512]{1,0:T(8,128)(2,1)S(1)}, bf16[256,512]{1,0:T(8,128)(2,1)}, u32[]{:S(2)}, u32[]{:S(2)}) %collective-permute-start.5) | collective-permute-done | bytes 262176 | tf_op jit(solution)/shard_map/ppermute | solution.py:657
  75.5 16.9 %attend.1 = (bf16[2,160,256]{2,1,0:T(8,128)(2,1)}, bf16[2,160,256]{2,1,0:T(8,128)(2,1)}, bf16[2,160,256]{2,1,0:T(8,128)(2,1)}, bf16[2,160,256]{2,1,0:T(8,128)(2,1)}, f32[2,2,640,128]{3,2,1,0:T(8,128)}) custom-call(s32[2,20]{1,0:T(2,128)S(1)} %copy-done.15, s32[2,5]{1,0:T(2,128)S(1)} %copy-done.16, s32[3]{0:T(128)S(1)} %pad_add_fusion.pos.pos_ref, ...), custom_call_target="tpu_custom_call" | custom-call | flops 16000000000 | bytes 48000000 | tf_op jit(solution)/shard_map/attend/pallas_call | solution.py:246
  98.7 8.4 %collective-permute-done.11.refs_10_.refs_6_ = bf16[256,512]{1,0:T(8,128)(2,1)S(1)} collective-permute-done((bf16[256,512]{1,0:T(8,128)(2,1)}, bf16[256,512]{1,0:T(8,128)(2,1)S(1)}, u32[]{:S(2)}, u32[]{:S(2)}) %collective-permute-start.11) | collective-permute-done | bytes 262176 | tf_op jit(solution)/shard_map/ppermute | solution.py:651
  113.1 6.0 %collective-permute-done.15.refs_3_ = bf16[2,160,256]{2,1,0:T(8,128)(2,1)S(1)} collective-permute-done((bf16[2,160,256]{2,1,0:T(8,128)(2,1)}, bf16[2,160,256]{2,1,0:T(8,128)(2,1)S(1)}, u32[]{:S(2)}, u32[]{:S(2)}) %collective-permute-start.15) | collective-permute-done | bytes 163872 | tf_op jit(solution)/shard_map/ppermute | solution.py:657
  126.8 13.6 %collective-permute-done.16.refs_1_ = bf16[320,1024]{1,0:T(8,128)(2,1)S(1)} collective-permute-done((bf16[320,1024]{1,0:T(8,128)(2,1)}, bf16[320,1024]{1,0:T(8,128)(2,1)S(1)}, u32[]{:S(2)}, u32[]{:S(2)}) %collective-permute-start.16) | collective-permute-done | bytes 655392 | tf_op jit(solution)/shard_map/ppermute | solution.py:654
  142.7 22.1 %feed.1 = (bf16[2,320,1024]{2,1,0:T(8,128)(2,1)}, bf16[2,320,1024]{2,1,0:T(8,128)(2,1)}, bf16[4,320,1024]{2,1,0:T(8,128)(2,1)}, bf16[4,320,1024]{2,1,0:T(8,128)(2,1)}) custom-call(bf16[320,1024]{1,0:T(8,128)(2,1)} %bitcast.129, bf16[320,1024]{1,0:T(8,128)(2,1)} %copy-done.41, bf16[320,1024]{1,0:T(8,128)(2,1)} %collective-permute-done.17.refs_2_, ...), custom_call_target="tpu_custom_call" | custom-call | flops 20000000000 | bytes 60000000 | tf_op jit(solution)/shard_map/feed/pallas_call | solution.py:246
  171.2 15.6 %feed_grads.1 = (bf16[2,4,2,512,256]{4,3,2,1,0:T(8,128)(2,1)}, bf16[2,320,1024]{2,1,0:T(8,128)(2,1)}, bf16[2,320,1024]{2,1,0:T(8,128)(2,1)}) custom-call(bf16[320,1024]{1,0:T(8,128)(2,1)} %bitcast.130, bf16[320,1024]{1,0:T(8,128)(2,1)} %copy-done.41, bf16[320,1024]{1,0:T(8,128)(2,1)} %collective-permute-done.17.refs_2_, ...), custom_call_target="tpu_custom_call" | custom-call | flops 16000000000 | bytes 48000000 | tf_op jit(solution)/shard_map/feed_grads/pallas_call | solution.py:246
  188.4 6.6 %branch_back.1 = (f32[2,160,1024]{2,1,0:T(8,128)}, bf16[2,160,1024]{2,1,0:T(8,128)(2,1)}, bf16[2,160,256]{2,1,0:T(8,128)(2,1)}, bf16[2,160,256]{2,1,0:T(8,128)(2...) custom-call(s32[3]{0:T(128)S(1)} %pad_add_fusion.pos.pos_ref, ...), custom_call_target="tpu_custom_call" | custom-call | flops 4000000000 | bytes 12000000 | tf_op jit(solution)/shard_map/branch_back/pallas_call | solution.py:246
  203.7 6.2 %collective-permute-start.26 = (bf16[2,160,256]{2,1,0:T(8,128)(2,1)S(1)}, bf16[2,160,256]{2,1,0:T(8,128)(2,1)S(1)}, u32[]{:S(2)}, u32[]{:S(2)}) collective-permute-start(bf16[2,160,256]{2,1,0:T(8,128)(2,1)S(1)} %copy-done.53), channel_id=1, source_target_pairs={{0,1},{1,2},{2,3},{3,0},{4,5},{5,6},{6,7},{7,4},{8,9},{9,10},{10,1... | collective-permute-start | bytes 491528 | tf_op jit(solution)/shard_map/ppermute | solution.py:660
  226.1 6.9 %collective-permute-start.30 = (bf16[2,160,1024]{2,1,0:T(8,128)(2,1)S(1)}, bf16[2,160,1024]{2,1,0:T(8,128)(2,1)S(1)}, u32[]{:S(2)}, u32[]{:S(2)}) collective-permute-start(bf16[2,160,1024]{2,1,0:T(8,128)(2,1)S(1)} %bitcast.94), channel_id=1, source_target_pairs={{0,1},{1,2},{2,3},{4,5},{5,6},{6,7},{8,9},{9,10},{10,11},{12,13},{... | collective-permute-start | bytes 1966088 | tf_op jit(solution)/shard_map/ppermute | solution.py:969
  235.6 23.4 %attend_back.1 = (bf16[2,160,256]{2,1,0:T(8,128)(2,1)}, bf16[2,160,256]{2,1,0:T(8,128)(2,1)}, bf16[2,160,256]{2,1,0:T(8,128)(2,1)}, bf16[2,160,256]{2,1,0:T(8,12...) custom-call(s32[2,20]{1,0:T(2,128)S(1)} %copy-done.15, ...), custom_call_target="tpu_custom_call" | custom-call | flops 24000000000 | bytes 72000000 | tf_op jit(solution)/shard_map/attend_back/pallas_call | solution.py:246
  260.5 6.0 %collective-permute-done.32.got = bf16[2,2,2,768,256]{4,3,2,1,0:T(8,128)(2,1)} collective-permute-done((bf16[2,2,2,768,256]{4,3,2,1,0:T(8,128)(2,1)}, bf16[2,2,2,768,256]{4,3,2,1,0:T(8,128)(2,1)}, u32[]{:S(2)}, u32[]{:S(2)}) %collective-permute-start.32) | collective-permute-done | bytes 3145760 | tf_op jit(solution)/shard_map/ppermute | solution.py:654
  287.3 16.9 %collective-permute-done.35.refs_2_ = bf16[2,160,1024]{2,1,0:T(8,128)(2,1)S(1)} collective-permute-done((bf16[2,160,1024]{2,1,0:T(8,128)(2,1)S(1)}, bf16[2,160,1024]{2,1,0:T(8,128)(2,1)S(1)}, u32[]{:S(2)}, u32[]{:S(2)}) %collective-permute-start.35) | collective-permute-done | bytes 655392 | tf_op jit(solution)/shard_map/ppermute | solution.py:989
  304.2 26.5 %collective-permute-done.36.refs_4_ = bf16[2,160,1024]{2,1,0:T(8,128)(2,1)S(1)} collective-permute-done((bf16[2,160,1024]{2,1,0:T(8,128)(2,1)S(1)}, bf16[2,160,1024]{2,1,0:T(8,128)(2,1)S(1)}, u32[]{:S(2)}, u32[]{:S(2)}) %collective-permute-start.36) | collective-permute-done | bytes 655392 | tf_op jit(solution)/shard_map/ppermute | solution.py:989
  330.9 5.9 %combine.1 = (bf16[2,2,768,256]{3,2,1,0:T(8,128)(2,1)}, bf16[3,2,192,256]{3,2,1,0:T(8,128)(2,1)}, bf16[3,2,192,256]{3,2,1,0:T(8,128)(2,1)}, bf16[3,2,192,256]{3,2,1,0:T(8,128)(2,1)}, bf16[3,2,192,256]{3,2,1,0:T(8,128)(2,1)}) custom-call(s32[3]{0:T(128)S(1)} %pad_add_fusion.pos.pos_ref, bf16[2,2,2,768,256]{4,3,2,1,0:T(8,128)(2,1)} %get-tuple-element.185.own, ...), custom_call_target="tpu_custom_call" | custom-call | flops 4000000000 | bytes 12000000 | tf_op jit(solution)/shard_map/combine/pallas_call | solution.py:246
  342.0 7.4 %qkv_grads.1 = (bf16[2,2,128,768]{3,2,1,0:T(8,128)(2,1)}, f32[2,128,768]{2,1,0:T(8,128)}, f32[2,128,768]{2,1,0:T(8,128)}) custom-call(s32[3]{0:T(128)S(1)} %pad_add_fusion.pos.pos_ref, bf16[2,768,1024]{2,1,0:T(8,128)(2,1)} %copy-done.18, bf16[2,640,256]{2,1,0:T(8,128)(2,1)} %get-tuple-element.180.gq, bf16[2,2,768,256]{3,2,1,0:T(8,128)(2,1)} %get-tuple-element.199.gkv), custom_call_target="tpu_custom_call" | custom-call | flops 8000000000 | bytes 24000000 | tf_op jit(solution)/shard_map/qkv_grads/pallas_call | solution.py:246
  349.4 21.7 %collective-permute-done.37.refs_1_ = bf16[3,2,192,256]{3,2,1,0:T(8,128)(2,1)S(1)} collective-permute-done((bf16[3,2,192,256]{3,2,1,0:T(8,128)(2,1)}, bf16[3,2,192,256]{3,2,1,0:T(8,128)(2,1)S(1)}, u32[]{:S(2)}, u32[]{:S(2)}) %collective-permute-start.37) | collective-permute-done | bytes 589856 | tf_op jit(solution)/shard_map/ppermute | solution.py:657
  371.1 55.7 %collective-permute-done.38.refs_2_ = bf16[3,2,192,256]{3,2,1,0:T(8,128)(2,1)S(1)} collective-permute-done((bf16[3,2,192,256]{3,2,1,0:T(8,128)(2,1)}, bf16[3,2,192,256]{3,2,1,0:T(8,128)(2,1)S(1)}, u32[]{:S(2)}, u32[]{:S(2)}) %collective-permute-start.38) | collective-permute-done | bytes 589856 | tf_op jit(solution)/shard_map/ppermute | solution.py:657
  432.4 10.5 %input_back.1 = (bf16[2,192,1024]{2,1,0:T(8,128)(2,1)}, f32[8,1024]{1,0:T(8,128)}) custom-call(s32[3]{0:T(128)S(1)} %pad_add_fusion.pos.pos_ref, bf16[3,2,192,256]{3,2,1,0:T(8,128)(2,1)} %get-tuple-element.216.refs_0_, bf16[3,2,192,256]{3,2,1,0:T(8,128)(2,1)} %copy-done.44, bf16[3,2,192,256]{3,2,1,0:T(8,128)(2,1)} %copy-done.45, ...), custom_call_target="tpu_custom_call" | custom-call | flops 4000000000 | bytes 12000000 | tf_op jit(solution)/shard_map/input_back/pallas_call | solution.py:246
  456.4 14.0 %collective-permute-done.47 = f32[6,1024]{1,0:T(8,128)S(1)} collective-permute-done((f32[6,1024]{1,0:T(8,128)S(1)}, f32[6,1024]{1,0:T(8,128)S(1)}, u32[]{:S(2)}, u32[]{:S(2)}) %collective-permute-start.47) | collective-permute-done | bytes 24608 | tf_op jit(solution)/shard_map/ppermute | solution.py:654
  470.5 9.8 %collective-permute-done.43.refs_3_ = bf16[2,192,1024]{2,1,0:T(8,128)(2,1)S(1)} collective-permute-done((bf16[2,192,1024]{2,1,0:T(8,128)(2,1)S(1)}, bf16[2,192,1024]{2,1,0:T(8,128)(2,1)S(1)}, u32[]{:S(2)}, u32[]{:S(2)}) %collective-permute-start.43) | collective-permute-done | bytes 786464 | tf_op jit(solution)/shard_map/ppermute | solution.py:989
  523.1 13.2 %collective-permute-done.49.refs_4_ = bf16[2,192,1024]{2,1,0:T(8,128)(2,1)} collective-permute-done((bf16[2,192,1024]{2,1,0:T(8,128)(2,1)S(1)}, bf16[2,192,1024]{2,1,0:T(8,128)(2,1)}, u32[]{:S(2)}, u32[]{:S(2)}) %collective-permute-start.49) | collective-permute-done | bytes 786464 | tf_op jit(solution)/shard_map/ppermute | solution.py:1117
  (292 shorter events, 182.6 us)
Async XLA Ops:
  8.0 134.6 %all-gather.5.cloned.1.call-start = ((), (), s32[]{:S(2)}) async-start(), calls=%async_computation.4 | async-start | bytes 4718592 | tf_op jit(solution)/shard_map/all_gather | solution.py:796
  17.1 252.8 %reduce-scatter.3.cloned.1.call-start = ((), (), s32[]{:S(2)}) async-start(), calls=%async_computation.2 | async-start | bytes 6291456 | tf_op jit(solution)/shard_map/reduce_scatter | solution.py:1000
  32.5 37.0 %collective-permute-start.3 = (bf16[2,768,512]{2,1,0:T(8,128)(2,1)S(1)}, bf16[2,768,512]{2,1,0:T(8,128)(2,1)}, u32[]{:S(2)}, u32[]{:S(2)}) collective-permute-start(bf16[2,768,512]{2,1,0:T(8,128)(2,1)S(1)} %get-tuple-element.132.refs_0_.refs_4_), channel_id=1, source_target_pairs={{0,8},{4,12},{8,0},{12,4},{1,9},{5,13},{9,1},{13,5},{2,10},{6,14},... | collective-permute-start | bytes 4718600 | tf_op jit(solution)/shard_map/ppermute | solution.py:654
  38.0 31.3 %collective-permute-start.5 = (bf16[256,512]{1,0:T(8,128)(2,1)S(1)}, bf16[256,512]{1,0:T(8,128)(2,1)}, u32[]{:S(2)}, u32[]{:S(2)}) collective-permute-start(bf16[256,512]{1,0:T(8,128)(2,1)S(1)} %copy-done.47), channel_id=1, source_target_pairs={{0,2},{1,3},{2,0},{3,1},{4,6},{5,7},{6,4},{7,5},{8,10},{9,11},{10,... | collective-permute-start | bytes 786440 | tf_op jit(solution)/shard_map/ppermute | solution.py:657
  38.0 31.3 %collective-permute-start.6 = (bf16[256,512]{1,0:T(8,128)(2,1)S(1)}, bf16[256,512]{1,0:T(8,128)(2,1)}, u32[]{:S(2)}, u32[]{:S(2)}) collective-permute-start(bf16[256,512]{1,0:T(8,128)(2,1)S(1)} %copy-done.47), channel_id=1, source_target_pairs={{0,1},{1,2},{2,3},{3,0},{4,5},{5,6},{6,7},{7,4},{8,9},{9,10},{10,1... | collective-permute-start | bytes 786440 | tf_op jit(solution)/shard_map/ppermute | solution.py:657
  40.2 33.3 %collective-permute-start.2 = (bf16[2,768,512]{2,1,0:T(8,128)(2,1)S(1)}, bf16[2,768,512]{2,1,0:T(8,128)(2,1)}, u32[]{:S(2)}, u32[]{:S(2)}) collective-permute-start(bf16[2,768,512]{2,1,0:T(8,128)(2,1)S(1)} %get-tuple-element.132.refs_0_.refs_4_), channel_id=1, source_target_pairs={{0,4},{4,0},{8,12},{12,8},{1,5},{5,1},{9,13},{13,9},{2,6},{6,2},{1... | collective-permute-start | bytes 4718600 | tf_op jit(solution)/shard_map/ppermute | solution.py:654
  71.4 41.7 %collective-permute-start.8 = (bf16[320,1024]{1,0:T(8,128)(2,1)S(1)}, bf16[320,1024]{1,0:T(8,128)(2,1)}, u32[]{:S(2)}, u32[]{:S(2)}) collective-permute-start(bf16[320,1024]{1,0:T(8,128)(2,1)S(1)} %bitcast.107), channel_id=1, source_target_pairs={{0,8},{4,12},{8,0},{12,4},{1,9},{5,13},{9,1},{13,5},{2,10},{6,14},... | collective-permute-start | bytes 1966088 | tf_op jit(solution)/shard_map/ppermute | solution.py:654
  72.9 23.2 %collective-permute-start.10 = (bf16[256,512]{1,0:T(8,128)(2,1)}, bf16[256,512]{1,0:T(8,128)(2,1)S(1)}, u32[]{:S(2)}, u32[]{:S(2)}) collective-permute-start(bf16[256,512]{1,0:T(8,128)(2,1)} %collective-permute-done.4.refs_5_.refs_1_), channel_id=1, source_target_pairs={{0,16},{16,0},{1,17},{17,1},{2,18},{18,2},{3,19},{19,3},{4,20},{20... | collective-permute-start | bytes 786440 | tf_op jit(solution)/shard_map/ppermute | solution.py:651
  73.4 33.7 %collective-permute-start.11 = (bf16[256,512]{1,0:T(8,128)(2,1)}, bf16[256,512]{1,0:T(8,128)(2,1)S(1)}, u32[]{:S(2)}, u32[]{:S(2)}) collective-permute-start(bf16[256,512]{1,0:T(8,128)(2,1)} %collective-permute-done.5.refs_6_.refs_2_), channel_id=1, source_target_pairs={{0,16},{16,0},{1,17},{17,1},{2,18},{18,2},{3,19},{19,3},{4,20},{20... | collective-permute-start | bytes 786440 | tf_op jit(solution)/shard_map/ppermute | solution.py:651
  74.9 38.1 %collective-permute-start.12 = (bf16[256,512]{1,0:T(8,128)(2,1)}, bf16[256,512]{1,0:T(8,128)(2,1)}, u32[]{:S(2)}, u32[]{:S(2)}) collective-permute-start(bf16[256,512]{1,0:T(8,128)(2,1)} %collective-permute-done.6.refs_7_.refs_3_), channel_id=1, source_target_pairs={{0,16},{16,0},{1,17},{17,1},{2,18},{18,2},{3,19},{19,3},{4,20},{20... | collective-permute-start | bytes 786440 | tf_op jit(solution)/shard_map/ppermute | solution.py:651
  187.6 244.7 %all-gather.7.cloned.1.call-start = ((), (), s32[]{:S(2)}) async-start(), calls=%async_computation.5 | async-start | bytes 6488064 | tf_op jit(solution)/shard_map/all_gather | solution.py:853
  188.2 257.5 %reduce-scatter.5.cloned.1.call-start = ((), (), s32[]{:S(2)}) async-start(), calls=%async_computation.3 | async-start | bytes 2949120 | tf_op jit(solution)/shard_map/reduce_scatter | solution.py:1021
  226.1 32.9 %collective-permute-start.30 = (bf16[2,160,1024]{2,1,0:T(8,128)(2,1)S(1)}, bf16[2,160,1024]{2,1,0:T(8,128)(2,1)S(1)}, u32[]{:S(2)}, u32[]{:S(2)}) collective-permute-start(bf16[2,160,1024]{2,1,0:T(8,128)(2,1)S(1)} %bitcast.94), channel_id=1, source_target_pairs={{0,1},{1,2},{2,3},{4,5},{5,6},{6,7},{8,9},{9,10},{10,11},{12,13},{... | collective-permute-start | bytes 1966088 | tf_op jit(solution)/shard_map/ppermute | solution.py:969
  233.0 27.6 %collective-permute-start.31 = (bf16[2,160,1024]{2,1,0:T(8,128)(2,1)S(1)}, bf16[2,160,1024]{2,1,0:T(8,128)(2,1)S(1)}, u32[]{:S(2)}, u32[]{:S(2)}) collective-permute-start(bf16[2,160,1024]{2,1,0:T(8,128)(2,1)S(1)} %bitcast.95), channel_id=1, source_target_pairs={{1,0},{2,1},{3,2},{5,4},{6,5},{7,6},{9,8},{10,9},{11,10},{13,12},{... | collective-permute-start | bytes 1966088 | tf_op jit(solution)/shard_map/ppermute | solution.py:970
  234.3 24.7 %collective-permute-start.29 = (bf16[4,64,1024]{2,1,0:T(8,128)(2,1)S(1)}, bf16[4,64,1024]{2,1,0:T(8,128)(2,1)S(1)}, u32[]{:S(2)}, u32[]{:S(2)}) collective-permute-start(bf16[4,64,1024]{2,1,0:T(8,128)(2,1)S(1)} %get-tuple-element.183), channel_id=1, source_target_pairs={{0,8},{4,12},{8,0},{12,4},{1,9},{5,13},{9,1},{13,5},{2,10},{6,14},... | collective-permute-start | bytes 1572872 | tf_op jit(solution)/shard_map/ppermute | solution.py:654
  269.9 60.8 %collective-permute-start.33 = (bf16[2,2,768,256]{3,2,1,0:T(8,128)(2,1)}, bf16[2,2,768,256]{3,2,1,0:T(8,128)(2,1)}, u32[]{:S(2)}, u32[]{:S(2)}) collective-permute-start(bf16[2,2,768,256]{3,2,1,0:T(8,128)(2,1)} %fusion), channel_id=1, source_target_pairs={{0,8},{4,12},{8,0},{12,4},{1,9},{5,13},{9,1},{13,5},{2,10},{6,14},... | collective-permute-start | bytes 4718600 | tf_op jit(solution)/shard_map/ppermute | solution.py:654
  275.8 28.5 %collective-permute-start.35 = (bf16[2,160,1024]{2,1,0:T(8,128)(2,1)S(1)}, bf16[2,160,1024]{2,1,0:T(8,128)(2,1)S(1)}, u32[]{:S(2)}, u32[]{:S(2)}) collective-permute-start(bf16[2,160,1024]{2,1,0:T(8,128)(2,1)S(1)} %bitcast.96), channel_id=1, source_target_pairs={{0,3},{3,0},{4,7},{7,4},{8,11},{11,8},{12,15},{15,12},{16,19},{19,... | collective-permute-start | bytes 1966088 | tf_op jit(solution)/shard_map/ppermute | solution.py:989
  281.5 49.2 %collective-permute-start.36 = (bf16[2,160,1024]{2,1,0:T(8,128)(2,1)S(1)}, bf16[2,160,1024]{2,1,0:T(8,128)(2,1)S(1)}, u32[]{:S(2)}, u32[]{:S(2)}) collective-permute-start(bf16[2,160,1024]{2,1,0:T(8,128)(2,1)S(1)} %bitcast.97), channel_id=1, source_target_pairs={{0,2},{1,3},{2,0},{3,1},{4,6},{5,7},{6,4},{7,5},{8,10},{9,11},{10,... | collective-permute-start | bytes 1966088 | tf_op jit(solution)/shard_map/ppermute | solution.py:989
  336.8 34.3 %collective-permute-start.37 = (bf16[3,2,192,256]{3,2,1,0:T(8,128)(2,1)}, bf16[3,2,192,256]{3,2,1,0:T(8,128)(2,1)S(1)}, u32[]{:S(2)}, u32[]{:S(2)}) collective-permute-start(bf16[3,2,192,256]{3,2,1,0:T(8,128)(2,1)} %get-tuple-element.208), channel_id=1, source_target_pairs={{0,3},{1,0},{2,1},{3,2},{4,7},{5,4},{6,5},{7,6},{8,11},{9,8},{10,9... | collective-permute-start | bytes 1769480 | tf_op jit(solution)/shard_map/ppermute | solution.py:657
  339.2 87.6 %collective-permute-start.38 = (bf16[3,2,192,256]{3,2,1,0:T(8,128)(2,1)}, bf16[3,2,192,256]{3,2,1,0:T(8,128)(2,1)S(1)}, u32[]{:S(2)}, u32[]{:S(2)}) collective-permute-start(bf16[3,2,192,256]{3,2,1,0:T(8,128)(2,1)} %get-tuple-element.209), channel_id=1, source_target_pairs={{0,2},{1,3},{2,0},{3,1},{4,6},{5,7},{6,4},{7,5},{8,10},{9,11},{10,... | collective-permute-start | bytes 1769480 | tf_op jit(solution)/shard_map/ppermute | solution.py:657
  339.2 87.6 %collective-permute-start.39 = (bf16[3,2,192,256]{3,2,1,0:T(8,128)(2,1)}, bf16[3,2,192,256]{3,2,1,0:T(8,128)(2,1)S(1)}, u32[]{:S(2)}, u32[]{:S(2)}) collective-permute-start(bf16[3,2,192,256]{3,2,1,0:T(8,128)(2,1)} %get-tuple-element.210), channel_id=1, source_target_pairs={{0,1},{1,2},{2,3},{3,0},{4,5},{5,6},{6,7},{7,4},{8,9},{9,10},{10,1... | collective-permute-start | bytes 1769480 | tf_op jit(solution)/shard_map/ppermute | solution.py:657
  444.1 36.1 %collective-permute-start.43 = (bf16[2,192,1024]{2,1,0:T(8,128)(2,1)S(1)}, bf16[2,192,1024]{2,1,0:T(8,128)(2,1)S(1)}, u32[]{:S(2)}, u32[]{:S(2)}) collective-permute-start(bf16[2,192,1024]{2,1,0:T(8,128)(2,1)S(1)} %copy-done.2), channel_id=1, source_target_pairs={{0,2},{1,3},{2,0},{3,1},{4,6},{5,7},{6,4},{7,5},{8,10},{9,11},{10,... | collective-permute-start | bytes 2359304 | tf_op jit(solution)/shard_map/ppermute | solution.py:989
  445.7 34.6 %collective-permute-start.48 = (bf16[1152,256]{1,0:T(8,128)(2,1)}, bf16[1152,256]{1,0:T(8,128)(2,1)S(1)}, u32[]{:S(2)}, u32[]{:S(2)}) collective-permute-start(bf16[1152,256]{1,0:T(8,128)(2,1)} %bitcast.99), channel_id=1, source_target_pairs={{0,8},{4,12},{8,0},{12,4},{1,9},{5,13},{9,1},{13,5},{2,10},{6,14},... | collective-permute-start | bytes 1769480 | tf_op jit(solution)/shard_map/ppermute | solution.py:654
  501.4 34.9 %collective-permute-start.49 = (bf16[2,192,1024]{2,1,0:T(8,128)(2,1)S(1)}, bf16[2,192,1024]{2,1,0:T(8,128)(2,1)}, u32[]{:S(2)}, u32[]{:S(2)}) collective-permute-start(bf16[2,192,1024]{2,1,0:T(8,128)(2,1)S(1)} %collective-permute-done.43.refs_3_), channel_id=1, source_target_pairs={{2,3},{1,0},{3,2},{0,1},{6,7},{5,4},{7,6},{4,5},{10,11},{9,8},{11,... | collective-permute-start | bytes 2359304 | tf_op jit(solution)/shard_map/ppermute | solution.py:1117
  (95 other events, 1205.0 us)
Sparse Core Ops, SparseCore 0:
  17.3 108.7 all-gather.4
  187.0 61.4 reduce-scatter.2
  330.9 89.7 reduce-scatter.4
Sparse Core Ops, SparseCore 1:
  191.5 130.2 all-gather.6

commit v3 on v2

--- a/solution.py
+++ b/solution.py
@@ -61,10 +61,10 @@
 
 
 def bias_tables(rb_ref, h, levels, seg, bm_ref):
-    row = lax.broadcasted_iota(jnp.int32, (seg, seg), 0)
-    col = lax.broadcasted_iota(jnp.int32, (seg, seg), 1)
+    key = lax.broadcasted_iota(jnp.int32, (seg, seg), 0)
+    query = lax.broadcasted_iota(jnp.int32, (seg, seg), 1)
     for lev in range(levels):
-        dist = lev * seg + row - col
+        dist = lev * seg + query - key
         low, high = lev * seg - (seg - 1), lev * seg + seg - 1
         if low >= EDGES[-1]:
             val = jnp.full((seg, seg), rb_ref[h, BUCKETS - 1], F32)
@@ -77,7 +77,7 @@
             val = jnp.where(dist >= 0, val, MASKED)
         if high >= WINDOW:
             val = jnp.where(dist < WINDOW, val, MASKED)
-        bm_ref[:, lev * seg : (lev + 1) * seg] = val
+        bm_ref[lev * seg : (lev + 1) * seg, :] = val
 
 
 def chain(par_ref, t, first, levels, all_segs, local_segs, ctx):
@@ -93,62 +93,74 @@
     return out
 
 
-def scores_of(q, kw_ref, bm_ref, line, length, levels, seg, factor):
-    win = levels * seg
-    col = lax.broadcasted_iota(jnp.int32, (1, seg), 1)
-    raw = mm_nt(q, kw_ref[...]) * factor
-    parts = []
-    for lev in range(levels):
-        part = raw[:, lev * seg : (lev + 1) * seg] + bm_ref[:, lev * seg : (lev + 1) * seg]
-        if lev == 0:
-            part = part + jnp.where(col < length, 0.0, MASKED)
-        else:
-            part = part + jnp.where(line[lev][0], 0.0, MASKED)
-        parts.append(part)
-    parts.append(raw[:, win:])
-    return jnp.concatenate(parts, axis=1)
-
-
-def fill_sources(parts_k, parts_v, kall, vall, kw, vw, rows, win):
-    for b in range(len(parts_k)):
-        for src, dst, wide in ((parts_k[b], kall, kw), (parts_v[b], vall, vw)):
-            dst[b] = src[0, :rows, :]
-            n = src.shape[1] - rows
-            wide[win + b * n : win + (b + 1) * n, :] = src[0, rows:, :]
-
-
-def fetch_window(line, kall, vall, kw, vw, seg):
-    for lev, (_, part, block) in enumerate(line):
-        start = pl.multiple_of(block * seg, seg)
-        kw[lev * seg : (lev + 1) * seg, :] = kall[part, pl.ds(start, seg), :]
-        vw[lev * seg : (lev + 1) * seg, :] = vall[part, pl.ds(start, seg), :]
+def window_score(raw, lev, bm_ref, line, length, seg):
+    part = raw + bm_ref[lev * seg : (lev + 1) * seg, :]
+    if lev == 0:
+        key = lax.broadcasted_iota(jnp.int32, (seg, 1), 0)
+        return part + jnp.where(key < length, 0.0, MASKED)
+    return part + jnp.where(line[lev][0], 0.0, MASKED)
+
+
+def fold(value, op):
+    out = value[0:8]
+    for i in range(8, value.shape[0], 8):
+        out = op(out, value[i : i + 8])
+    return out
 
 
 def attend_kernel(dims, par_ref, len_ref, pos_ref, rb_ref, q_ref, *refs):
     levels, seg, local_segs, all_segs, factor, nt = dims
     parts_k, parts_v = refs[0:4], refs[4:8]
     att_refs, lse_ref = refs[8 : 8 + nt], refs[8 + nt]
-    kall, vall, kw, vw, bm, whole = refs[9 + nt :]
+    kall, vall_t, kws, vw_ts, bm, whole, q_t, raws_a, probs_a = refs[9 + nt :]
     t, h = pl.program_id(0), pl.program_id(1)
     ctx, zi = pos_ref[0], pos_ref[1]
     rows, win = local_segs * seg, levels * seg
+    each = (kws.shape[1] - win) // 4
+    blocks = kws.shape[1] // seg
     bias_tables(rb_ref, h, levels, seg, bm)
-    fill_sources(parts_k, parts_v, kall, vall, kw, vw, rows, win)
+    for b in range(4):
+        at = slice(win + b * each, win + (b + 1) * each)
+        kall[b] = parts_k[b][0, :rows, :]
+        turned = parts_v[b][0].T
+        vall_t[b] = turned[:, :rows]
+        for i in range(2):
+            kws[i, at, :] = parts_k[b][0, rows:, :]
+            vw_ts[i, :, at] = turned[:, rows:]
+    q_t[...] = q_ref[0, :rows, :].T
 
     def one(s, carry):
+        kw, vw_t, raws, probs = (r.at[s % 2] for r in (kws, vw_ts, raws_a, probs_a))
         line = chain(par_ref, t, ctx * local_segs + s, levels, all_segs, local_segs, ctx)
-        fetch_window(line, kall, vall, kw, vw, seg)
-        at = pl.ds(pl.multiple_of(s * seg, seg), seg)
-        score = scores_of(q_ref[0, at, :], kw, bm, line, len_ref[t, s], levels, seg, factor)
-        top = jnp.max(score, axis=1, keepdims=True)
-        prob = jnp.exp(score - top)
-        total = jnp.sum(prob, axis=1, keepdims=True)
-        lse_ref[0, 0, at, :] = jnp.broadcast_to(top + jnp.log(total), (seg, 128))
-        att = mm(prob.astype(BF), vw[...]) / total
-        whole[at, :] = att.astype(BF)
+        for lev, (_, part, block) in enumerate(line):
+            start = pl.ds(pl.multiple_of(block * seg, seg), seg)
+            kw[lev * seg : (lev + 1) * seg, :] = kall[part, start, :]
+            vw_t[:, lev * seg : (lev + 1) * seg] = vall_t[part, :, start]
+        at = slice(s * seg, (s + 1) * seg)
+        turned = q_t[:, at]
+        top = None
+        for c in range(blocks):
+            raw = mm(kw[c * seg : (c + 1) * seg, :], turned) * factor
+            if c < levels:
+                raw = window_score(raw, c, bm, line, len_ref[t, s], seg)
+            raws[c * seg : (c + 1) * seg, :] = raw
+            high = fold(raw, jnp.maximum)
+            top = high if top is None else jnp.maximum(top, high)
+        top = jnp.max(top, axis=0, keepdims=True)
+        total = None
+        for c in range(blocks):
+            prob = jnp.exp(raws[c * seg : (c + 1) * seg, :] - top)
+            probs[c * seg : (c + 1) * seg, :] = prob.astype(BF)
+            part = fold(prob, jnp.add)
+            total = part if total is None else total + part
+        total = jnp.sum(total, axis=0, keepdims=True)
+        lse_ref[0, 0, 0:1, at] = top + jnp.log(total)
+        att = mm(vw_t[...], probs[...]) / total
+        whole[at, :] = att.T.astype(BF)
         return carry
 
-    lax.fori_loop(0, local_segs, one, 0)
+    for s in range(local_segs):
+        one(s, 0)
     n = rows // nt
     for j in range(nt):
         k = lax.rem(zi - j + nt, nt)
@@ -161,20 +173,33 @@
     do_refs, lse_ref = refs[8 : 8 + nt], refs[8 + nt]
     dq_refs = refs[9 + nt : 9 + 2 * nt]
     dq_ref, near_ref, far_ref, db_ref = refs[9 + 2 * nt : 13 + 2 * nt]
-    kall, vall, kw, vw, bm, dk, dv, near, far, dos = refs[13 + 2 * nt :]
+    kall, vall, kall_t, kws, vws, kw_ts, bm, dk, dv, near, far, dos, do_t, q_t, raws_a, dps_a, dss_a, pbs_a = refs[
+        13 + 2 * nt :
+    ]
     h, t = pl.program_id(0), pl.program_id(1)
     ctx, zi = pos_ref[0], pos_ref[1]
     rows, win = local_segs * seg, levels * seg
-    states = kw.shape[0] - win
-    each = states // 4
+    each = (kws.shape[1] - win) // 4
+    blocks = kws.shape[1] // seg
     n = rows // nt
     bias_tables(rb_ref, h, levels, seg, bm)
-    fill_sources(parts_k, parts_v, kall, vall, kw, vw, rows, win)
+    for b in range(4):
+        at = slice(win + b * each, win + (b + 1) * each)
+        kall[b] = parts_k[b][0, :rows, :]
+        vall[b] = parts_v[b][0, :rows, :]
+        turned = parts_k[b][0].T
+        kall_t[b] = turned[:, :rows]
+        for i in range(2):
+            kws[i, at, :] = parts_k[b][0, rows:, :]
+            vws[i, at, :] = parts_v[b][0, rows:, :]
+            kw_ts[i, :, at] = turned[:, rows:]
     dk[...] = jnp.zeros(dk.shape, F32)
     dv[...] = jnp.zeros(dv.shape, F32)
     for j in range(nt):
         k = lax.rem(zi - j + nt, nt)
         dos[pl.ds(pl.multiple_of(k * n, n), n), :] = do_refs[j][0]
+    q_t[...] = q_ref[0, :rows, :].T
+    do_t[...] = dos[...].T
 
     @pl.when(t == 0)
     def _():
@@ -182,34 +207,61 @@
         far[...] = jnp.zeros(far.shape, F32)
 
     def one(s, carry):
+        kw, vw, kw_t = (r.at[s % 2] for r in (kws, vws, kw_ts))
+        raws, dps, dss, pbs = (r.at[s % 2] for r in (raws_a, dps_a, dss_a, pbs_a))
         line = chain(par_ref, t, ctx * local_segs + s, levels, all_segs, local_segs, ctx)
-        fetch_window(line, kall, vall, kw, vw, seg)
-        at = pl.ds(pl.multiple_of(s * seg, seg), seg)
-        q = q_ref[0, at, :]
-        do = dos[at, :]
-        score = scores_of(q, kw, bm, line, len_ref[t, s], levels, seg, factor)
-        prob = jnp.exp(score - lse_ref[0, 0, at, :][:, 0:1])
-        dprob = mm_nt(do, vw[...])
-        delta = jnp.sum(prob * dprob, axis=1, keepdims=True)
-        dscore = (prob * (dprob - delta)).astype(BF)
-        dq_ref[0, at, :] = (mm(dscore, kw[...]) * factor).astype(BF)
-        near[...] += dscore[:, : 2 * seg].astype(F32)
-        tail = dscore[:, 2 * seg : 3 * seg].astype(F32)
-        for lev in range(3, levels):
-            tail = tail + dscore[:, lev * seg : (lev + 1) * seg].astype(F32)
-        far[...] += tail
-        gk = mm_tn(dscore, q) * factor
-        gv = mm_tn(prob.astype(BF), do)
         for lev, (_, part, block) in enumerate(line):
             start = pl.ds(pl.multiple_of(block * seg, seg), seg)
-            dk[part, start, :] += gk[lev * seg : (lev + 1) * seg]
-            dv[part, start, :] += gv[lev * seg : (lev + 1) * seg]
-        for b in range(4):
-            dk[b, rows:, :] += gk[win + b * each : win + (b + 1) * each]
-            dv[b, rows:, :] += gv[win + b * each : win + (b + 1) * each]
+            at = slice(lev * seg, (lev + 1) * seg)
+            kw[at, :] = kall[part, start, :]
+            vw[at, :] = vall[part, start, :]
+            kw_t[:, at] = kall_t[part, :, start]
+        at = slice(s * seg, (s + 1) * seg)
+        turned, do_turned = q_t[:, at], do_t[:, at]
+        lse = lse_ref[0, 0, 0:1, at]
+        delta = None
+        for c in range(blocks):
+            cut = slice(c * seg, (c + 1) * seg)
+            raw = mm(kw[cut, :], turned) * factor
+            if c < levels:
+                raw = window_score(raw, c, bm, line, len_ref[t, s], seg)
+            prob = jnp.exp(raw - lse)
+            dprob = mm(vw[cut, :], do_turned)
+            raws[cut, :] = prob
+            dps[cut, :] = dprob
+            pbs[cut, :] = prob.astype(BF)
+            part = fold(prob * dprob, jnp.add)
+            delta = part if delta is None else delta + part
+        delta = jnp.sum(delta, axis=0, keepdims=True)
+        for c in range(blocks):
+            cut = slice(c * seg, (c + 1) * seg)
+            dscore = (raws[cut, :] * (dps[cut, :] - delta)).astype(BF)
+            dss[cut, :] = dscore
+            if c < 2:
+                near[cut, :] += dscore.astype(F32)
+            elif c < levels:
+                far[...] += dscore.astype(F32)
+        dq = mm(kw_t[...], dss[...]) * factor
+        dq_ref[0, at, :] = dq.T.astype(BF)
+        q, do = q_ref[0, at, :], dos[at, :]
+        for c in range(blocks):
+            cut = slice(c * seg, (c + 1) * seg)
+            gk = mm(dss[cut, :], q) * factor
+            gv = mm(pbs[cut, :], do)
+            if c < levels:
+                _, part, block = line[c]
+                to = pl.ds(pl.multiple_of(block * seg, seg), seg)
+                dk[part, to, :] += gk
+                dv[part, to, :] += gv
+            else:
+                for i in range(0, seg, each):
+                    b = ((c - levels) * seg + i) // each
+                    dk[b, rows:, :] += gk[i : i + each]
+                    dv[b, rows:, :] += gv[i : i + each]
         return carry
 
-    lax.fori_loop(0, local_segs, one, 0)
+    for s in range(local_segs):
+        one(s, 0)
     for ref, pair in ((near_ref, (0, 2)), (far_ref, (1, 3))):
         for place, b in enumerate(pair):
             ref[place, 0, 0] = dk[b].astype(BF)
@@ -220,15 +272,15 @@
 
     @pl.when(t == pl.num_programs(1) - 1)
     def _():
-        row = lax.broadcasted_iota(jnp.int32, (seg, seg), 0)
-        col = lax.broadcasted_iota(jnp.int32, (seg, seg), 1)
+        key = lax.broadcasted_iota(jnp.int32, (seg, seg), 0)
+        query = lax.broadcasted_iota(jnp.int32, (seg, seg), 1)
         edges = [-(10**6)] + list(EDGES) + [10**6]
         for b in range(BUCKETS):
             total = far[...] if b == BUCKETS - 1 else jnp.zeros((seg, seg), F32)
             for lev in range(2):
-                dist = lev * seg + row - col
+                dist = lev * seg + query - key
                 inside = (dist >= edges[b]) & (dist < edges[b + 1])
-                total = total + jnp.where(inside, near[:, lev * seg : (lev + 1) * seg], 0.0)
+                total = total + jnp.where(inside, near[lev * seg : (lev + 1) * seg, :], 0.0)
             db_ref[0, b : b + 1, :] = jnp.sum(total, axis=0, keepdims=True)
 
 
@@ -257,13 +309,40 @@
     factor = head_dim ** (-0.5)
     dims = (levels, seg, local_segs, all_segs, factor, nt)
     assert EDGES[-1] <= 2 * seg - (seg - 1)
-    base_scratch = [
-        pltpu.VMEM((4, rows, head_dim), BF),
-        pltpu.VMEM((4, rows, head_dim), BF),
-        pltpu.VMEM((wide, head_dim), BF),
-        pltpu.VMEM((wide, head_dim), BF),
-        pltpu.VMEM((seg, win), F32),
+    assert seg == head_dim == 128 and wide % seg == 0 and seg % each == 0
+    vm = lambda dt, *shape: pltpu.VMEM(shape, dt)
+    forward_scratch = [
+        vm(BF, 4, rows, head_dim),
+        vm(BF, 4, head_dim, rows),
+        vm(BF, 2, wide, head_dim),
+        vm(BF, 2, head_dim, wide),
+        vm(F32, win, seg),
+        vm(BF, rows, head_dim),
+        vm(BF, head_dim, rows),
+        vm(F32, 2, wide, seg),
+        vm(BF, 2, wide, seg),
     ]
+    backward_scratch = [
+        vm(BF, 4, rows, head_dim),
+        vm(BF, 4, rows, head_dim),
+        vm(BF, 4, head_dim, rows),
+        vm(BF, 2, wide, head_dim),
+        vm(BF, 2, wide, head_dim),
+        vm(BF, 2, head_dim, wide),
+        vm(F32, win, seg),
+        vm(F32, 4, tall, head_dim),
+        vm(F32, 4, tall, head_dim),
+        vm(F32, 2 * seg, seg),
+        vm(F32, seg, seg),
+        vm(BF, rows, head_dim),
+        vm(BF, head_dim, rows),
+        vm(BF, head_dim, rows),
+        vm(F32, 2, wide, seg),
+        vm(F32, 2, wide, seg),
+        vm(BF, 2, wide, seg),
+        vm(BF, 2, wide, seg),
+    ]
+    lse_shape = jax.ShapeDtypeStruct((trees, heads, 8, rows), F32)
 
     def specs(order):
         def at(col):
@@ -286,14 +365,14 @@
     forward = hbm_call(
         4,
         functools.partial(attend_kernel, dims),
-        out_shape=(chunk_shape,) * nt + (jax.ShapeDtypeStruct((trees, heads, rows, 128), F32),),
+        out_shape=(chunk_shape,) * nt + (lse_shape,),
         grid_spec=pltpu.PrefetchScalarGridSpec(
             num_scalar_prefetch=4,
             grid=(trees, heads),
             in_specs=specs(th),
             out_specs=(chunk_spec(th),) * nt
-            + (pl.BlockSpec((1, 1, rows, 128), lambda t, h, *_: (t, h, 0, 0)),),
-            scratch_shapes=base_scratch + [pltpu.VMEM((rows, head_dim), BF)],
+            + (pl.BlockSpec((1, 1, 8, rows), lambda t, h, *_: (t, h, 0, 0)),),
+            scratch_shapes=forward_scratch,
         ),
         compiler_params=pltpu.CompilerParams(vmem_limit_bytes=24 << 20),
         cost_estimate=cost(16),
@@ -317,7 +396,7 @@
             grid=(heads, trees),
             in_specs=specs(ht)
             + [chunk_spec(ht)] * nt
-            + [pl.BlockSpec((1, 1, rows, 128), lambda h, t, *_: (t, h, 0, 0))],
+            + [pl.BlockSpec((1, 1, 8, rows), lambda h, t, *_: (t, h, 0, 0))],
             out_specs=(chunk_spec(ht),) * nt
             + (
                 pl.BlockSpec((1, rows, head_dim), lambda h, t, *_: (t, 0, h)),
@@ -325,14 +404,7 @@
                 pair_spec,
                 pl.BlockSpec((1, BUCKETS, 128), lambda h, t, *_: (h, 0, 0)),
             ),
-            scratch_shapes=base_scratch
-            + [
-                pltpu.VMEM((4, tall, head_dim), F32),
-                pltpu.VMEM((4, tall, head_dim), F32),
-                pltpu.VMEM((seg, 2 * seg), F32),
-                pltpu.VMEM((seg, seg), F32),
-                pltpu.VMEM((rows, head_dim), BF),
-            ],
+            scratch_shapes=backward_scratch,
         ),
         compiler_params=pltpu.CompilerParams(vmem_limit_bytes=32 << 20),
         cost_estimate=cost(24),
@@ -400,8 +472,8 @@
 
 
 def load_projection(pos, blocks, w):
-    n = len(blocks) if blocks[0].shape[1] == w.shape[1] else len(blocks) // 2
     rows, depth = blocks[0].shape
+    n = w.shape[0] // rows
     for j in range(n):
         at = slice(j * rows, (j + 1) * rows)
         if n == len(blocks):
@@ -409,77 +481,71 @@
         else:
             fi = pos[2]
             w[at, pl.ds(pl.multiple_of(fi * depth, depth), depth)] = blocks[j][...]
-            w[at, pl.ds(pl.multiple_of((1 - fi) * depth, depth), depth)] = blocks[n + j][...]
+            w[at, pl.ds(pl.multiple_of((1 - fi) * depth, depth), depth)] = blocks[n][j]
 
 
 def mix_kernel(n, pos, *refs):
     att, blocks = refs[:n], refs[n:-8]
     tok, cell, gain, shift, hid_ref, n2_ref, stat_ref, w = refs[-8:]
 
-    @pl.when(pl.program_id(0) == 0)
-    def _():
-        load_projection(pos, blocks, w)
-        stat_ref[...] = jnp.zeros(stat_ref.shape, F32)
-
+    load_projection(pos, blocks, w)
+    stat_ref[...] = jnp.zeros(stat_ref.shape, F32)
     cols = att[0].shape[2]
-    branch = mm(att[0][0], w[:cols, :])
-    for j in range(1, n):
-        branch = branch + mm(att[j][0], w[j * cols : (j + 1) * cols, :])
-    x = tok[0].astype(F32)
+    shape = tok.shape
+    mine = shape[0] * shape[1]
+    branch = None
+    for j in range(n):
+        part = mm(att[j][...].reshape(mine, cols), w[j * cols : (j + 1) * cols, :])
+        branch = part if branch is None else branch + part
+    x = tok[...].astype(F32).reshape(mine, shape[2])
     gated = cell[...] * branch
     hidden = x + gated
-    hid_ref[0] = hidden
+    hid_ref[...] = hidden.reshape(shape)
     xhat, _ = norm_stats(hidden)
-    n2_ref[0] = (xhat * gain[...] + shift[...]).astype(BF)
-    stat_ref[0:1, :] += jnp.sum(x * x, axis=0, keepdims=True)
-    stat_ref[1:2, :] += jnp.sum(gated * gated, axis=0, keepdims=True)
+    n2_ref[...] = (xhat * gain[...] + shift[...]).astype(BF).reshape(shape)
+    stat_ref[0:1, :] = jnp.sum(x * x, axis=0, keepdims=True)
+    stat_ref[1:2, :] = jnp.sum(gated * gated, axis=0, keepdims=True)
 
 
 def ff_kernel(*refs):
-    xs, gs = refs[0:4], refs[4:8]
-    pack, near_ref, far_ref, act_ref, gup_ref, xall, gall, win, wout = refs[8:]
-    nt, nf, _, depth, fc = pack.shape
-    width = nf * depth
-    for z in range(nt):
+    xs, gs = refs[0:2], refs[2:4]
+    pack, first_ref, second_ref, act_ref, gup_ref, acc = refs[4:]
+    nf, depth = pack.shape[1], pack.shape[3]
+    z = pl.program_id(0)
+    mine = xs[0].shape[0]
+    cut = [slice(f * depth, (f + 1) * depth) for f in range(nf)]
+    for p in range(2):
+        up = mm(xs[p][:, cut[0]], pack[0, 0, 0])
+        back = mm(gs[p][:, cut[0]], pack[0, 0, 1])
+        for f in range(1, nf):
+            up = up + mm(xs[p][:, cut[f]], pack[0, f, 0])
+            back = back + mm(gs[p][:, cut[f]], pack[0, f, 1])
+        value, slope = gelu_parts(up)
+        act_ref[p] = value.astype(BF)
+        gup = (back * slope).astype(BF)
+        gup_ref[p] = gup
+        at = slice(p * mine, (p + 1) * mine)
         for f in range(nf):
-            win[z, f * depth : (f + 1) * depth, :] = pack[z, f, 0]
-            wout[z, f * depth : (f + 1) * depth, :] = pack[z, f, 1]
-    for p in range(4):
-        xall[p] = xs[p][...]
-        gall[p] = gs[p][...]
-    step = 256
-
-    def one(i, carry):
-        p = lax.rem(i + 2, 4)
-        x, g = xall[p], gall[p]
-        for z in range(nt):
-            value, slope = gelu_parts(mm(x, win[z]))
-            act_ref[p, :, z * fc : (z + 1) * fc] = value.astype(BF)
-            gup_ref[p, :, z * fc : (z + 1) * fc] = (mm(g, wout[z]) * slope).astype(BF)
-        for n in range(0, width, step):
-            part = mm_nt(gup_ref[p, :, :fc], win[0, n : n + step, :])
-            for z in range(1, nt):
-                part = part + mm_nt(
-                    gup_ref[p, :, z * fc : (z + 1) * fc], win[z, n : n + step, :]
-                )
-            part = part.astype(BF)
-
-            @pl.when(p < 2)
+            part = mm_nt(gup, pack[0, f, 0])
+
+            @pl.when(z == 0)
             def _():
-                near_ref[p, :, n : n + step] = part
-
-            @pl.when(p >= 2)
+                acc[at, cut[f]] = part
+
+            @pl.when(z > 0)
             def _():
-                far_ref[p - 2, :, n : n + step] = part
-
-        return carry
-
-    lax.fori_loop(0, 4, one, 0)
+                acc[at, cut[f]] += part
+
+    @pl.when(z == pl.num_programs(0) - 1)
+    def _():
+        first_ref[...] = acc[:mine, :].astype(BF)
+        second_ref[...] = acc[mine:, :].astype(BF)
 
 
 def ff_grad_kernel(*refs):
     xs, gs = refs[0:4], refs[4:8]
-    act, gup, pack, sent_ref, near_ref, far_ref, xall, gall, acc, wout = refs[8:]
+    act_a, gup_a, act_b, gup_b, pack = refs[8:13]
+    sent_ref, near_ref, far_ref, xall, gall, acc, wout, act, gup = refs[13:]
     _, nf, _, depth, fc = pack.shape
     mine = xs[0].shape[0]
 
@@ -492,16 +558,22 @@
 
     for f in range(nf):
         wout[f * depth : (f + 1) * depth, :] = pack[0, f, 1]
-    a = act[...].reshape(4 * mine, fc)
-    acc[...] += mm_nt(a, wout[...])
-    for i, part in ((0, mm_tn(xall[...], gup[...].reshape(4 * mine, fc))), (1, mm_tn(gall[...], a))):
+    for half, (a_ref, u_ref) in enumerate(((act_a, gup_a), (act_b, gup_b))):
+        for p in range(2):
+            at = slice((2 * half + p) * mine, (2 * half + p + 1) * mine)
+            act[at, :] = a_ref[p]
+            gup[at, :] = u_ref[p]
+    acc[...] += mm_nt(act[...], wout[...])
+    for i, part in ((0, mm_tn(xall[...], gup[...])), (1, mm_tn(gall[...], act[...]))):
         for f in range(nf):
             sent_ref[f, 0, i] = part[f * depth : (f + 1) * depth].astype(BF)
 
     @pl.when(pl.program_id(0) == pl.num_programs(0) - 1)
     def _():
-        near_ref[...] = acc[: 2 * mine, :].reshape(near_ref.shape).astype(BF)
-        far_ref[...] = acc[2 * mine :, :].reshape(far_ref.shape).astype(BF)
+        for i, ref in enumerate((near_ref, far_ref)):
+            for p in range(2):
+                lo = (2 * p + i) * mine
+                ref[p] = acc[lo : lo + mine, :].astype(BF)
 
 
 def branch_back_kernel(nt, pos, *refs):
@@ -509,23 +581,22 @@
     gh_ref, gb_ref = refs[-(nt + 4) : -(nt + 2)]
     ga_refs, stat_ref, w = refs[-(nt + 2) : -2], refs[-2], refs[-1]
 
-    @pl.when(pl.program_id(0) == 0)
-    def _():
-        load_projection(pos, blocks, w)
-        stat_ref[...] = jnp.zeros(stat_ref.shape, F32)
-
-    grad = own[0, 0].astype(F32) + got[0, 0].astype(F32) + far[0].astype(F32)
-    xhat, scale = norm_stats(hid[0])
-    gh = cot[0].astype(F32) + norm_back(grad, xhat, scale, gain[...])
-    gh_ref[0] = gh
+    load_projection(pos, blocks, w)
+    stat_ref[...] = jnp.zeros(stat_ref.shape, F32)
+    shape = cot.shape
+    mine = shape[0] * shape[1]
+    flat = lambda v: v.astype(F32).reshape(mine, shape[2])
+    grad = flat(own[...]) + flat(got[...]) + flat(far[...])
+    xhat, scale = norm_stats(flat(hid[...]))
+    gh = flat(cot[...]) + norm_back(grad, xhat, scale, gain[...])
+    gh_ref[...] = gh.reshape(shape)
     gb = (cell[...] * gh).astype(BF)
-    gb_ref[0] = gb
+    gb_ref[...] = gb.reshape(shape)
     cols = ga_refs[0].shape[2]
     for j, ref in enumerate(ga_refs):
-        ref[0] = mm_nt(gb, w[j * cols : (j + 1) * cols, :]).astype(BF)
-
-    stat_ref[0:1, :] += jnp.sum(grad * xhat, axis=0, keepdims=True)
-    stat_ref[1:2, :] += jnp.sum(grad, axis=0, keepdims=True)
+        ref[...] = mm_nt(gb, w[j * cols : (j + 1) * cols, :]).astype(BF).reshape(ref.shape)
+    stat_ref[0:1, :] = jnp.sum(grad * xhat, axis=0, keepdims=True)
+    stat_ref[1:2, :] = jnp.sum(grad, axis=0, keepdims=True)
 
 
 def combine_kernel(rows, pos, own, got, far, *refs):
@@ -552,31 +623,53 @@
 
 def input_back_kernel(nt, pos, *refs):
     blocks = refs[:nt]
-    w, tok, st, gh, gain, out_ref, stat_ref = refs[nt:]
+    parts, (tok, st, gh, gain, out_ref, stat_ref, w, every) = refs[nt : nt + 4], refs[nt + 4 :]
+    m = parts[0].shape[1]
+    nf = parts[0].shape[0] // nt
+    for flip, part in zip((0, 2, 1, 3), parts):
+        for z in range(nt):
+            for f in range(nf):
+                at = (f * 4 + jnp.bitwise_xor(pos[0], flip)) * m
+                w[z, pl.ds(pl.multiple_of(at, m), m), :] = part[z * nf + f]
     cols = blocks[0].shape[3]
-    n = tok.shape[1]
-    every = None
+    trees, n = tok.shape[0], tok.shape[1]
+    tall = blocks[0].shape[2]
+    total = None
     for j in range(nt):
         k = lax.rem(pos[1] + j, nt)
         for i in range(3):
-            part = mm_nt(blocks[j][i, 0], w[k, :, i * cols : (i + 1) * cols])
-            every = part if every is None else every + part
-
-    @pl.when(pl.program_id(0) == 0)
-    def _():
-        stat_ref[...] = jnp.zeros(stat_ref.shape, F32)
-
-    for x_ref, grad, lo, hi, extra in (
-        (tok, every[:n], 0, n, gh),
-        (st, every[n:], n, every.shape[0], None),
-    ):
-        xhat, scale = norm_stats(x_ref[0].astype(F32))
-        back = norm_back(grad, xhat, scale, gain[...])
-        if extra is not None:
-            back = back + extra[0]
-        out_ref[0, lo:hi, :] = back.astype(BF)
-        stat_ref[0:1, :] += jnp.sum(grad * xhat, axis=0, keepdims=True)
-        stat_ref[1:2, :] += jnp.sum(grad, axis=0, keepdims=True)
+            left = blocks[j][i].reshape(trees * tall, cols)
+            part = mm_nt(left, w[k, :, i * cols : (i + 1) * cols])
+            total = part if total is None else total + part
+    every[...] = total
+    stat_ref[...] = jnp.zeros(stat_ref.shape, F32)
+    for t in range(trees):
+        for x_ref, lo, hi, extra in ((tok, 0, n, gh), (st, n, tall, None)):
+            grad = every[t * tall + lo : t * tall + hi, :]
+            xhat, scale = norm_stats(x_ref[t].astype(F32))
+            back = norm_back(grad, xhat, scale, gain[...])
+            if extra is not None:
+                back = back + extra[t]
+            out_ref[t, lo:hi, :] = back.astype(BF)
+            stat_ref[0:1, :] += jnp.sum(grad * xhat, axis=0, keepdims=True)
+            stat_ref[1:2, :] += jnp.sum(grad, axis=0, keepdims=True)
+
+
+def attn_grad_kernel(nt, pos, *refs):
+    blocks, grad = refs[:nt], refs[nt]
+    far_ref, mid_ref, own_ref, acc = refs[nt + 1 :]
+    n = own_ref.shape[1]
+    rows = grad.shape[0] * grad.shape[1]
+    right = grad[...].reshape(rows, grad.shape[2])
+    for j in range(nt):
+        acc[...] = mm_tn(blocks[j][...].reshape(rows, acc.shape[0]), right)
+        for flip, ref in ((0, own_ref), (2, mid_ref), (1, far_ref), (3, far_ref)):
+            k = jnp.bitwise_xor(pos[0], flip)
+            piece = acc[pl.ds(pl.multiple_of(k * n, n), n), :]
+            if flip & 1:
+                ref[flip // 2, j] = piece.astype(BF)
+            else:
+                ref[j] = piece
 
 
 def qkv_grad_kernel(nf, pos, x, gq, gkv, far_ref, mid_ref, own_ref, acc, right):
@@ -620,27 +713,32 @@
             lo = lo + n
 
 
-def finish_ff_kernel(rows, pos, *refs):
-    gin, gout, gatt = refs[4:]
+def finish_ff_kernel(pos, *refs):
+    gin, gout = refs[4:]
     depth, fc = gin.shape[0], refs[0].shape[1]
     for flip, b in zip((0, 2, 1, 3), refs[:4]):
         k = jnp.bitwise_xor(pos[0], flip)
         at = pl.ds(pl.multiple_of(k * fc, fc), fc)
         gin[:, at] = b[:depth, :].astype(F32)
-        gout[at, :] = b[depth : 2 * depth, :].astype(F32).T
-        att = pl.ds(pl.multiple_of(k * rows, rows), rows)
-        for i in range(depth // fc):
-            lo = 2 * depth + i * rows
-            gatt[att, i * fc : (i + 1) * fc] = b[lo : lo + rows, :].astype(F32)
+        gout[at, :] = b[depth:, :].astype(F32).T
 
 
 def finish_qkv_kernel(pos, *refs):
     for flip, b in zip((0, 2, 1, 3), refs[:4]):
         n = b.shape[0]
-        at = pl.ds(pl.multiple_of(jnp.bitwise_xor(pos[0], flip) * n, n), n)
-        for i, out in enumerate(refs[4:]):
-            cols = out.shape[1]
+        k = jnp.bitwise_xor(pos[0], flip)
+        at = pl.ds(pl.multiple_of(k * n, n), n)
+        cols = refs[4].shape[1]
+        for i, out in enumerate(refs[4:7]):
             out[at, :] = b[:, i * cols : (i + 1) * cols].astype(F32)
+        for out in refs[7:]:
+            m = n * (b.shape[1] - 3 * cols) // out.shape[1]
+            wide = b.shape[1] - 3 * cols
+            at = pl.ds(pl.multiple_of(k * m, m), m)
+            for i in range(n // m):
+                out[at, i * wide : (i + 1) * wide] = b[
+                    i * m : (i + 1) * m, 3 * cols :
+                ].astype(F32)
 
 
 def build(mesh):
@@ -797,7 +895,7 @@
         packs = packs.reshape(nt, nf, 2, depth, fc)
 
         o_blocks = [w_attn_out] + [pz(w_attn_out, j) for j in range(1, nt)]
-        o_over = [px(w_attn_out)] if nf == 2 else []
+        o_over = []
 
         normed = call(
             norm_kernel,
@@ -833,7 +931,7 @@
         kv_y, grad_low, *o_blocks = gate(kv_y, grad_low, *o_blocks)
         kv_cy = pc(kv_y, 1)
         if nf == 2:
-            o_over += [px(b) for b in o_blocks[1:]]
+            o_over = [px(jnp.stack(o_blocks))]
         else:
             full = lax.all_gather(jnp.stack(o_blocks), "fsdp", axis=2, tiled=True)
             o_blocks = [full[j] for j in range(nt)]
@@ -849,21 +947,21 @@
         quarter = jnp.concatenate(
             [half_of(w, ci, 0, nc) for w in (w_query, w_key, w_value)], axis=1
         )
-        att_send[0], quarter, grad_y, *o_over = gate(att_send[0], quarter, grad_y, *o_over)
-        all_w = lax.all_gather(quarter, ("tensor", "fsdp", "context"), axis=0, tiled=False)
-        all_w = all_w.reshape(nt, nf * depth, 3 * cols)
+        att_send[0], quarter = gate(att_send[0], quarter)
+        all_q = lax.all_gather(quarter, ("tensor", "fsdp"), axis=0, tiled=False)
+
+        att = [att_send[0]] + [pz(att_send[j], j) for j in range(1, nt)]
+        att[1], grad_y, *o_over = gate(att[1], grad_y, *o_over)
         grad_rows = [grad_low, grad_y, grad_c, pc(grad_y, 1)]
-
-        att = [att_send[0]] + [pz(att_send[j], j) for j in range(1, nt)]
-        chunk = pl.BlockSpec((1, zr, width), lambda t, *_: (t, 0, 0))
-        chunk_z = pl.BlockSpec((1, zr, width), lambda t, pos: (t, pos[1], 0))
-        small = pl.BlockSpec((1, zr, cols), lambda t, *_: (t, 0, 0))
+        chunk = whole((trees, zr, width))
+        chunk_z = pl.BlockSpec((trees, zr, width), lambda i, pos: (0, pos[1], 0))
+        small = whole((trees, zr, cols))
         o_all = tuple(o_blocks) + tuple(o_over)
-        o_specs = [whole(o_all[0].shape)] * len(o_all)
+        o_specs = [whole(o.shape) for o in o_all]
         o_scratch = [pltpu.VMEM((nt * cols, width), BF)]
         hidden, normed_two, stat_a = call(
             functools.partial(mix_kernel, nt),
-            (trees,),
+            (1,),
             [small] * nt + o_specs + [chunk_z, row_1, row_1, row_1],
             (chunk, chunk, stat_spec),
             (sds((trees, zr, width), F32), sds((trees, zr, width), BF), stat),
@@ -874,33 +972,41 @@
 
         rows_two = normed_two.reshape(mine, width)
         rows_y = pc(rows_two, 2)
-        ff_rows = [rows_two, rows_y, pc(rows_two, 1), pc(rows_y, 1)]
+        rows_c = pc(rows_two, 1)
         block = whole((mine, width))
         units = nt * fc
-        half_spec, full_spec = whole((2, mine, width)), whole((4, mine, units))
-        half_sds, full_sds = sds((2, mine, width), BF), sds((4, mine, units), BF)
-        gn_near, gn_far, active, grad_up = call(
+        half_spec = whole((2, mine, width))
+        half_sds, full_sds = sds((2, mine, width), BF), sds((2, mine, units), BF)
+        unit_spec = pl.BlockSpec((2, mine, fc), lambda z, *_: (0, 0, z))
+        pack_spec = pl.BlockSpec((1,) + packs.shape[1:], lambda z, *_: (z, 0, 0, 0, 0))
+        feed = call(
             ff_kernel,
-            (1,),
-            [block] * 8 + [whole(packs.shape)],
-            (half_spec, half_spec, full_spec, full_spec),
-            (half_sds, half_sds, full_sds, full_sds),
-            [pltpu.VMEM((4, mine, width), BF)] * 2 + [pltpu.VMEM((nt, width, fc), BF)] * 2,
+            (nt,),
+            [block] * 4 + [pack_spec],
+            (block, block, unit_spec, unit_spec),
+            (sds((mine, width), BF), sds((mine, width), BF), full_sds, full_sds),
+            [pltpu.VMEM((2 * mine, width), F32)],
             prefetch=0,
-            vmem=48,
+            vmem=32,
             name="feed",
             keep=True,
-            us=20,
-        )(*ff_rows, *grad_rows, packs)
-        gn_got = pc(gn_far, 1)
-        gn_mid = (gn_near[1].astype(F32) + gn_got[1].astype(F32)).astype(BF)
+            us=9,
+        )
+        gn_own, gn_c, act_a, gup_a = feed(rows_two, rows_c, grad_rows[0], grad_rows[2], packs)
+        rows_y, gn_own, gn_c = gate(rows_y, gn_own, gn_c)
+        rows_cy = pc(rows_y, 1)
+        gn_got = [pc(gn_c, 1)]
+        gn_y, gn_cy, act_b, gup_b = feed(rows_y, rows_cy, grad_rows[1], grad_rows[3], packs)
+        ff_rows = [rows_two, rows_c, rows_y, rows_cy]
+        cot_rows = [grad_rows[0], grad_rows[2], grad_rows[1], grad_rows[3]]
+        gn_got.append(pc(gn_cy, 1))
+        gn_mid = (gn_y.astype(F32) + gn_got[1].astype(F32)).astype(BF)
+        gn_mid, gn_got[0], act_b, gup_b = gate(gn_mid, gn_got[0], act_b, gup_b)
         gn_end = pc(gn_mid, 2)
-        unit_spec = pl.BlockSpec((4, mine, fc), lambda z, *_: (0, 0, z))
-        pack_spec = pl.BlockSpec((1,) + packs.shape[1:], lambda z, *_: (z, 0, 0, 0, 0))
         ff_sent, ff_near, ff_far = call(
             ff_grad_kernel,
             (nt,),
-            [block] * 8 + [unit_spec, unit_spec, pack_spec],
+            [block] * 8 + [unit_spec] * 4 + [pack_spec],
             (
                 pl.BlockSpec((nf, 1, 2, depth, fc), lambda z, *_: (0, z, 0, 0, 0)),
                 half_spec,
@@ -908,21 +1014,21 @@
             ),
             (sds((nf, nt, 2, depth, fc), BF), half_sds, half_sds),
             [pltpu.VMEM((4 * mine, width), BF)] * 2
-            + [pltpu.VMEM((4 * mine, width), F32), pltpu.VMEM((width, fc), BF)],
+            + [pltpu.VMEM((4 * mine, width), F32), pltpu.VMEM((width, fc), BF)]
+            + [pltpu.VMEM((4 * mine, fc), BF)] * 2,
             prefetch=0,
             vmem=56,
             name="feed_grads",
             keep=True,
             us=16,
-        )(*ff_rows, *grad_rows, active, grad_up, packs)
-        gn_end, ff_sent, ff_near, ff_far = gate(gn_end, ff_sent, ff_near, ff_far)
+        )(*ff_rows, *cot_rows, act_a, gup_a, act_b, gup_b, packs)
+        gn_end, ff_sent, ff_near, ff_far, all_q = gate(gn_end, ff_sent, ff_near, ff_far, all_q)
         ff_got = pc(ff_far, 1)
 
-        pair = pl.BlockSpec((1, 1, zr, width), lambda t, *_: (0, t, 0, 0))
         grad_hidden, grad_branch, *rest = call(
             functools.partial(branch_back_kernel, nt),
-            (trees,),
-            o_specs + [pair, pair, chunk, chunk, chunk_z, row_1, row_1],
+            (1,),
+            o_specs + [chunk] * 4 + [chunk_z, row_1, row_1],
             (chunk, chunk) + (small,) * nt + (stat_spec,),
             (sds((trees, zr, width), F32), sds((trees, zr, width), BF))
             + (sds((trees, zr, cols), BF),) * nt
@@ -933,8 +1039,8 @@
         )(
             pos,
             *o_all,
-            gn_near.reshape(2, trees, zr, width),
-            gn_got.reshape(2, trees, zr, width),
+            gn_own.reshape(trees, zr, width),
+            gn_got[0].reshape(trees, zr, width),
             gn_end.reshape(trees, zr, width),
             hidden,
             cotangent,
@@ -943,25 +1049,34 @@
         )
         stat_b = rest.pop()
         ff_got, grad_branch, *rest = gate(ff_got, grad_branch, *rest)
+        all_q, rest[0] = gate(all_q, rest[0])
+        all_y = pc(all_q, 2)
         grad_heads = [rest[0]] + [ps(rest[j], j) for j in range(1, nt)]
         ff_mid = (ff_near[1].astype(F32) + ff_got[1].astype(F32)).astype(BF)
         ff_end = pc(ff_mid, 2)
-        part_attn = mm_tn(
-            jnp.concatenate([a.reshape(mine, cols) for a in att], axis=1),
-            grad_branch.reshape(mine, width),
-        ).reshape(nt, cols, width)
-        cut = lambda k: half_of(part_attn, k, 1, nc)
-        attn_got = pc(jnp.stack([cut(ci ^ 1), cut(ci ^ 3)]).astype(BF), 1).astype(F32)
-        attn_near = cut(ci) + attn_got[0]
-        attn_mid = (cut(ci ^ 2) + attn_got[1]).astype(BF)
+        o_rows = cols // nc
+        att_specs = (whole((2, nt, o_rows, width)),) + (whole((nt, o_rows, width)),) * 2
+        attn_far, attn_mid, attn_near = call(
+            functools.partial(attn_grad_kernel, nt),
+            (1,),
+            [whole((trees, zr, cols))] * nt + [whole((trees, zr, width))],
+            att_specs,
+            (
+                sds((2, nt, o_rows, width), BF),
+                sds((nt, o_rows, width), F32),
+                sds((nt, o_rows, width), F32),
+            ),
+            [pltpu.VMEM((cols, width), F32)],
+            name="attn_grads",
+            us=4,
+        )(pos, *att, grad_branch)
 
         mlp_out = ff_near[0].astype(F32) + ff_got[0].astype(F32) + ff_end.astype(F32)
         result = (hidden.reshape(mine, width) + mlp_out).astype(BF)
-        result, attn_near, attn_mid, *grad_heads = gate(
-            result, attn_near, attn_mid, *grad_heads
+        result, attn_near, attn_mid, attn_far, *grad_heads = gate(
+            result, attn_near, attn_mid, attn_far, *grad_heads
         )
         result = result.reshape(trees, zr, width)
-        o_rows = cols // nc
 
         def spread_near(x):
             if nt == 4:
@@ -989,36 +1104,44 @@
             return lax.ppermute(x, "tensor", pairs + [(b, a) for a, b in pairs])
 
         first_at = [jnp.maximum(zi - 1, 0), jnp.minimum(zi + 1, nt - 1), zi]
-        ends = (zi == 0) | (zi == 3)
 
         out_near = spread_near(result)
-        attn_end = pc(attn_mid, 2)
+        attn_got = pc(attn_far, 1)
 
         *dq_send, grad_q, kv_near, kv_far, bias_rows = backward(
             *tables, *sources, *grad_heads, log_total
         )
         ff_half = lax.psum_scatter(ff_sent, "fsdp", scatter_dimension=0, tiled=True)[0]
         ff_half = ff_half.reshape(nt, 2 * depth, fc)
-        kv_far, kv_near, attn_end, *out_near = gate(kv_far, kv_near, attn_end, *out_near)
+        kv_far, kv_near, attn_got, all_y, *out_near = gate(
+            kv_far, kv_near, attn_got, all_y, *out_near
+        )
         kv_got = pc(kv_far, 1)
         kv_mid = (kv_near[1].astype(F32) + kv_got[1].astype(F32)).astype(BF)
-        kv_mid, result, attn_end, ff_half = gate(kv_mid, result, attn_end, ff_half)
+        own = lax.psum_scatter(ff_half, "tensor", scatter_dimension=0, tiled=True)[0]
+        kv_mid, result, attn_got, attn_near, attn_mid, all_q, all_y = gate(
+            kv_mid, result, attn_got, attn_near, attn_mid, all_q, all_y
+        )
+        all_w = [all_q, all_y, pc(all_q, 1), pc(all_y, 1)]
         kv_end = pc(kv_mid, 2)
         if nt == 4:
-            out_far = [swap(result, [(0, 3)]), swap(result, [(0, 2), (1, 3)])]
+            out_far = [swap(result, [(0, 2), (1, 3)])]
+            out_far.append(
+                lax.ppermute(out_far[0], "tensor", [(2, 3), (1, 0), (3, 2), (0, 1)])
+            )
         else:
             out_far = [pz(result, j) for j in range(2, nt - 1)]
-        attn_sum = attn_near + attn_end.astype(F32)
-        attn_sum = scatter_f(attn_sum, 2).astype(BF)
+        attn_two = jnp.stack([attn_near, attn_mid]) + attn_got.astype(F32)
+        attn_two = scatter_f(attn_two, 3)
+        attn_end = pc(attn_two[1].astype(BF), 2)
+        kv_end, attn_two, attn_end, all_w, *out_far = gate(
+            kv_end, attn_two, attn_end, all_w, *out_far
+        )
+        attn_sum = (attn_two[0] + attn_end.astype(F32)).astype(BF)
         attn_sum = lax.dynamic_slice_in_dim(
             jnp.concatenate([attn_sum, attn_sum], axis=0), nt - zi, nt, 0
         )
-        if depth == 2 * fc:
-            ff_half = jnp.concatenate(
-                [ff_half, attn_sum[:, :, :fc], attn_sum[:, :, fc:]], axis=1
-            )
-        kv_end, ff_half, attn_sum, *out_far = gate(kv_end, ff_half, attn_sum, *out_far)
-        own = lax.psum_scatter(ff_half, "tensor", scatter_dimension=0, tiled=True)[0]
+        attn_own = lax.psum_scatter(attn_sum, "tensor", scatter_dimension=0, tiled=True)[0]
         five = pl.BlockSpec((1, 1, 1, tall, cols), lambda t, k, *_: (0, k, t, 0, 0))
         four = pl.BlockSpec((1, 1, tall, cols), lambda t, k, *_: (k, t, 0, 0))
         send = pl.BlockSpec((3, 1, zr + zs, cols), lambda t, k, *_: (0, t, 0, 0))
@@ -1056,30 +1179,38 @@
             us=8,
         )(pos, normed, grad_q, grad_kv)
         if nt == 4:
-            places = [first_at[0], first_at[1], jnp.where(ends, 3 - zi, zi), zi, zi ^ 2]
-            blocks = [out_near[0], out_near[1], out_far[0], result, out_far[1]]
+            places = first_at + [zi ^ 2, 3 - zi]
+            blocks = [out_near[0], out_near[1], result, *out_far]
         else:
             blocks = [result, *out_near, *out_far]
             places = [zi, (zi + 1) % nt, (zi - 1) % nt] + [(zi + j) % nt for j in range(2, nt - 1)]
         (output,) = ordered(blocks, places, (zr,))
-        qkv_far, qkv_mid, qkv_own, output, *dqkv = gate(
-            qkv_far, qkv_mid, qkv_own, output, *dqkv
-        )
-        qkv_got = pc(qkv_far, 1).astype(F32)
-
-        chunk_sz = pl.BlockSpec((1, zs, width), lambda t, pos: (t, pos[1], 0))
+        own_y = pc(own, 2)
+        qkv_mid, qkv_own, qkv_far, own_y, output, attn_own, *dqkv = gate(
+            qkv_mid, qkv_own, qkv_far, own_y, output, attn_own, *dqkv
+        )
+        qkv_got = pc(qkv_far, 1)
+        own_blocks = (own, own_y, pc(own, 1), pc(own_y, 1))
+
+        chunk_sz = pl.BlockSpec((trees, zs, width), lambda i, pos: (0, pos[1], 0))
         grads_own, stat_c = call(
             functools.partial(input_back_kernel, nt),
-            (trees,),
-            [pl.BlockSpec((3, 1, zr + zs, cols), lambda t, *_: (0, t, 0, 0))] * nt
-            + [whole(all_w.shape), chunk_z, chunk_sz, chunk, row_1],
-            (pl.BlockSpec((1, zr + zs, width), lambda t, *_: (t, 0, 0)), stat_spec),
+            (1,),
+            [whole((3, trees, zr + zs, cols))] * nt
+            + [whole(all_q.shape)] * 4
+            + [chunk_z, chunk_sz, chunk, row_1],
+            (whole((trees, zr + zs, width)), stat_spec),
             (sds((trees, zr + zs, width), BF), stat),
-            vmem=32,
+            [
+                pltpu.VMEM((nt, nf * depth, 3 * cols), BF),
+                pltpu.VMEM((trees * (zr + zs), width), F32),
+            ],
+            vmem=44,
             name="input_back",
             keep=True,
-        )(pos, *dqkv, all_w, tokens, state, grad_hidden, gain_1)
-        qkv_got, grads_own = gate(qkv_got, grads_own)
+        )(pos, *dqkv, *all_w, tokens, state, grad_hidden, gain_1)
+        grads_own, qkv_got, *own_blocks = gate(grads_own, qkv_got, *own_blocks)
+        qkv_got = qkv_got.astype(F32)
 
         bias_own = jnp.sum(bias_rows, axis=2)
         bias_all = lax.dynamic_update_slice(
@@ -1098,29 +1229,20 @@
         sums = jnp.concatenate([stat_c[:2], early], axis=0)
 
         in_near = spread_near(grads_own)
+        *in_near, sums, attn_own, qkv_got = gate(*in_near, sums, attn_own, qkv_got)
+        qkv_end = pc((qkv_mid + qkv_got[1]).astype(BF), 2)
         if nt == 4:
-            in_far = [swap(grads_own, [(0, 2), (1, 3)])]
+            c = swap(grads_own, [(0, 2), (1, 3)])
+            d = lax.ppermute(c, "tensor", [(2, 3), (1, 0), (3, 2), (0, 1)])
+            places = first_at + [zi ^ 2, 3 - zi]
+            blocks = [in_near[0], in_near[1], grads_own, c, d]
         else:
             in_far = [pz(grads_own, j) for j in range(2, nt - 1)]
-        qkv_end = pc((qkv_mid + qkv_got[1]).astype(BF), 2)
-        if depth == 2 * fc:
-            parts = [own]
-        else:
-            parts = [own, lax.psum_scatter(attn_sum, "tensor", scatter_dimension=0, tiled=True)[0]]
-        parts_y = [pc(p, 2) for p in parts]
+            blocks = [grads_own, *in_near, *in_far]
+        tokens_grad, state_grad = ordered(blocks, places, (zr, zs))
         sums = sums + px(sums) if nf == 2 else lax.psum(sums, "fsdp")
         sums = sums + pc(sums, 1)
         sums = sums + pc(sums, 2)
-        in_far[0], qkv_end, sums, *parts_y = gate(in_far[0], qkv_end, sums, *parts_y)
-        if nt == 4:
-            in_far.append(
-                lax.ppermute(in_far[0], "tensor", [(2, 3), (1, 0), (3, 2), (0, 1)])
-            )
-            places = first_at + [zi ^ 2, 3 - zi]
-            blocks = [in_near[0], in_near[1], grads_own, in_far[0], in_far[1]]
-        else:
-            blocks = [grads_own, *in_near, *in_far]
-        tokens_grad, state_grad = ordered(blocks, places, (zr, zs))
         if nt & (nt - 1):
             sums = lax.psum(sums, "tensor")
         else:
@@ -1130,45 +1252,35 @@
                 k = 2 * k
 
         qkv_sum = scatter_f(qkv_own + qkv_got[0] + qkv_end.astype(F32), 0)[0].astype(BF)
+        if depth % o_rows == 0 and depth * o_rows % dq_rows == 0 and nf == 2:
+            folded = jnp.concatenate([attn_own[:, :fc], attn_own[:, fc:]], axis=0)
+            qkv_sum = jnp.concatenate([qkv_sum, folded], axis=1)
+        else:
+            attn_full = gather_c(attn_own, 0).astype(F32)
+            folded = None
         qkv_y = pc(qkv_sum, 2)
         qkv_blocks = (qkv_sum, qkv_y, pc(qkv_sum, 1), pc(qkv_y, 1))
-        grad_qkv = call(
+        last_shapes = ((depth, cols),) * 3
+        if folded is not None:
+            last_shapes += ((nc * o_rows, depth),)
+        *grad_qkv, grad_attn_out = call(
             finish_qkv_kernel,
             (1,),
-            [whole((dq_rows, 3 * cols))] * 4,
-            (whole((depth, cols)),) * 3,
-            (sds((depth, cols), F32),) * 3,
+            [whole(qkv_sum.shape)] * 4,
+            tuple(whole(v) for v in last_shapes),
+            tuple(sds(v, F32) for v in last_shapes),
             name="finish_qkv",
-            us=1,
-        )(pos, *qkv_blocks)
-        over = [pc(p, 1) for p in parts] + [pc(p, 1) for p in parts_y]
-        if depth == 2 * fc:
-            grad_in, grad_out, grad_attn_out = call(
-                functools.partial(finish_ff_kernel, o_rows),
-                (1,),
-                [whole(own.shape)] * 4,
-                (whole((depth, nc * fc)), whole((nc * fc, depth)), whole((nc * o_rows, depth))),
-                (
-                    sds((depth, nc * fc), F32),
-                    sds((nc * fc, depth), F32),
-                    sds((nc * o_rows, depth), F32),
-                ),
-                name="finish_ff",
-                us=1,
-            )(pos, own, parts_y[0], over[0], over[1])
-        else:
-            flips = (ci, ci ^ 2, ci ^ 1, ci ^ 3)
-            ff_blocks = [parts[0], parts_y[0], over[0], over[2]]
-            at = [k * fc for k in flips]
-            grad_in = place([b[:depth] for b in ff_blocks], at, 1, nc * fc).astype(F32)
-            grad_out = place([b[depth:].T for b in ff_blocks], at, 0, nc * fc).astype(F32)
-            grad_attn_out = place(
-                [parts[1], parts_y[1], over[1], over[3]],
-                [k * o_rows for k in flips],
-                0,
-                nc * o_rows,
-            ).astype(F32)
-
+            us=0,
+        )(pos, *qkv_blocks) + (() if folded is not None else (attn_full,))
+        grad_in, grad_out = call(
+            finish_ff_kernel,
+            (1,),
+            [whole(own.shape)] * 4,
+            (whole((depth, nc * fc)), whole((nc * fc, depth))),
+            (sds((depth, nc * fc), F32), sds((nc * fc, depth), F32)),
+            name="finish_ff",
+            us=0,
+        )(pos, *own_blocks)
         last = sums[4:].reshape(-1)
         bias_sum = last[: bias_all.size].reshape(bias_all.shape)
         grad_bias = lax.dynamic_slice_in_dim(bias_sum, zi * heads, heads, 0)

time: 548 us -> 511 us (0.932); the launches traced: 547 us -> 503 us
  waiting for transfers between devices: 269 us -> 240 us
  other arithmetic: 29.3 us -> 19.2 us
    ppermute x9, waiting for transfers between devices: 112 us -> 36 us  [pz(): return lax.ppermute(x, 'tensor', [(a, (a - j) % nt) for a in range(nt)])]
    reduce_scatter x0 -> x1, waiting for transfers between devices: none -> 42.6 us  [on_device(): lax.psum_scatter(attn_sum, 'tensor', scatter_dimension=0, tiled=True)[0]]
    ppermute x2, starting transfers between devices: 0.01 us -> 18.1 us  [on_device(): sums = sums + lax.ppermute(sums, 'tensor', [(a, a ^ k) for a in range(nt)])]
    all_gather x1, waiting for transfers between devices: 0.03 us -> 11 us  [on_device(): all_q = lax.all_gather(quarter, ('tensor', 'fsdp'), axis=0, tiled=False)]
    ppermute x2, waiting for transfers between devices: 3.66 us -> 10.9 us  [spread_near(): lax.ppermute(x, 'tensor', [(0, 1), (1, 2), (2, 3)])]
    ppermute x1 -> x2, waiting for transfers between devices: 13.2 us -> 6.31 us  [the longest x1 6.14 us: on_device(): lax.ppermute(out_far[0], 'tensor', [(2, 3), (1, 0), (3, 2), (0, 1)])]
    ppermute x3, starting transfers between devices: 11.7 us -> 5.05 us  [ps(): return lax.ppermute(x, 'tensor', [(a, (a + j) % nt) for a in range(nt)])]
    ppermute x28 -> x32, waiting for transfers between devices: 46.9 us -> 40.9 us  [pc(): return lax.ppermute(x, 'context', [(a, a ^ k) for a in range(nc)])]
  transfers between devices with their start and end apart: 62 -> 64, of which waited for: 29 -> 27; matrix products, arithmetic and copies ran while one was open for 7% -> 5% of each run, Pallas kernels for 19% -> 25%
where the time goes in v3:
time: 511 us; the launch traced here: 503 us
  waiting for transfers between devices  240 us (47%)
  Pallas kernels  130 us (25%)
  starting transfers between devices  74.2 us (15%)
  local copies, waits for them, and re-layouts  24 us (5%)
  other arithmetic  19.2 us (4%)
  between operations  15.1 us (3%)
    pallas_call x10, Pallas kernels, run(): return kernel(*args[:prefetch], *rest)  110 us
    ppermute x2, waiting for transfers between devices, swap(): return lax.ppermute(x, 'tensor', pairs + [(b, a) for a, b in pairs])  52.6 us
    reduce_scatter x1, waiting for transfers between devices, on_device(): lax.psum_scatter(attn_sum, 'tensor', scatter_dimension=0, tiled=True)[0]  42.6 us
    ppermute x32, waiting for transfers between devices, pc(): return lax.ppermute(x, 'context', [(a, a ^ k) for a in range(nc)])  40.9 us
    ppermute x9, waiting for transfers between devices, pz(): return lax.ppermute(x, 'tensor', [(a, (a - j) % nt) for a in range(nt)])  36 us
    ppermute x5, waiting for transfers between devices, px(): return lax.ppermute(x, 'fsdp', [(0, 1), (1, 0)])  30.9 us
    ppermute x2, starting transfers between devices, on_device(): sums = sums + lax.ppermute(sums, 'tensor', [(a, a ^ k) for a in range(nt)])  18.1 us
    ppermute x32, starting transfers between devices, pc(): return lax.ppermute(x, 'context', [(a, a ^ k) for a in range(nc)])  17.8 us
  transfers between devices with their start and end apart: 64, of which 27 were waited for; matrix products, arithmetic and copies ran while one was open for 5% of the time, Pallas kernels for 25%

profile of v3, /device:TPU:0, one launch (start us, length us, event | category | flops | bytes accessed | tf_op | source)
XLA Modules:
  0.0 503.1 jit_solution(3323969267221401897)
XLA Ops:
  14.9 9.0 %collective-permute-done.refs_3_ = bf16[256,768]{1,0:T(8,128)(2,1)S(1)} collective-permute-done((bf16[256,768]{1,0:T(8,128)(2,1)S(1)}, bf16[256,768]{1,0:T(8,128)(2,1)S(1)}, u32[]{:S(2)}, u32[]{:S(2)}) %collective-permute-start) | collective-permute-done | bytes 393248 | tf_op jit(solution)/shard_map/ppermute | solution.py:749
  41.7 6.5 %collective-permute-done.4.refs_5_.refs_1_ = bf16[256,512]{1,0:T(8,128)(2,1)S(1)} collective-permute-done((bf16[256,512]{1,0:T(8,128)(2,1)S(1)}, bf16[256,512]{1,0:T(8,128)(2,1)S(1)}, u32[]{:S(2)}, u32[]{:S(2)}) %collective-permute-start.4) | collective-permute-done | bytes 262176 | tf_op jit(solution)/shard_map/ppermute | solution.py:755
  48.2 22.6 %collective-permute-done.5.refs_6_.refs_2_ = bf16[256,512]{1,0:T(8,128)(2,1)S(1)} collective-permute-done((bf16[256,512]{1,0:T(8,128)(2,1)S(1)}, bf16[256,512]{1,0:T(8,128)(2,1)S(1)}, u32[]{:S(2)}, u32[]{:S(2)}) %collective-permute-start.5) | collective-permute-done | bytes 262176 | tf_op jit(solution)/shard_map/ppermute | solution.py:755
  76.2 13.8 %attend.1 = (bf16[2,160,256]{2,1,0:T(8,128)(2,1)}, bf16[2,160,256]{2,1,0:T(8,128)(2,1)}, bf16[2,160,256]{2,1,0:T(8,128)(2,1)}, bf16[2,160,256]{2,1,0:T(8,128)(2,1)}, f32[2,2,8,640]{3,2,1,0:T(8,128)}) custom-call(s32[2,20]{1,0:T(2,128)S(1)} %copy-done.22, s32[2,5]{1,0:T(2,128)S(1)} %copy-done.23, s32[3]{0:T(128)S(1)} %pad_add_fusion.pos.pos_ref, ...), custom_call_target="tpu_custom_call" | custom-call | flops 16000000000 | bytes 48000000 | tf_op jit(solution)/shard_map/attend/pallas_call | solution.py:298
  94.1 14.3 %collective-permute-done.10.refs_8_.refs_4_ = bf16[4,256,512]{2,1,0:T(8,128)(2,1)} collective-permute-done((bf16[4,256,512]{2,1,0:T(8,128)(2,1)S(1)}, bf16[4,256,512]{2,1,0:T(8,128)(2,1)}, u32[]{:S(2)}, u32[]{:S(2)}) %collective-permute-start.10) | collective-permute-done | bytes 1048608 | tf_op jit(solution)/shard_map/ppermute | solution.py:749
  108.4 6.8 %collective-permute-done.11.refs_2_ = bf16[2,160,256]{2,1,0:T(8,128)(2,1)S(1)} collective-permute-done((bf16[2,160,256]{2,1,0:T(8,128)(2,1)}, bf16[2,160,256]{2,1,0:T(8,128)(2,1)S(1)}, u32[]{:S(2)}, u32[]{:S(2)}) %collective-permute-start.11) | collective-permute-done | bytes 163872 | tf_op jit(solution)/shard_map/ppermute | solution.py:755
  115.9 4.9 mix.1
  124.0 12.7 %feed.2 = (bf16[320,1024]{1,0:T(8,128)(2,1)}, bf16[320,1024]{1,0:T(8,128)(2,1)}, bf16[2,320,1024]{2,1,0:T(8,128)(2,1)}, bf16[2,320,1024]{2,1,0:T(8,128)(2,1)}) custom-call(bf16[320,1024]{1,0:T(8,128)(2,1)} %bitcast.105, bf16[320,1024]{1,0:T(8,128)(2,1)} %copy-done.47, bf16[320,1024]{1,0:T(8,128)(2,1)} %bitcast.5.refs_2_.refs_4_, ...), custom_call_target="tpu_custom_call" | custom-call | flops 8999999488 | bytes 27000000 | tf_op jit(solution)/shard_map/feed/pallas_call | solution.py:298
  141.2 12.7 %feed.3 = (bf16[320,1024]{1,0:T(8,128)(2,1)}, bf16[320,1024]{1,0:T(8,128)(2,1)}, bf16[2,320,1024]{2,1,0:T(8,128)(2,1)}, bf16[2,320,1024]{2,1,0:T(8,128)(2,1)}) custom-call(bf16[320,1024]{1,0:T(8,128)(2,1)} %copy-done.48, bf16[320,1024]{1,0:T(8,128)(2,1)} %copy-done.51, bf16[320,1024]{1,0:T(8,128)(2,1)} %collective-permute-done.9.refs_2_.refs_6_, ...), custom_call_target="tpu_custom_call" | custom-call | flops 8999999488 | bytes 27000000 | tf_op jit(solution)/shard_map/feed/pallas_call | solution.py:298
  158.6 15.6 %feed_grads.1 = (bf16[2,4,2,512,256]{4,3,2,1,0:T(8,128)(2,1)}, bf16[2,320,1024]{2,1,0:T(8,128)(2,1)}, bf16[2,320,1024]{2,1,0:T(8,128)(2,1)}) custom-call(bf16[320,1024]{1,0:T(8,128)(2,1)} %bitcast.106, bf16[320,1024]{1,0:T(8,128)(2,1)} %copy-done.47, bf16[320,1024]{1,0:T(8,128)(2,1)} %copy-done.48, bf16[320,1024]{1,0:T(8,128)(2,1)} %copy-done.51, ...), custom_call_target="tpu_custom_call" | custom-call | flops 16000000000 | bytes 48000000 | tf_op jit(solution)/shard_map/feed_grads/pallas_call | solution.py:298
  174.2 11.0 %all-gather.7.cloned.1.call-done = bf16[1024,768]{1,0:T(8,128)(2,1)} async-done(((bf16[128,768]{1,0:T(8,128)(2,1)}), bf16[1024,768]{1,0:T(8,128)(2,1)}) %all-gather.7.cloned.1.call-update) | async-done | bytes 1572880 | tf_op jit(solution)/shard_map/all_gather | solution.py:951
  186.7 6.2 %branch_back.1 = (f32[2,160,1024]{2,1,0:T(8,128)}, bf16[2,160,1024]{2,1,0:T(8,128)(2,1)}, bf16[2,160,256]{2,1,0:T(8,128)(2,1)}, bf16[2,160,256]{2,1,0:T(8,128)(2...) custom-call(s32[3]{0:T(128)S(1)} %pad_add_fusion.pos.pos_ref, ...), custom_call_target="tpu_custom_call" | custom-call | flops 4000000000 | bytes 12000000 | tf_op jit(solution)/shard_map/branch_back/pallas_call | solution.py:298
  202.4 8.5 %collective-permute-done.22 = bf16[320,1024]{1,0:T(8,128)(2,1)S(1)} collective-permute-done((bf16[320,1024]{1,0:T(8,128)(2,1)S(1)}, bf16[320,1024]{1,0:T(8,128)(2,1)S(1)}, u32[]{:S(2)}, u32[]{:S(2)}) %collective-permute-start.22) | collective-permute-done | bytes 655392 | tf_op jit(solution)/shard_map/ppermute | solution.py:752
  217.7 21.9 %attend_back.1 = (bf16[2,160,256]{2,1,0:T(8,128)(2,1)}, bf16[2,160,256]{2,1,0:T(8,128)(2,1)}, bf16[2,160,256]{2,1,0:T(8,128)(2,1)}, bf16[2,160,256]{2,1,0:T(8,12...) custom-call(s32[2,20]{1,0:T(2,128)S(1)} %copy-done.22, ...), custom_call_target="tpu_custom_call" | custom-call | flops 24000000000 | bytes 72000000 | tf_op jit(solution)/shard_map/attend_back/pallas_call | solution.py:298
  245.4 5.9 %collective-permute-done.30.got = bf16[2,2,2,768,256]{4,3,2,1,0:T(8,128)(2,1)} collective-permute-done((bf16[2,2,2,768,256]{4,3,2,1,0:T(8,128)(2,1)}, bf16[2,2,2,768,256]{4,3,2,1,0:T(8,128)(2,1)}, u32[]{:S(2)}, u32[]{:S(2)}) %collective-permute-start.30) | collective-permute-done | bytes 3145760 | tf_op jit(solution)/shard_map/ppermute | solution.py:752
  262.7 52.6 %collective-permute-done.36.refs_3_ = bf16[2,160,1024]{2,1,0:T(8,128)(2,1)} collective-permute-done((bf16[2,160,1024]{2,1,0:T(8,128)(2,1)S(1)}, bf16[2,160,1024]{2,1,0:T(8,128)(2,1)}, u32[]{:S(2)}, u32[]{:S(2)}) %collective-permute-start.36) | collective-permute-done | bytes 655392 | tf_op jit(solution)/shard_map/ppermute | solution.py:1104
  319.3 6.7 %collective-permute-done.33 = bf16[4,64,512]{2,1,0:T(8,128)(2,1)S(1)} collective-permute-done((bf16[4,64,512]{2,1,0:T(8,128)(2,1)S(1)}, bf16[4,64,512]{2,1,0:T(8,128)(2,1)S(1)}, u32[]{:S(2)}, u32[]{:S(2)}) %collective-permute-start.33) | collective-permute-done | bytes 262176 | tf_op jit(solution)/shard_map/ppermute | solution.py:752
  326.1 6.1 %collective-permute-done.37.refs_4_ = bf16[2,160,1024]{2,1,0:T(8,128)(2,1)S(1)} collective-permute-done((bf16[2,160,1024]{2,1,0:T(8,128)(2,1)}, bf16[2,160,1024]{2,1,0:T(8,128)(2,1)S(1)}, u32[]{:S(2)}, u32[]{:S(2)}) %collective-permute-start.37) | collective-permute-done | bytes 655392 | tf_op jit(solution)/shard_map/ppermute | solution.py:1130
  332.2 5.9 %combine.1 = (bf16[2,2,768,256]{3,2,1,0:T(8,128)(2,1)}, bf16[3,2,192,256]{3,2,1,0:T(8,128)(2,1)}, bf16[3,2,192,256]{3,2,1,0:T(8,128)(2,1)}, bf16[3,2,192,256]{3,2,1,0:T(8,128)(2,1)}, bf16[3,2,192,256]{3,2,1,0:T(8,128)(2,1)}) custom-call(s32[3]{0:T(128)S(1)} %pad_add_fusion.pos.pos_ref, bf16[2,2,2,768,256]{4,3,2,1,0:T(8,128)(2,1)} %get-tuple-element.233.own, ...), custom_call_target="tpu_custom_call" | custom-call | flops 4000000000 | bytes 12000000 | tf_op jit(solution)/shard_map/combine/pallas_call | solution.py:298
  346.2 7.3 %qkv_grads.1 = (bf16[2,2,128,768]{3,2,1,0:T(8,128)(2,1)}, f32[2,128,768]{2,1,0:T(8,128)}, f32[2,128,768]{2,1,0:T(8,128)}) custom-call(s32[3]{0:T(128)S(1)} %pad_add_fusion.pos.pos_ref, bf16[2,768,1024]{2,1,0:T(8,128)(2,1)} %copy-done.25, bf16[2,640,256]{2,1,0:T(8,128)(2,1)} %get-tuple-element.227.gq, bf16[2,2,768,256]{3,2,1,0:T(8,128)(2,1)} %get-tuple-element.251.gkv), custom_call_target="tpu_custom_call" | custom-call | flops 8000000000 | bytes 24000000 | tf_op jit(solution)/shard_map/qkv_grads/pallas_call | solution.py:298
  353.5 42.6 %reduce-scatter.8.cloned.1.call-done = bf16[1,64,512]{2,1,0:T(8,128)(2,1)} async-done(((bf16[4,64,512]{2,1,0:T(8,128)(2,1)}), bf16[1,64,512]{2,1,0:T(8,128)(2,1)}) %reduce-scatter.8.cloned.1.call-update) | async-done | bytes 65552 | tf_op jit(solution)/shard_map/reduce_scatter | solution.py:1144
  401.2 9.4 %input_back.1 = (bf16[2,192,1024]{2,1,0:T(8,128)(2,1)}, f32[8,1024]{1,0:T(8,128)}) custom-call(s32[3]{0:T(128)S(1)} %pad_add_fusion.pos.pos_ref, bf16[3,2,192,256]{3,2,1,0:T(8,128)(2,1)} %get-tuple-element.270.refs_0_, bf16[3,2,192,256]{3,2,1,0:T(8,128)(2,1)} %collective-permute-done.39.refs_1_, bf16[3,2,192,256]{3,2,1,0:T(8,128)(2,1)} %collective-permute-done.40.refs_2_, ...), custom_call_target="tpu_custom_call" | custom-call | flops 4000000000 | bytes 12000000 | tf_op jit(solution)/shard_map/input_back/pallas_call | solution.py:298
  420.0 10.9 %collective-permute-done.45.refs_0_ = bf16[2,192,1024]{2,1,0:T(8,128)(2,1)S(1)} collective-permute-done((bf16[2,192,1024]{2,1,0:T(8,128)(2,1)}, bf16[2,192,1024]{2,1,0:T(8,128)(2,1)S(1)}, u32[]{:S(2)}, u32[]{:S(2)}) %collective-permute-start.45) | collective-permute-done | bytes 786464 | tf_op jit(solution)/shard_map/ppermute | solution.py:1084
  447.1 18.1 %collective-permute-start.57 = (f32[6,1024]{1,0:T(8,128)S(1)}, f32[6,1024]{1,0:T(8,128)S(1)}, u32[]{:S(2)}, u32[]{:S(2)}) collective-permute-start(f32[6,1024]{1,0:T(8,128)S(1)} %add.134), channel_id=1, source_target_pairs={{0,1},{1,0},{2,3},{3,2},{4,5},{5,4},{6,7},{7,6},{8,9},{9,8},{10,11... | collective-permute-start | bytes 73736 | tf_op jit(solution)/shard_map/ppermute | solution.py:1251
  (301 shorter events, 155.9 us)
Async XLA Ops:
  7.2 116.0 %all-gather.5.cloned.1.call-start = ((), (), s32[]{:S(2)}) async-start(), calls=%async_computation.6 | async-start | bytes 4718592 | tf_op jit(solution)/shard_map/all_gather | solution.py:894
  11.8 173.4 %all-gather.7.cloned.1.call-start = ((), (), s32[]{:S(2)}) async-start(), calls=%async_computation.7 | async-start | bytes 1769472 | tf_op jit(solution)/shard_map/all_gather | solution.py:951
  33.3 37.6 %collective-permute-start.3 = (bf16[2,768,512]{2,1,0:T(8,128)(2,1)S(1)}, bf16[2,768,512]{2,1,0:T(8,128)(2,1)}, u32[]{:S(2)}, u32[]{:S(2)}) collective-permute-start(bf16[2,768,512]{2,1,0:T(8,128)(2,1)S(1)} %get-tuple-element.164.refs_0_.refs_4_), channel_id=1, source_target_pairs={{0,8},{4,12},{8,0},{12,4},{1,9},{5,13},{9,1},{13,5},{2,10},{6,14},... | collective-permute-start | bytes 4718600 | tf_op jit(solution)/shard_map/ppermute | solution.py:752
  38.7 32.2 %collective-permute-start.5 = (bf16[256,512]{1,0:T(8,128)(2,1)S(1)}, bf16[256,512]{1,0:T(8,128)(2,1)S(1)}, u32[]{:S(2)}, u32[]{:S(2)}) collective-permute-start(bf16[256,512]{1,0:T(8,128)(2,1)S(1)} %copy-done.39), channel_id=1, source_target_pairs={{0,2},{1,3},{2,0},{3,1},{4,6},{5,7},{6,4},{7,5},{8,10},{9,11},{10,... | collective-permute-start | bytes 786440 | tf_op jit(solution)/shard_map/ppermute | solution.py:755
  38.7 32.2 %collective-permute-start.6 = (bf16[256,512]{1,0:T(8,128)(2,1)S(1)}, bf16[256,512]{1,0:T(8,128)(2,1)S(1)}, u32[]{:S(2)}, u32[]{:S(2)}) collective-permute-start(bf16[256,512]{1,0:T(8,128)(2,1)S(1)} %copy-done.39), channel_id=1, source_target_pairs={{0,1},{1,2},{2,3},{3,0},{4,5},{5,6},{6,7},{7,4},{8,9},{9,10},{10,1... | collective-permute-start | bytes 786440 | tf_op jit(solution)/shard_map/ppermute | solution.py:755
  41.7 34.5 %collective-permute-start.2 = (bf16[2,768,512]{2,1,0:T(8,128)(2,1)S(1)}, bf16[2,768,512]{2,1,0:T(8,128)(2,1)}, u32[]{:S(2)}, u32[]{:S(2)}) collective-permute-start(bf16[2,768,512]{2,1,0:T(8,128)(2,1)S(1)} %get-tuple-element.164.refs_0_.refs_4_), channel_id=1, source_target_pairs={{0,4},{4,0},{8,12},{12,8},{1,5},{5,1},{9,13},{13,9},{2,6},{6,2},{1... | collective-permute-start | bytes 4718600 | tf_op jit(solution)/shard_map/ppermute | solution.py:752
  73.0 35.4 %collective-permute-start.10 = (bf16[4,256,512]{2,1,0:T(8,128)(2,1)S(1)}, bf16[4,256,512]{2,1,0:T(8,128)(2,1)}, u32[]{:S(2)}, u32[]{:S(2)}) collective-permute-start(bf16[4,256,512]{2,1,0:T(8,128)(2,1)S(1)} %pad_maximum_fusion), channel_id=1, source_target_pairs={{0,16},{16,0},{1,17},{17,1},{2,18},{18,2},{3,19},{19,3},{4,20},{20... | collective-permute-start | bytes 3145736 | tf_op jit(solution)/shard_map/ppermute | solution.py:749
  94.1 28.0 %collective-permute-start.15 = (bf16[320,1024]{1,0:T(8,128)(2,1)}, bf16[320,1024]{1,0:T(8,128)(2,1)S(1)}, u32[]{:S(2)}, u32[]{:S(2)}) collective-permute-start(bf16[320,1024]{1,0:T(8,128)(2,1)} %bitcast.5.refs_2_.refs_4_), channel_id=1, source_target_pairs={{0,4},{4,0},{8,12},{12,8},{1,5},{5,1},{9,13},{13,9},{2,6},{6,2},{1... | collective-permute-start | bytes 1966088 | tf_op jit(solution)/shard_map/ppermute | solution.py:752
  138.2 107.1 %reduce-scatter.4.cloned.1.call-start = ((), (), s32[]{:S(2)}) async-start(), calls=%async_computation.3 | async-start | bytes 6291456 | tf_op jit(solution)/shard_map/reduce_scatter | solution.py:1114
  157.6 27.6 %collective-permute-start.20 = (bf16[320,1024]{1,0:T(8,128)(2,1)S(1)}, bf16[320,1024]{1,0:T(8,128)(2,1)S(1)}, u32[]{:S(2)}, u32[]{:S(2)}) collective-permute-start(bf16[320,1024]{1,0:T(8,128)(2,1)S(1)} %add_convert_fusion.2), channel_id=1, source_target_pairs={{0,8},{4,12},{8,0},{12,4},{1,9},{5,13},{9,1},{13,5},{2,10},{6,14},... | collective-permute-start | bytes 1966088 | tf_op jit(solution)/shard_map/ppermute | solution.py:752
  186.0 158.7 %reduce-scatter.6.cloned.1.call-start = ((), (), s32[]{:S(2)}) async-start(), calls=%async_computation.4 | async-start | bytes 2621440 | tf_op jit(solution)/shard_map/reduce_scatter | solution.py:1121
  199.9 44.4 %collective-permute-start.27 = (bf16[8,128,768]{2,1,0:T(8,128)(2,1)}, bf16[8,128,768]{2,1,0:T(8,128)(2,1)}, u32[]{:S(2)}, u32[]{:S(2)}) collective-permute-start(bf16[8,128,768]{2,1,0:T(8,128)(2,1)} %bitcast.19.refs_4_), channel_id=1, source_target_pairs={{0,8},{4,12},{8,0},{12,4},{1,9},{5,13},{9,1},{13,5},{2,10},{6,14},... | collective-permute-start | bytes 4718600 | tf_op jit(solution)/shard_map/ppermute | solution.py:752
  245.3 150.7 %reduce-scatter.8.cloned.1.call-start = ((), (), s32[]{:S(2)}) async-start(), calls=%async_computation.5 | async-start | bytes 327680 | tf_op jit(solution)/shard_map/reduce_scatter | solution.py:1144
  254.7 77.5 %collective-permute-start.31 = (bf16[2,2,768,256]{3,2,1,0:T(8,128)(2,1)}, bf16[2,2,768,256]{3,2,1,0:T(8,128)(2,1)}, u32[]{:S(2)}, u32[]{:S(2)}) collective-permute-start(bf16[2,2,768,256]{3,2,1,0:T(8,128)(2,1)} %fusion), channel_id=1, source_target_pairs={{0,8},{4,12},{8,0},{12,4},{1,9},{5,13},{9,1},{13,5},{2,10},{6,14},... | collective-permute-start | bytes 4718600 | tf_op jit(solution)/shard_map/ppermute | solution.py:752
  256.2 76.0 %collective-permute-start.34 = (bf16[8,128,768]{2,1,0:T(8,128)(2,1)}, bf16[8,128,768]{2,1,0:T(8,128)(2,1)}, u32[]{:S(2)}, u32[]{:S(2)}) collective-permute-start(bf16[8,128,768]{2,1,0:T(8,128)(2,1)} %bitcast.19.refs_4_), channel_id=1, source_target_pairs={{0,4},{4,0},{8,12},{12,8},{1,5},{5,1},{9,13},{13,9},{2,6},{6,2},{1... | collective-permute-start | bytes 4718600 | tf_op jit(solution)/shard_map/ppermute | solution.py:752
  256.2 76.0 %collective-permute-start.35 = (bf16[8,128,768]{2,1,0:T(8,128)(2,1)}, bf16[8,128,768]{2,1,0:T(8,128)(2,1)}, u32[]{:S(2)}, u32[]{:S(2)}) collective-permute-start(bf16[8,128,768]{2,1,0:T(8,128)(2,1)} %collective-permute-done.27.refs_5_), channel_id=1, source_target_pairs={{0,4},{4,0},{8,12},{12,8},{1,5},{5,1},{9,13},{13,9},{2,6},{6,2},{1... | collective-permute-start | bytes 4718600 | tf_op jit(solution)/shard_map/ppermute | solution.py:752
  256.7 58.6 %collective-permute-start.36 = (bf16[2,160,1024]{2,1,0:T(8,128)(2,1)S(1)}, bf16[2,160,1024]{2,1,0:T(8,128)(2,1)}, u32[]{:S(2)}, u32[]{:S(2)}) collective-permute-start(bf16[2,160,1024]{2,1,0:T(8,128)(2,1)S(1)} %bitcast.79), channel_id=1, source_target_pairs={{0,2},{1,3},{2,0},{3,1},{4,6},{5,7},{6,4},{7,5},{8,10},{9,11},{10,... | collective-permute-start | bytes 1966088 | tf_op jit(solution)/shard_map/ppermute | solution.py:1104
  261.8 53.5 %collective-permute-start.32 = (bf16[2,4,64,512]{3,2,1,0:T(8,128)(2,1)S(1)}, bf16[2,4,64,512]{3,2,1,0:T(8,128)(2,1)S(1)}, u32[]{:S(2)}, u32[]{:S(2)}) collective-permute-start(bf16[2,4,64,512]{3,2,1,0:T(8,128)(2,1)S(1)} %dynamic-slice_convert_fusion), channel_id=1, source_target_pairs={{0,16},{16,0},{1,17},{17,1},{2,18},{18,2},{3,19},{19,3},{4,20},{20... | collective-permute-start | bytes 1572872 | tf_op jit(solution)/shard_map/ppermute | solution.py:749
  338.2 57.9 %collective-permute-start.39 = (bf16[3,2,192,256]{3,2,1,0:T(8,128)(2,1)}, bf16[3,2,192,256]{3,2,1,0:T(8,128)(2,1)}, u32[]{:S(2)}, u32[]{:S(2)}) collective-permute-start(bf16[3,2,192,256]{3,2,1,0:T(8,128)(2,1)} %get-tuple-element.263), channel_id=1, source_target_pairs={{0,3},{1,0},{2,1},{3,2},{4,7},{5,4},{6,5},{7,6},{8,11},{9,8},{10,9... | collective-permute-start | bytes 1769480 | tf_op jit(solution)/shard_map/ppermute | solution.py:755
  339.6 56.5 %collective-permute-start.40 = (bf16[3,2,192,256]{3,2,1,0:T(8,128)(2,1)}, bf16[3,2,192,256]{3,2,1,0:T(8,128)(2,1)}, u32[]{:S(2)}, u32[]{:S(2)}) collective-permute-start(bf16[3,2,192,256]{3,2,1,0:T(8,128)(2,1)} %get-tuple-element.264), channel_id=1, source_target_pairs={{0,2},{1,3},{2,0},{3,1},{4,6},{5,7},{6,4},{7,5},{8,10},{9,11},{10,... | collective-permute-start | bytes 1769480 | tf_op jit(solution)/shard_map/ppermute | solution.py:755
  340.0 56.1 %collective-permute-start.41 = (bf16[3,2,192,256]{3,2,1,0:T(8,128)(2,1)}, bf16[3,2,192,256]{3,2,1,0:T(8,128)(2,1)}, u32[]{:S(2)}, u32[]{:S(2)}) collective-permute-start(bf16[3,2,192,256]{3,2,1,0:T(8,128)(2,1)} %get-tuple-element.265), channel_id=1, source_target_pairs={{0,1},{1,2},{2,3},{3,0},{4,5},{5,6},{6,7},{7,4},{8,9},{9,10},{10,1... | collective-permute-start | bytes 1769480 | tf_op jit(solution)/shard_map/ppermute | solution.py:755
  344.7 51.4 %collective-permute-start.38 = (bf16[1024,256]{1,0:T(8,128)(2,1)}, bf16[1024,256]{1,0:T(8,128)(2,1)S(1)}, u32[]{:S(2)}, u32[]{:S(2)}) collective-permute-start(bf16[1024,256]{1,0:T(8,128)(2,1)} %bitcast.83), channel_id=1, source_target_pairs={{0,8},{4,12},{8,0},{12,4},{1,9},{5,13},{9,1},{13,5},{2,10},{6,14},... | collective-permute-start | bytes 1572872 | tf_op jit(solution)/shard_map/ppermute | solution.py:752
  414.0 56.1 %collective-permute-start.47 = (bf16[2,192,1024]{2,1,0:T(8,128)(2,1)}, bf16[2,192,1024]{2,1,0:T(8,128)(2,1)}, u32[]{:S(2)}, u32[]{:S(2)}) collective-permute-start(bf16[2,192,1024]{2,1,0:T(8,128)(2,1)} %get-tuple-element.283.refs_2_), channel_id=1, source_target_pairs={{0,2},{1,3},{2,0},{3,1},{4,6},{5,7},{6,4},{7,5},{8,10},{9,11},{10,... | collective-permute-start | bytes 2359304 | tf_op jit(solution)/shard_map/ppermute | solution.py:1104
  435.5 39.4 %collective-permute-start.49 = (bf16[2,128,768]{2,1,0:T(8,128)(2,1)}, bf16[2,128,768]{2,1,0:T(8,128)(2,1)}, u32[]{:S(2)}, u32[]{:S(2)}) collective-permute-start(bf16[2,128,768]{2,1,0:T(8,128)(2,1)} %fusion.2), channel_id=1, source_target_pairs={{0,8},{4,12},{8,0},{12,4},{1,9},{5,13},{9,1},{13,5},{2,10},{6,14},... | collective-permute-start | bytes 1179656 | tf_op jit(solution)/shard_map/ppermute | solution.py:752
  (100 other events, 1128.4 us)
Sparse Core Ops, SparseCore 0:
  11.9 106.4 all-gather.4
  138.3 46.7 all-gather.6
  187.5 53.1 reduce-scatter.3
  245.4 62.7 reduce-scatter.5
  341.7 54.3 reduce-scatter.7

commit v4 on v3

--- a/solution.py
+++ b/solution.py
@@ -173,14 +173,14 @@
     do_refs, lse_ref = refs[8 : 8 + nt], refs[8 + nt]
     dq_refs = refs[9 + nt : 9 + 2 * nt]
     dq_ref, near_ref, far_ref, db_ref = refs[9 + 2 * nt : 13 + 2 * nt]
-    kall, vall, kall_t, kws, vws, kw_ts, bm, dk, dv, near, far, dos, do_t, q_t, raws_a, dps_a, dss_a, pbs_a = refs[
+    kall, vall, kall_t, kw, vw, kw_t, bm, dk, dv, near, far, dos, do_t, q_t, raws, dps, dss, pbs = refs[
         13 + 2 * nt :
     ]
     h, t = pl.program_id(0), pl.program_id(1)
     ctx, zi = pos_ref[0], pos_ref[1]
     rows, win = local_segs * seg, levels * seg
-    each = (kws.shape[1] - win) // 4
-    blocks = kws.shape[1] // seg
+    each = (kw.shape[0] - win) // 4
+    blocks = kw.shape[0] // seg
     n = rows // nt
     bias_tables(rb_ref, h, levels, seg, bm)
     for b in range(4):
@@ -189,10 +189,9 @@
         vall[b] = parts_v[b][0, :rows, :]
         turned = parts_k[b][0].T
         kall_t[b] = turned[:, :rows]
-        for i in range(2):
-            kws[i, at, :] = parts_k[b][0, rows:, :]
-            vws[i, at, :] = parts_v[b][0, rows:, :]
-            kw_ts[i, :, at] = turned[:, rows:]
+        kw[at, :] = parts_k[b][0, rows:, :]
+        vw[at, :] = parts_v[b][0, rows:, :]
+        kw_t[:, at] = turned[:, rows:]
     dk[...] = jnp.zeros(dk.shape, F32)
     dv[...] = jnp.zeros(dv.shape, F32)
     for j in range(nt):
@@ -207,8 +206,6 @@
         far[...] = jnp.zeros(far.shape, F32)
 
     def one(s, carry):
-        kw, vw, kw_t = (r.at[s % 2] for r in (kws, vws, kw_ts))
-        raws, dps, dss, pbs = (r.at[s % 2] for r in (raws_a, dps_a, dss_a, pbs_a))
         line = chain(par_ref, t, ctx * local_segs + s, levels, all_segs, local_segs, ctx)
         for lev, (_, part, block) in enumerate(line):
             start = pl.ds(pl.multiple_of(block * seg, seg), seg)
@@ -216,7 +213,7 @@
             kw[at, :] = kall[part, start, :]
             vw[at, :] = vall[part, start, :]
             kw_t[:, at] = kall_t[part, :, start]
-        at = slice(s * seg, (s + 1) * seg)
+        at = pl.ds(pl.multiple_of(s * seg, seg), seg)
         turned, do_turned = q_t[:, at], do_t[:, at]
         lse = lse_ref[0, 0, 0:1, at]
         delta = None
@@ -260,8 +257,7 @@
                     dv[b, rows:, :] += gv[i : i + each]
         return carry
 
-    for s in range(local_segs):
-        one(s, 0)
+    lax.fori_loop(0, local_segs, one, 0)
     for ref, pair in ((near_ref, (0, 2)), (far_ref, (1, 3))):
         for place, b in enumerate(pair):
             ref[place, 0, 0] = dk[b].astype(BF)
@@ -326,9 +322,9 @@
         vm(BF, 4, rows, head_dim),
         vm(BF, 4, rows, head_dim),
         vm(BF, 4, head_dim, rows),
-        vm(BF, 2, wide, head_dim),
-        vm(BF, 2, wide, head_dim),
-        vm(BF, 2, head_dim, wide),
+        vm(BF, wide, head_dim),
+        vm(BF, wide, head_dim),
+        vm(BF, head_dim, wide),
         vm(F32, win, seg),
         vm(F32, 4, tall, head_dim),
         vm(F32, 4, tall, head_dim),
@@ -337,10 +333,10 @@
         vm(BF, rows, head_dim),
         vm(BF, head_dim, rows),
         vm(BF, head_dim, rows),
-        vm(F32, 2, wide, seg),
-        vm(F32, 2, wide, seg),
-        vm(BF, 2, wide, seg),
-        vm(BF, 2, wide, seg),
+        vm(F32, wide, seg),
+        vm(F32, wide, seg),
+        vm(BF, wide, seg),
+        vm(BF, wide, seg),
     ]
     lse_shape = jax.ShapeDtypeStruct((trees, heads, 8, rows), F32)
 
@@ -485,20 +481,19 @@
 
 
 def mix_kernel(n, pos, *refs):
-    att, blocks = refs[:n], refs[n:-8]
-    tok, cell, gain, shift, hid_ref, n2_ref, stat_ref, w = refs[-8:]
+    att, blocks = refs[:n], refs[n:-10]
+    tok, cell, gain, shift, hid_ref, n2_ref, stat_ref, w, left, branch = refs[-10:]
 
     load_projection(pos, blocks, w)
     stat_ref[...] = jnp.zeros(stat_ref.shape, F32)
     cols = att[0].shape[2]
     shape = tok.shape
     mine = shape[0] * shape[1]
-    branch = None
     for j in range(n):
-        part = mm(att[j][...].reshape(mine, cols), w[j * cols : (j + 1) * cols, :])
-        branch = part if branch is None else branch + part
+        left[:, j * cols : (j + 1) * cols] = att[j][...].reshape(mine, cols)
+    branch[...] = mm(left[...], w[...])
     x = tok[...].astype(F32).reshape(mine, shape[2])
-    gated = cell[...] * branch
+    gated = cell[...] * branch[...]
     hidden = x + gated
     hid_ref[...] = hidden.reshape(shape)
     xhat, _ = norm_stats(hidden)
@@ -509,51 +504,53 @@
 
 def ff_kernel(*refs):
     xs, gs = refs[0:2], refs[2:4]
-    pack, first_ref, second_ref, act_ref, gup_ref, acc = refs[4:]
+    pack, first_ref, second_ref, act_ref, gup_ref, acc, xall, gall = refs[4:]
     nf, depth = pack.shape[1], pack.shape[3]
     z = pl.program_id(0)
     mine = xs[0].shape[0]
     cut = [slice(f * depth, (f + 1) * depth) for f in range(nf)]
-    for p in range(2):
-        up = mm(xs[p][:, cut[0]], pack[0, 0, 0])
-        back = mm(gs[p][:, cut[0]], pack[0, 0, 1])
+
+    @pl.when(z == 0)
+    def _():
+        for p in range(2):
+            xall[p] = xs[p][...]
+            gall[p] = gs[p][...]
+        acc[...] = jnp.zeros(acc.shape, F32)
+
+    def one(p, carry):
+        up = mm(xall[p, :, cut[0]], pack[0, 0, 0])
+        back = mm(gall[p, :, cut[0]], pack[0, 0, 1])
         for f in range(1, nf):
-            up = up + mm(xs[p][:, cut[f]], pack[0, f, 0])
-            back = back + mm(gs[p][:, cut[f]], pack[0, f, 1])
+            up = up + mm(xall[p, :, cut[f]], pack[0, f, 0])
+            back = back + mm(gall[p, :, cut[f]], pack[0, f, 1])
         value, slope = gelu_parts(up)
         act_ref[p] = value.astype(BF)
         gup = (back * slope).astype(BF)
         gup_ref[p] = gup
-        at = slice(p * mine, (p + 1) * mine)
         for f in range(nf):
-            part = mm_nt(gup, pack[0, f, 0])
-
-            @pl.when(z == 0)
-            def _():
-                acc[at, cut[f]] = part
-
-            @pl.when(z > 0)
-            def _():
-                acc[at, cut[f]] += part
+            acc[p, :, cut[f]] += mm_nt(gup, pack[0, f, 0])
+        return carry
+
+    lax.fori_loop(0, 2, one, 0)
 
     @pl.when(z == pl.num_programs(0) - 1)
     def _():
-        first_ref[...] = acc[:mine, :].astype(BF)
-        second_ref[...] = acc[mine:, :].astype(BF)
+        first_ref[...] = acc[0].astype(BF)
+        second_ref[...] = acc[1].astype(BF)
 
 
 def ff_grad_kernel(*refs):
     xs, gs = refs[0:4], refs[4:8]
     act_a, gup_a, act_b, gup_b, pack = refs[8:13]
-    sent_ref, near_ref, far_ref, xall, gall, acc, wout, act, gup = refs[13:]
+    sent_ref, near_ref, far_ref, rows, acc, wout, units = refs[13:]
     _, nf, _, depth, fc = pack.shape
     mine = xs[0].shape[0]
 
     @pl.when(pl.program_id(0) == 0)
     def _():
         for p in range(4):
-            xall[p * mine : (p + 1) * mine, :] = xs[p][...]
-            gall[p * mine : (p + 1) * mine, :] = gs[p][...]
+            rows[0, p * mine : (p + 1) * mine, :] = xs[p][...]
+            rows[1, p * mine : (p + 1) * mine, :] = gs[p][...]
         acc[...] = jnp.zeros(acc.shape, F32)
 
     for f in range(nf):
@@ -561,12 +558,18 @@
     for half, (a_ref, u_ref) in enumerate(((act_a, gup_a), (act_b, gup_b))):
         for p in range(2):
             at = slice((2 * half + p) * mine, (2 * half + p + 1) * mine)
-            act[at, :] = a_ref[p]
-            gup[at, :] = u_ref[p]
-    acc[...] += mm_nt(act[...], wout[...])
-    for i, part in ((0, mm_tn(xall[...], gup[...])), (1, mm_tn(gall[...], act[...]))):
+            units[1, at, :] = a_ref[p]
+            units[0, at, :] = u_ref[p]
+
+    acc[...] += mm_nt(units[1], wout[...])
+
+    def grads(i, carry):
+        part = mm_tn(rows[i], units[i])
         for f in range(nf):
             sent_ref[f, 0, i] = part[f * depth : (f + 1) * depth].astype(BF)
+        return carry
+
+    lax.fori_loop(0, 2, grads, 0)
 
     @pl.when(pl.program_id(0) == pl.num_programs(0) - 1)
     def _():
@@ -623,25 +626,38 @@
 
 def input_back_kernel(nt, pos, *refs):
     blocks = refs[:nt]
-    parts, (tok, st, gh, gain, out_ref, stat_ref, w, every) = refs[nt : nt + 4], refs[nt + 4 :]
+    parts, (tok, st, gh, gain, out_ref, stat_ref, w, left, every) = (
+        refs[nt : nt + 4],
+        refs[nt + 4 :],
+    )
     m = parts[0].shape[1]
     nf = parts[0].shape[0] // nt
-    for flip, part in zip((0, 2, 1, 3), parts):
-        for z in range(nt):
-            for f in range(nf):
-                at = (f * 4 + jnp.bitwise_xor(pos[0], flip)) * m
-                w[z, pl.ds(pl.multiple_of(at, m), m), :] = part[z * nf + f]
     cols = blocks[0].shape[3]
     trees, n = tok.shape[0], tok.shape[1]
     tall = blocks[0].shape[2]
-    total = None
+    for flip, part in zip((0, 2, 1, 3), parts):
+
+        def put(i, carry, flip=flip, part=part):
+            z = lax.div(i, nf)
+            at = ((i - z * nf) * 4 + jnp.bitwise_xor(pos[0], flip)) * m
+            w[z, pl.ds(pl.multiple_of(at, m), m), :] = part[i]
+            return carry
+
+        lax.fori_loop(0, nt * nf, put, 0)
     for j in range(nt):
-        k = lax.rem(pos[1] + j, nt)
         for i in range(3):
-            left = blocks[j][i].reshape(trees * tall, cols)
-            part = mm_nt(left, w[k, :, i * cols : (i + 1) * cols])
-            total = part if total is None else total + part
-    every[...] = total
+            left[j, :, i * cols : (i + 1) * cols] = blocks[j][i].reshape(trees * tall, cols)
+    step = 256
+
+    def one(i, carry):
+        at = pl.ds(pl.multiple_of(i * step, step), step)
+        total = mm_nt(left[0], w[pos[1], at, :])
+        for j in range(1, nt):
+            total = total + mm_nt(left[j], w[lax.rem(pos[1] + j, nt), at, :])
+        every[:, at] = total
+        return carry
+
+    lax.fori_loop(0, every.shape[1] // step, one, 0)
     stat_ref[...] = jnp.zeros(stat_ref.shape, F32)
     for t in range(trees):
         for x_ref, lo, hi, extra in ((tok, 0, n, gh), (st, n, tall, None)):
@@ -657,12 +673,14 @@
 
 def attn_grad_kernel(nt, pos, *refs):
     blocks, grad = refs[:nt], refs[nt]
-    far_ref, mid_ref, own_ref, acc = refs[nt + 1 :]
+    far_ref, mid_ref, own_ref, acc, left = refs[nt + 1 :]
     n = own_ref.shape[1]
     rows = grad.shape[0] * grad.shape[1]
-    right = grad[...].reshape(rows, grad.shape[2])
     for j in range(nt):
-        acc[...] = mm_tn(blocks[j][...].reshape(rows, acc.shape[0]), right)
+        left[j] = blocks[j][...].reshape(rows, acc.shape[0])
+
+    def one(j, carry):
+        acc[...] = mm_tn(left[j], grad[...].reshape(rows, grad.shape[2]))
         for flip, ref in ((0, own_ref), (2, mid_ref), (1, far_ref), (3, far_ref)):
             k = jnp.bitwise_xor(pos[0], flip)
             piece = acc[pl.ds(pl.multiple_of(k * n, n), n), :]
@@ -670,6 +688,9 @@
                 ref[flip // 2, j] = piece.astype(BF)
             else:
                 ref[j] = piece
+        return carry
+
+    lax.fori_loop(0, nt, one, 0)
 
 
 def qkv_grad_kernel(nf, pos, x, gq, gkv, far_ref, mid_ref, own_ref, acc, right):
@@ -680,15 +701,17 @@
     right[rows:, :cols] = jnp.zeros((tall - rows, cols), BF)
     right[:, cols : 2 * cols] = gkv[0, 0]
     right[:, 2 * cols :] = gkv[1, 0]
-    part = mm_tn(x[0], right[...])
 
     @pl.when(t == 0)
     def _():
-        acc[...] = part
-
-    @pl.when(t > 0)
-    def _():
-        acc[...] += part
+        acc[...] = jnp.zeros(acc.shape, F32)
+
+    def one(i, carry):
+        at = pl.ds(pl.multiple_of(i * cols, cols), cols)
+        acc[:, at] += mm_tn(x[0], right[:, at])
+        return carry
+
+    lax.fori_loop(0, 3, one, 0)
 
     @pl.when(t == pl.num_programs(0) - 1)
     def _():
@@ -965,7 +988,8 @@
             [small] * nt + o_specs + [chunk_z, row_1, row_1, row_1],
             (chunk, chunk, stat_spec),
             (sds((trees, zr, width), F32), sds((trees, zr, width), BF), stat),
-            o_scratch,
+            o_scratch
+            + [pltpu.VMEM((mine, nt * cols), BF), pltpu.VMEM((mine, width), F32)],
             name="mix",
             keep=True,
         )(pos, *att, *o_all, tokens, cell, gain_2, shift_2)
@@ -985,7 +1009,7 @@
             [block] * 4 + [pack_spec],
             (block, block, unit_spec, unit_spec),
             (sds((mine, width), BF), sds((mine, width), BF), full_sds, full_sds),
-            [pltpu.VMEM((2 * mine, width), F32)],
+            [pltpu.VMEM((2, mine, width), F32)] + [pltpu.VMEM((2, mine, width), BF)] * 2,
             prefetch=0,
             vmem=32,
             name="feed",
@@ -1013,9 +1037,12 @@
                 half_spec,
             ),
             (sds((nf, nt, 2, depth, fc), BF), half_sds, half_sds),
-            [pltpu.VMEM((4 * mine, width), BF)] * 2
-            + [pltpu.VMEM((4 * mine, width), F32), pltpu.VMEM((width, fc), BF)]
-            + [pltpu.VMEM((4 * mine, fc), BF)] * 2,
+            [
+                pltpu.VMEM((2, 4 * mine, width), BF),
+                pltpu.VMEM((4 * mine, width), F32),
+                pltpu.VMEM((width, fc), BF),
+                pltpu.VMEM((2, 4 * mine, fc), BF),
+            ],
             prefetch=0,
             vmem=56,
             name="feed_grads",
@@ -1066,7 +1093,7 @@
                 sds((nt, o_rows, width), F32),
                 sds((nt, o_rows, width), F32),
             ),
-            [pltpu.VMEM((cols, width), F32)],
+            [pltpu.VMEM((cols, width), F32), pltpu.VMEM((nt, mine, cols), BF)],
             name="attn_grads",
             us=4,
         )(pos, *att, grad_branch)
@@ -1203,6 +1230,7 @@
             (sds((trees, zr + zs, width), BF), stat),
             [
                 pltpu.VMEM((nt, nf * depth, 3 * cols), BF),
+                pltpu.VMEM((nt, trees * (zr + zs), 3 * cols), BF),
                 pltpu.VMEM((trees * (zr + zs), width), F32),
             ],
             vmem=44,

time: 511 us -> 505 us (0.988); the launches traced: 503 us -> 504 us
  transfers between devices with their start and end apart: 64 -> 64, of which waited for: 27 -> 27; matrix products, arithmetic and copies ran while one was open for 5% -> 5% of each run, Pallas kernels for 25% -> 26%
where the time goes in v4:
time: 505 us; the launch traced here: 504 us
  waiting for transfers between devices  238 us (47%)
  Pallas kernels  134 us (27%)
  starting transfers between devices  74 us (15%)
  local copies, waits for them, and re-layouts  24 us (5%)
  other arithmetic  19.2 us (4%)
  between operations  14.6 us (3%)
    pallas_call x10, Pallas kernels, run(): return kernel(*args[:prefetch], *rest)  113 us
    ppermute x2, waiting for transfers between devices, swap(): return lax.ppermute(x, 'tensor', pairs + [(b, a) for a, b in pairs])  52.6 us
    reduce_scatter x1, waiting for transfers between devices, on_device(): lax.psum_scatter(attn_sum, 'tensor', scatter_dimension=0, tiled=True)[0]  41.8 us
    ppermute x32, waiting for transfers between devices, pc(): return lax.ppermute(x, 'context', [(a, a ^ k) for a in range(nc)])  39.8 us
    ppermute x9, waiting for transfers between devices, pz(): return lax.ppermute(x, 'tensor', [(a, (a - j) % nt) for a in range(nt)])  36 us
    ppermute x5, waiting for transfers between devices, px(): return lax.ppermute(x, 'fsdp', [(0, 1), (1, 0)])  30.9 us
    ppermute x2, starting transfers between devices, on_device(): sums = sums + lax.ppermute(sums, 'tensor', [(a, a ^ k) for a in range(nt)])  18.1 us
    ppermute x32, starting transfers between devices, pc(): return lax.ppermute(x, 'context', [(a, a ^ k) for a in range(nc)])  17.8 us
  transfers between devices with their start and end apart: 64, of which 27 were waited for; matrix products, arithmetic and copies ran while one was open for 5% of the time, Pallas kernels for 26%

profile of v4, /device:TPU:0, one launch (start us, length us, event | category | flops | bytes accessed | tf_op | source)
XLA Modules:
  0.0 503.8 jit_solution(6615209027568651639)
XLA Ops:
  14.9 9.0 %collective-permute-done.refs_3_ = bf16[256,768]{1,0:T(8,128)(2,1)S(1)} collective-permute-done((bf16[256,768]{1,0:T(8,128)(2,1)S(1)}, bf16[256,768]{1,0:T(8,128)(2,1)S(1)}, u32[]{:S(2)}, u32[]{:S(2)}) %collective-permute-start) | collective-permute-done | bytes 393248 | tf_op jit(solution)/shard_map/ppermute | solution.py:772
  41.7 6.5 %collective-permute-done.4.refs_5_.refs_1_ = bf16[256,512]{1,0:T(8,128)(2,1)S(1)} collective-permute-done((bf16[256,512]{1,0:T(8,128)(2,1)S(1)}, bf16[256,512]{1,0:T(8,128)(2,1)S(1)}, u32[]{:S(2)}, u32[]{:S(2)}) %collective-permute-start.4) | collective-permute-done | bytes 262176 | tf_op jit(solution)/shard_map/ppermute | solution.py:778
  48.2 22.6 %collective-permute-done.5.refs_6_.refs_2_ = bf16[256,512]{1,0:T(8,128)(2,1)S(1)} collective-permute-done((bf16[256,512]{1,0:T(8,128)(2,1)S(1)}, bf16[256,512]{1,0:T(8,128)(2,1)S(1)}, u32[]{:S(2)}, u32[]{:S(2)}) %collective-permute-start.5) | collective-permute-done | bytes 262176 | tf_op jit(solution)/shard_map/ppermute | solution.py:778
  76.2 13.8 %attend.1 = (bf16[2,160,256]{2,1,0:T(8,128)(2,1)}, bf16[2,160,256]{2,1,0:T(8,128)(2,1)}, bf16[2,160,256]{2,1,0:T(8,128)(2,1)}, bf16[2,160,256]{2,1,0:T(8,128)(2,1)}, f32[2,2,8,640]{3,2,1,0:T(8,128)}) custom-call(s32[2,20]{1,0:T(2,128)S(1)} %copy-done.22, s32[2,5]{1,0:T(2,128)S(1)} %copy-done.23, s32[3]{0:T(128)S(1)} %pad_add_fusion.pos.pos_ref, ...), custom_call_target="tpu_custom_call" | custom-call | flops 16000000000 | bytes 48000000 | tf_op jit(solution)/shard_map/attend/pallas_call | solution.py:294
  94.1 14.3 %collective-permute-done.10.refs_8_.refs_4_ = bf16[4,256,512]{2,1,0:T(8,128)(2,1)} collective-permute-done((bf16[4,256,512]{2,1,0:T(8,128)(2,1)S(1)}, bf16[4,256,512]{2,1,0:T(8,128)(2,1)}, u32[]{:S(2)}, u32[]{:S(2)}) %collective-permute-start.10) | collective-permute-done | bytes 1048608 | tf_op jit(solution)/shard_map/ppermute | solution.py:772
  108.4 6.8 %collective-permute-done.11.refs_2_ = bf16[2,160,256]{2,1,0:T(8,128)(2,1)S(1)} collective-permute-done((bf16[2,160,256]{2,1,0:T(8,128)(2,1)}, bf16[2,160,256]{2,1,0:T(8,128)(2,1)S(1)}, u32[]{:S(2)}, u32[]{:S(2)}) %collective-permute-start.11) | collective-permute-done | bytes 163872 | tf_op jit(solution)/shard_map/ppermute | solution.py:778
  115.9 4.9 mix.1
  123.9 10.8 %feed.2 = (bf16[320,1024]{1,0:T(8,128)(2,1)}, bf16[320,1024]{1,0:T(8,128)(2,1)}, bf16[2,320,1024]{2,1,0:T(8,128)(2,1)}, bf16[2,320,1024]{2,1,0:T(8,128)(2,1)}) custom-call(bf16[320,1024]{1,0:T(8,128)(2,1)} %bitcast.105, bf16[320,1024]{1,0:T(8,128)(2,1)} %copy-done.47, bf16[320,1024]{1,0:T(8,128)(2,1)} %bitcast.5.refs_2_.refs_4_, ...), custom_call_target="tpu_custom_call" | custom-call | flops 8999999488 | bytes 27000000 | tf_op jit(solution)/shard_map/feed/pallas_call | solution.py:294
  141.1 10.8 %feed.3 = (bf16[320,1024]{1,0:T(8,128)(2,1)}, bf16[320,1024]{1,0:T(8,128)(2,1)}, bf16[2,320,1024]{2,1,0:T(8,128)(2,1)}, bf16[2,320,1024]{2,1,0:T(8,128)(2,1)}) custom-call(bf16[320,1024]{1,0:T(8,128)(2,1)} %copy-done.48, bf16[320,1024]{1,0:T(8,128)(2,1)} %copy-done.51, bf16[320,1024]{1,0:T(8,128)(2,1)} %collective-permute-done.9.refs_2_.refs_6_, ...), custom_call_target="tpu_custom_call" | custom-call | flops 8999999488 | bytes 27000000 | tf_op jit(solution)/shard_map/feed/pallas_call | solution.py:294
  156.7 17.5 %feed_grads.1 = (bf16[2,4,2,512,256]{4,3,2,1,0:T(8,128)(2,1)}, bf16[2,320,1024]{2,1,0:T(8,128)(2,1)}, bf16[2,320,1024]{2,1,0:T(8,128)(2,1)}) custom-call(bf16[320,1024]{1,0:T(8,128)(2,1)} %bitcast.106, bf16[320,1024]{1,0:T(8,128)(2,1)} %copy-done.47, bf16[320,1024]{1,0:T(8,128)(2,1)} %copy-done.48, bf16[320,1024]{1,0:T(8,128)(2,1)} %copy-done.51, ...), custom_call_target="tpu_custom_call" | custom-call | flops 16000000000 | bytes 48000000 | tf_op jit(solution)/shard_map/feed_grads/pallas_call | solution.py:294
  174.3 10.7 %all-gather.7.cloned.1.call-done = bf16[1024,768]{1,0:T(8,128)(2,1)} async-done(((bf16[128,768]{1,0:T(8,128)(2,1)}), bf16[1024,768]{1,0:T(8,128)(2,1)}) %all-gather.7.cloned.1.call-update) | async-done | bytes 1572880 | tf_op jit(solution)/shard_map/all_gather | solution.py:974
  186.5 6.2 %branch_back.1 = (f32[2,160,1024]{2,1,0:T(8,128)}, bf16[2,160,1024]{2,1,0:T(8,128)(2,1)}, bf16[2,160,256]{2,1,0:T(8,128)(2,1)}, bf16[2,160,256]{2,1,0:T(8,128)(2...) custom-call(s32[3]{0:T(128)S(1)} %pad_add_fusion.pos.pos_ref, ...), custom_call_target="tpu_custom_call" | custom-call | flops 4000000000 | bytes 12000000 | tf_op jit(solution)/shard_map/branch_back/pallas_call | solution.py:294
  202.9 7.7 %collective-permute-done.22 = bf16[320,1024]{1,0:T(8,128)(2,1)S(1)} collective-permute-done((bf16[320,1024]{1,0:T(8,128)(2,1)S(1)}, bf16[320,1024]{1,0:T(8,128)(2,1)S(1)}, u32[]{:S(2)}, u32[]{:S(2)}) %collective-permute-start.22) | collective-permute-done | bytes 655392 | tf_op jit(solution)/shard_map/ppermute | solution.py:775
  217.2 23.9 %attend_back.1 = (bf16[2,160,256]{2,1,0:T(8,128)(2,1)}, bf16[2,160,256]{2,1,0:T(8,128)(2,1)}, bf16[2,160,256]{2,1,0:T(8,128)(2,1)}, bf16[2,160,256]{2,1,0:T(8,12...) custom-call(s32[2,20]{1,0:T(2,128)S(1)} %copy-done.22, ...), custom_call_target="tpu_custom_call" | custom-call | flops 24000000000 | bytes 72000000 | tf_op jit(solution)/shard_map/attend_back/pallas_call | solution.py:294
  245.3 5.7 %collective-permute-done.30.got = bf16[2,2,2,768,256]{4,3,2,1,0:T(8,128)(2,1)} collective-permute-done((bf16[2,2,2,768,256]{4,3,2,1,0:T(8,128)(2,1)}, bf16[2,2,2,768,256]{4,3,2,1,0:T(8,128)(2,1)}, u32[]{:S(2)}, u32[]{:S(2)}) %collective-permute-start.30) | collective-permute-done | bytes 3145760 | tf_op jit(solution)/shard_map/ppermute | solution.py:775
  262.4 52.6 %collective-permute-done.36.refs_3_ = bf16[2,160,1024]{2,1,0:T(8,128)(2,1)} collective-permute-done((bf16[2,160,1024]{2,1,0:T(8,128)(2,1)S(1)}, bf16[2,160,1024]{2,1,0:T(8,128)(2,1)}, u32[]{:S(2)}, u32[]{:S(2)}) %collective-permute-start.36) | collective-permute-done | bytes 655392 | tf_op jit(solution)/shard_map/ppermute | solution.py:1131
  319.1 6.7 %collective-permute-done.33 = bf16[4,64,512]{2,1,0:T(8,128)(2,1)S(1)} collective-permute-done((bf16[4,64,512]{2,1,0:T(8,128)(2,1)S(1)}, bf16[4,64,512]{2,1,0:T(8,128)(2,1)S(1)}, u32[]{:S(2)}, u32[]{:S(2)}) %collective-permute-start.33) | collective-permute-done | bytes 262176 | tf_op jit(solution)/shard_map/ppermute | solution.py:775
  325.8 6.1 %collective-permute-done.37.refs_4_ = bf16[2,160,1024]{2,1,0:T(8,128)(2,1)S(1)} collective-permute-done((bf16[2,160,1024]{2,1,0:T(8,128)(2,1)}, bf16[2,160,1024]{2,1,0:T(8,128)(2,1)S(1)}, u32[]{:S(2)}, u32[]{:S(2)}) %collective-permute-start.37) | collective-permute-done | bytes 655392 | tf_op jit(solution)/shard_map/ppermute | solution.py:1157
  332.0 5.9 %combine.1 = (bf16[2,2,768,256]{3,2,1,0:T(8,128)(2,1)}, bf16[3,2,192,256]{3,2,1,0:T(8,128)(2,1)}, bf16[3,2,192,256]{3,2,1,0:T(8,128)(2,1)}, bf16[3,2,192,256]{3,2,1,0:T(8,128)(2,1)}, bf16[3,2,192,256]{3,2,1,0:T(8,128)(2,1)}) custom-call(s32[3]{0:T(128)S(1)} %pad_add_fusion.pos.pos_ref, bf16[2,2,2,768,256]{4,3,2,1,0:T(8,128)(2,1)} %get-tuple-element.233.own, ...), custom_call_target="tpu_custom_call" | custom-call | flops 4000000000 | bytes 12000000 | tf_op jit(solution)/shard_map/combine/pallas_call | solution.py:294
  345.7 8.3 %qkv_grads.1 = (bf16[2,2,128,768]{3,2,1,0:T(8,128)(2,1)}, f32[2,128,768]{2,1,0:T(8,128)}, f32[2,128,768]{2,1,0:T(8,128)}) custom-call(s32[3]{0:T(128)S(1)} %pad_add_fusion.pos.pos_ref, bf16[2,768,1024]{2,1,0:T(8,128)(2,1)} %copy-done.25, bf16[2,640,256]{2,1,0:T(8,128)(2,1)} %get-tuple-element.227.gq, bf16[2,2,768,256]{3,2,1,0:T(8,128)(2,1)} %get-tuple-element.251.gkv), custom_call_target="tpu_custom_call" | custom-call | flops 8000000000 | bytes 24000000 | tf_op jit(solution)/shard_map/qkv_grads/pallas_call | solution.py:294
  354.0 41.8 %reduce-scatter.8.cloned.1.call-done = bf16[1,64,512]{2,1,0:T(8,128)(2,1)} async-done(((bf16[4,64,512]{2,1,0:T(8,128)(2,1)}), bf16[1,64,512]{2,1,0:T(8,128)(2,1)}) %reduce-scatter.8.cloned.1.call-update) | async-done | bytes 65552 | tf_op jit(solution)/shard_map/reduce_scatter | solution.py:1171
  400.9 10.8 %input_back.1 = (bf16[2,192,1024]{2,1,0:T(8,128)(2,1)}, f32[8,1024]{1,0:T(8,128)}) custom-call(s32[3]{0:T(128)S(1)} %pad_add_fusion.pos.pos_ref, bf16[3,2,192,256]{3,2,1,0:T(8,128)(2,1)} %get-tuple-element.270.refs_0_, bf16[3,2,192,256]{3,2,1,0:T(8,128)(2,1)} %collective-permute-done.39.refs_1_, bf16[3,2,192,256]{3,2,1,0:T(8,128)(2,1)} %collective-permute-done.40.refs_2_, ...), custom_call_target="tpu_custom_call" | custom-call | flops 4000000000 | bytes 12000000 | tf_op jit(solution)/shard_map/input_back/pallas_call | solution.py:294
  421.2 10.9 %collective-permute-done.45.refs_0_ = bf16[2,192,1024]{2,1,0:T(8,128)(2,1)S(1)} collective-permute-done((bf16[2,192,1024]{2,1,0:T(8,128)(2,1)}, bf16[2,192,1024]{2,1,0:T(8,128)(2,1)S(1)}, u32[]{:S(2)}, u32[]{:S(2)}) %collective-permute-start.45) | collective-permute-done | bytes 786464 | tf_op jit(solution)/shard_map/ppermute | solution.py:1111
  448.3 18.1 %collective-permute-start.57 = (f32[6,1024]{1,0:T(8,128)S(1)}, f32[6,1024]{1,0:T(8,128)S(1)}, u32[]{:S(2)}, u32[]{:S(2)}) collective-permute-start(f32[6,1024]{1,0:T(8,128)S(1)} %add.134), channel_id=1, source_target_pairs={{0,1},{1,0},{2,3},{3,2},{4,5},{5,4},{6,7},{7,6},{8,9},{9,8},{10,11... | collective-permute-start | bytes 73736 | tf_op jit(solution)/shard_map/ppermute | solution.py:1279
  (301 shorter events, 156.5 us)
Async XLA Ops:
  7.2 115.9 %all-gather.5.cloned.1.call-start = ((), (), s32[]{:S(2)}) async-start(), calls=%async_computation.6 | async-start | bytes 4718592 | tf_op jit(solution)/shard_map/all_gather | solution.py:917
  11.8 173.1 %all-gather.7.cloned.1.call-start = ((), (), s32[]{:S(2)}) async-start(), calls=%async_computation.7 | async-start | bytes 1769472 | tf_op jit(solution)/shard_map/all_gather | solution.py:974
  33.3 37.6 %collective-permute-start.3 = (bf16[2,768,512]{2,1,0:T(8,128)(2,1)S(1)}, bf16[2,768,512]{2,1,0:T(8,128)(2,1)}, u32[]{:S(2)}, u32[]{:S(2)}) collective-permute-start(bf16[2,768,512]{2,1,0:T(8,128)(2,1)S(1)} %get-tuple-element.164.refs_0_.refs_4_), channel_id=1, source_target_pairs={{0,8},{4,12},{8,0},{12,4},{1,9},{5,13},{9,1},{13,5},{2,10},{6,14},... | collective-permute-start | bytes 4718600 | tf_op jit(solution)/shard_map/ppermute | solution.py:775
  38.7 32.2 %collective-permute-start.5 = (bf16[256,512]{1,0:T(8,128)(2,1)S(1)}, bf16[256,512]{1,0:T(8,128)(2,1)S(1)}, u32[]{:S(2)}, u32[]{:S(2)}) collective-permute-start(bf16[256,512]{1,0:T(8,128)(2,1)S(1)} %copy-done.39), channel_id=1, source_target_pairs={{0,2},{1,3},{2,0},{3,1},{4,6},{5,7},{6,4},{7,5},{8,10},{9,11},{10,... | collective-permute-start | bytes 786440 | tf_op jit(solution)/shard_map/ppermute | solution.py:778
  38.7 32.2 %collective-permute-start.6 = (bf16[256,512]{1,0:T(8,128)(2,1)S(1)}, bf16[256,512]{1,0:T(8,128)(2,1)S(1)}, u32[]{:S(2)}, u32[]{:S(2)}) collective-permute-start(bf16[256,512]{1,0:T(8,128)(2,1)S(1)} %copy-done.39), channel_id=1, source_target_pairs={{0,1},{1,2},{2,3},{3,0},{4,5},{5,6},{6,7},{7,4},{8,9},{9,10},{10,1... | collective-permute-start | bytes 786440 | tf_op jit(solution)/shard_map/ppermute | solution.py:778
  41.7 34.5 %collective-permute-start.2 = (bf16[2,768,512]{2,1,0:T(8,128)(2,1)S(1)}, bf16[2,768,512]{2,1,0:T(8,128)(2,1)}, u32[]{:S(2)}, u32[]{:S(2)}) collective-permute-start(bf16[2,768,512]{2,1,0:T(8,128)(2,1)S(1)} %get-tuple-element.164.refs_0_.refs_4_), channel_id=1, source_target_pairs={{0,4},{4,0},{8,12},{12,8},{1,5},{5,1},{9,13},{13,9},{2,6},{6,2},{1... | collective-permute-start | bytes 4718600 | tf_op jit(solution)/shard_map/ppermute | solution.py:775
  73.0 35.4 %collective-permute-start.10 = (bf16[4,256,512]{2,1,0:T(8,128)(2,1)S(1)}, bf16[4,256,512]{2,1,0:T(8,128)(2,1)}, u32[]{:S(2)}, u32[]{:S(2)}) collective-permute-start(bf16[4,256,512]{2,1,0:T(8,128)(2,1)S(1)} %pad_maximum_fusion), channel_id=1, source_target_pairs={{0,16},{16,0},{1,17},{17,1},{2,18},{18,2},{3,19},{19,3},{4,20},{20... | collective-permute-start | bytes 3145736 | tf_op jit(solution)/shard_map/ppermute | solution.py:772
  138.2 106.8 %reduce-scatter.4.cloned.1.call-start = ((), (), s32[]{:S(2)}) async-start(), calls=%async_computation.3 | async-start | bytes 6291456 | tf_op jit(solution)/shard_map/reduce_scatter | solution.py:1141
  155.7 29.3 %collective-permute-start.20 = (bf16[320,1024]{1,0:T(8,128)(2,1)S(1)}, bf16[320,1024]{1,0:T(8,128)(2,1)S(1)}, u32[]{:S(2)}, u32[]{:S(2)}) collective-permute-start(bf16[320,1024]{1,0:T(8,128)(2,1)S(1)} %add_convert_fusion.2), channel_id=1, source_target_pairs={{0,8},{4,12},{8,0},{12,4},{1,9},{5,13},{9,1},{13,5},{2,10},{6,14},... | collective-permute-start | bytes 1966088 | tf_op jit(solution)/shard_map/ppermute | solution.py:775
  185.7 158.4 %reduce-scatter.6.cloned.1.call-start = ((), (), s32[]{:S(2)}) async-start(), calls=%async_computation.4 | async-start | bytes 2621440 | tf_op jit(solution)/shard_map/reduce_scatter | solution.py:1148
  199.6 44.4 %collective-permute-start.27 = (bf16[8,128,768]{2,1,0:T(8,128)(2,1)}, bf16[8,128,768]{2,1,0:T(8,128)(2,1)}, u32[]{:S(2)}, u32[]{:S(2)}) collective-permute-start(bf16[8,128,768]{2,1,0:T(8,128)(2,1)} %bitcast.19.refs_4_), channel_id=1, source_target_pairs={{0,8},{4,12},{8,0},{12,4},{1,9},{5,13},{9,1},{13,5},{2,10},{6,14},... | collective-permute-start | bytes 4718600 | tf_op jit(solution)/shard_map/ppermute | solution.py:775
  211.7 29.5 %collective-permute-start.28 = (bf16[2,160,1024]{2,1,0:T(8,128)(2,1)S(1)}, bf16[2,160,1024]{2,1,0:T(8,128)(2,1)S(1)}, u32[]{:S(2)}, u32[]{:S(2)}) collective-permute-start(bf16[2,160,1024]{2,1,0:T(8,128)(2,1)S(1)} %bitcast.77), channel_id=1, source_target_pairs={{0,1},{1,2},{2,3},{4,5},{5,6},{6,7},{8,9},{9,10},{10,11},{12,13},{... | collective-permute-start | bytes 1966088 | tf_op jit(solution)/shard_map/ppermute | solution.py:1111
  245.0 150.8 %reduce-scatter.8.cloned.1.call-start = ((), (), s32[]{:S(2)}) async-start(), calls=%async_computation.5 | async-start | bytes 327680 | tf_op jit(solution)/shard_map/reduce_scatter | solution.py:1171
  254.4 77.5 %collective-permute-start.31 = (bf16[2,2,768,256]{3,2,1,0:T(8,128)(2,1)}, bf16[2,2,768,256]{3,2,1,0:T(8,128)(2,1)}, u32[]{:S(2)}, u32[]{:S(2)}) collective-permute-start(bf16[2,2,768,256]{3,2,1,0:T(8,128)(2,1)} %fusion), channel_id=1, source_target_pairs={{0,8},{4,12},{8,0},{12,4},{1,9},{5,13},{9,1},{13,5},{2,10},{6,14},... | collective-permute-start | bytes 4718600 | tf_op jit(solution)/shard_map/ppermute | solution.py:775
  255.9 76.0 %collective-permute-start.34 = (bf16[8,128,768]{2,1,0:T(8,128)(2,1)}, bf16[8,128,768]{2,1,0:T(8,128)(2,1)}, u32[]{:S(2)}, u32[]{:S(2)}) collective-permute-start(bf16[8,128,768]{2,1,0:T(8,128)(2,1)} %bitcast.19.refs_4_), channel_id=1, source_target_pairs={{0,4},{4,0},{8,12},{12,8},{1,5},{5,1},{9,13},{13,9},{2,6},{6,2},{1... | collective-permute-start | bytes 4718600 | tf_op jit(solution)/shard_map/ppermute | solution.py:775
  255.9 76.0 %collective-permute-start.35 = (bf16[8,128,768]{2,1,0:T(8,128)(2,1)}, bf16[8,128,768]{2,1,0:T(8,128)(2,1)}, u32[]{:S(2)}, u32[]{:S(2)}) collective-permute-start(bf16[8,128,768]{2,1,0:T(8,128)(2,1)} %collective-permute-done.27.refs_5_), channel_id=1, source_target_pairs={{0,4},{4,0},{8,12},{12,8},{1,5},{5,1},{9,13},{13,9},{2,6},{6,2},{1... | collective-permute-start | bytes 4718600 | tf_op jit(solution)/shard_map/ppermute | solution.py:775
  256.5 58.6 %collective-permute-start.36 = (bf16[2,160,1024]{2,1,0:T(8,128)(2,1)S(1)}, bf16[2,160,1024]{2,1,0:T(8,128)(2,1)}, u32[]{:S(2)}, u32[]{:S(2)}) collective-permute-start(bf16[2,160,1024]{2,1,0:T(8,128)(2,1)S(1)} %bitcast.79), channel_id=1, source_target_pairs={{0,2},{1,3},{2,0},{3,1},{4,6},{5,7},{6,4},{7,5},{8,10},{9,11},{10,... | collective-permute-start | bytes 1966088 | tf_op jit(solution)/shard_map/ppermute | solution.py:1131
  261.6 53.5 %collective-permute-start.32 = (bf16[2,4,64,512]{3,2,1,0:T(8,128)(2,1)S(1)}, bf16[2,4,64,512]{3,2,1,0:T(8,128)(2,1)S(1)}, u32[]{:S(2)}, u32[]{:S(2)}) collective-permute-start(bf16[2,4,64,512]{3,2,1,0:T(8,128)(2,1)S(1)} %dynamic-slice_convert_fusion), channel_id=1, source_target_pairs={{0,16},{16,0},{1,17},{17,1},{2,18},{18,2},{3,19},{19,3},{4,20},{20... | collective-permute-start | bytes 1572872 | tf_op jit(solution)/shard_map/ppermute | solution.py:772
  337.9 57.9 %collective-permute-start.39 = (bf16[3,2,192,256]{3,2,1,0:T(8,128)(2,1)}, bf16[3,2,192,256]{3,2,1,0:T(8,128)(2,1)}, u32[]{:S(2)}, u32[]{:S(2)}) collective-permute-start(bf16[3,2,192,256]{3,2,1,0:T(8,128)(2,1)} %get-tuple-element.263), channel_id=1, source_target_pairs={{0,3},{1,0},{2,1},{3,2},{4,7},{5,4},{6,5},{7,6},{8,11},{9,8},{10,9... | collective-permute-start | bytes 1769480 | tf_op jit(solution)/shard_map/ppermute | solution.py:778
  339.3 56.5 %collective-permute-start.40 = (bf16[3,2,192,256]{3,2,1,0:T(8,128)(2,1)}, bf16[3,2,192,256]{3,2,1,0:T(8,128)(2,1)}, u32[]{:S(2)}, u32[]{:S(2)}) collective-permute-start(bf16[3,2,192,256]{3,2,1,0:T(8,128)(2,1)} %get-tuple-element.264), channel_id=1, source_target_pairs={{0,2},{1,3},{2,0},{3,1},{4,6},{5,7},{6,4},{7,5},{8,10},{9,11},{10,... | collective-permute-start | bytes 1769480 | tf_op jit(solution)/shard_map/ppermute | solution.py:778
  339.7 56.1 %collective-permute-start.41 = (bf16[3,2,192,256]{3,2,1,0:T(8,128)(2,1)}, bf16[3,2,192,256]{3,2,1,0:T(8,128)(2,1)}, u32[]{:S(2)}, u32[]{:S(2)}) collective-permute-start(bf16[3,2,192,256]{3,2,1,0:T(8,128)(2,1)} %get-tuple-element.265), channel_id=1, source_target_pairs={{0,1},{1,2},{2,3},{3,0},{4,5},{5,6},{6,7},{7,4},{8,9},{9,10},{10,1... | collective-permute-start | bytes 1769480 | tf_op jit(solution)/shard_map/ppermute | solution.py:778
  344.2 51.6 %collective-permute-start.38 = (bf16[1024,256]{1,0:T(8,128)(2,1)}, bf16[1024,256]{1,0:T(8,128)(2,1)S(1)}, u32[]{:S(2)}, u32[]{:S(2)}) collective-permute-start(bf16[1024,256]{1,0:T(8,128)(2,1)} %bitcast.83), channel_id=1, source_target_pairs={{0,8},{4,12},{8,0},{12,4},{1,9},{5,13},{9,1},{13,5},{2,10},{6,14},... | collective-permute-start | bytes 1572872 | tf_op jit(solution)/shard_map/ppermute | solution.py:775
  415.2 56.1 %collective-permute-start.47 = (bf16[2,192,1024]{2,1,0:T(8,128)(2,1)}, bf16[2,192,1024]{2,1,0:T(8,128)(2,1)}, u32[]{:S(2)}, u32[]{:S(2)}) collective-permute-start(bf16[2,192,1024]{2,1,0:T(8,128)(2,1)} %get-tuple-element.283.refs_2_), channel_id=1, source_target_pairs={{0,2},{1,3},{2,0},{3,1},{4,6},{5,7},{6,4},{7,5},{8,10},{9,11},{10,... | collective-permute-start | bytes 2359304 | tf_op jit(solution)/shard_map/ppermute | solution.py:1131
  436.7 39.4 %collective-permute-start.49 = (bf16[2,128,768]{2,1,0:T(8,128)(2,1)}, bf16[2,128,768]{2,1,0:T(8,128)(2,1)}, u32[]{:S(2)}, u32[]{:S(2)}) collective-permute-start(bf16[2,128,768]{2,1,0:T(8,128)(2,1)} %fusion.2), channel_id=1, source_target_pairs={{0,8},{4,12},{8,0},{12,4},{1,9},{5,13},{9,1},{13,5},{2,10},{6,14},... | collective-permute-start | bytes 1179656 | tf_op jit(solution)/shard_map/ppermute | solution.py:775
  (100 other events, 1134.5 us)
Sparse Core Ops, SparseCore 0:
  11.9 106.4 all-gather.4
  138.3 46.5 all-gather.6
  187.2 53.1 reduce-scatter.3
  245.2 62.7 reduce-scatter.5
  341.2 54.5 reduce-scatter.7

commit v5 on v4

--- a/solution.py
+++ b/solution.py
@@ -1161,8 +1161,8 @@
         attn_two = jnp.stack([attn_near, attn_mid]) + attn_got.astype(F32)
         attn_two = scatter_f(attn_two, 3)
         attn_end = pc(attn_two[1].astype(BF), 2)
-        kv_end, attn_two, attn_end, all_w, *out_far = gate(
-            kv_end, attn_two, attn_end, all_w, *out_far
+        kv_end, attn_two, attn_end, all_w, out_far[0] = gate(
+            kv_end, attn_two, attn_end, all_w, out_far[0]
         )
         attn_sum = (attn_two[0] + attn_end.astype(F32)).astype(BF)
         attn_sum = lax.dynamic_slice_in_dim(

time: 505 us -> 491 us (0.972)
  waiting for transfers between devices: 238 us -> 221 us
    ppermute x2, waiting for transfers between devices: 52.6 us -> 38.5 us  [swap(): return lax.ppermute(x, 'tensor', pairs + [(b, a) for a, b in pairs])]
    ppermute x5, waiting for transfers between devices: 30.9 us -> 41.3 us  [px(): return lax.ppermute(x, 'fsdp', [(0, 1), (1, 0)])]
    ppermute x32, waiting for transfers between devices: 39.8 us -> 32.7 us  [pc(): return lax.ppermute(x, 'context', [(a, a ^ k) for a in range(nc)])]
    unnamed x122 -> x124, local copies, waits for them, and re-layouts: 12.1 us -> 12.8 us
  transfers between devices with their start and end apart: 64 -> 64, of which waited for: 27 -> 27; matrix products, arithmetic and copies ran while one was open for 5% -> 6% of each run, Pallas kernels for 26% -> 27%
where the time goes in v5:
time: 491 us; the launch traced here: 490 us
  waiting for transfers between devices  221 us (45%)
  Pallas kernels  133 us (27%)
  starting transfers between devices  76.1 us (15%)
  local copies, waits for them, and re-layouts  24.7 us (5%)
  other arithmetic  20.2 us (4%)
  between operations  14.6 us (3%)
    pallas_call x10, Pallas kernels, run(): return kernel(*args[:prefetch], *rest)  113 us
    ppermute x5, waiting for transfers between devices, px(): return lax.ppermute(x, 'fsdp', [(0, 1), (1, 0)])  41.3 us
    ppermute x2, waiting for transfers between devices, swap(): return lax.ppermute(x, 'tensor', pairs + [(b, a) for a, b in pairs])  38.5 us
    reduce_scatter x1, waiting for transfers between devices, on_device(): lax.psum_scatter(attn_sum, 'tensor', scatter_dimension=0, tiled=True)[0]  36.9 us
    ppermute x9, waiting for transfers between devices, pz(): return lax.ppermute(x, 'tensor', [(a, (a - j) % nt) for a in range(nt)])  36 us
    ppermute x32, waiting for transfers between devices, pc(): return lax.ppermute(x, 'context', [(a, a ^ k) for a in range(nc)])  32.7 us
    ppermute x2, starting transfers between devices, on_device(): sums = sums + lax.ppermute(sums, 'tensor', [(a, a ^ k) for a in range(nt)])  18.4 us
    ppermute x32, starting transfers between devices, pc(): return lax.ppermute(x, 'context', [(a, a ^ k) for a in range(nc)])  17.1 us
  transfers between devices with their start and end apart: 64, of which 27 were waited for; matrix products, arithmetic and copies ran while one was open for 6% of the time, Pallas kernels for 27%

profile of v5, /device:TPU:0, one launch (start us, length us, event | category | flops | bytes accessed | tf_op | source)
XLA Modules:
  0.0 489.5 jit_solution(3436202133285624235)
XLA Ops:
  14.9 9.0 %collective-permute-done.refs_3_ = bf16[256,768]{1,0:T(8,128)(2,1)S(1)} collective-permute-done((bf16[256,768]{1,0:T(8,128)(2,1)S(1)}, bf16[256,768]{1,0:T(8,128)(2,1)S(1)}, u32[]{:S(2)}, u32[]{:S(2)}) %collective-permute-start) | collective-permute-done | bytes 393248 | tf_op jit(solution)/shard_map/ppermute | solution.py:772
  41.7 6.5 %collective-permute-done.4.refs_5_.refs_1_ = bf16[256,512]{1,0:T(8,128)(2,1)S(1)} collective-permute-done((bf16[256,512]{1,0:T(8,128)(2,1)S(1)}, bf16[256,512]{1,0:T(8,128)(2,1)S(1)}, u32[]{:S(2)}, u32[]{:S(2)}) %collective-permute-start.4) | collective-permute-done | bytes 262176 | tf_op jit(solution)/shard_map/ppermute | solution.py:778
  48.2 22.6 %collective-permute-done.5.refs_6_.refs_2_ = bf16[256,512]{1,0:T(8,128)(2,1)S(1)} collective-permute-done((bf16[256,512]{1,0:T(8,128)(2,1)S(1)}, bf16[256,512]{1,0:T(8,128)(2,1)S(1)}, u32[]{:S(2)}, u32[]{:S(2)}) %collective-permute-start.5) | collective-permute-done | bytes 262176 | tf_op jit(solution)/shard_map/ppermute | solution.py:778
  76.2 13.8 %attend.1 = (bf16[2,160,256]{2,1,0:T(8,128)(2,1)}, bf16[2,160,256]{2,1,0:T(8,128)(2,1)}, bf16[2,160,256]{2,1,0:T(8,128)(2,1)}, bf16[2,160,256]{2,1,0:T(8,128)(2,1)}, f32[2,2,8,640]{3,2,1,0:T(8,128)}) custom-call(s32[2,20]{1,0:T(2,128)S(1)} %copy-done.22, s32[2,5]{1,0:T(2,128)S(1)} %copy-done.23, s32[3]{0:T(128)S(1)} %pad_add_fusion.pos.pos_ref, ...), custom_call_target="tpu_custom_call" | custom-call | flops 16000000000 | bytes 48000000 | tf_op jit(solution)/shard_map/attend/pallas_call | solution.py:294
  94.1 14.3 %collective-permute-done.10.refs_8_.refs_4_ = bf16[4,256,512]{2,1,0:T(8,128)(2,1)} collective-permute-done((bf16[4,256,512]{2,1,0:T(8,128)(2,1)S(1)}, bf16[4,256,512]{2,1,0:T(8,128)(2,1)}, u32[]{:S(2)}, u32[]{:S(2)}) %collective-permute-start.10) | collective-permute-done | bytes 1048608 | tf_op jit(solution)/shard_map/ppermute | solution.py:772
  108.4 6.8 %collective-permute-done.11.refs_2_ = bf16[2,160,256]{2,1,0:T(8,128)(2,1)S(1)} collective-permute-done((bf16[2,160,256]{2,1,0:T(8,128)(2,1)}, bf16[2,160,256]{2,1,0:T(8,128)(2,1)S(1)}, u32[]{:S(2)}, u32[]{:S(2)}) %collective-permute-start.11) | collective-permute-done | bytes 163872 | tf_op jit(solution)/shard_map/ppermute | solution.py:778
  115.9 4.8 mix.1
  123.9 10.8 %feed.2 = (bf16[320,1024]{1,0:T(8,128)(2,1)}, bf16[320,1024]{1,0:T(8,128)(2,1)}, bf16[2,320,1024]{2,1,0:T(8,128)(2,1)}, bf16[2,320,1024]{2,1,0:T(8,128)(2,1)}) custom-call(bf16[320,1024]{1,0:T(8,128)(2,1)} %bitcast.105, bf16[320,1024]{1,0:T(8,128)(2,1)} %copy-done.48, bf16[320,1024]{1,0:T(8,128)(2,1)} %bitcast.5.refs_2_.refs_4_, ...), custom_call_target="tpu_custom_call" | custom-call | flops 8999999488 | bytes 27000000 | tf_op jit(solution)/shard_map/feed/pallas_call | solution.py:294
  141.1 10.8 %feed.3 = (bf16[320,1024]{1,0:T(8,128)(2,1)}, bf16[320,1024]{1,0:T(8,128)(2,1)}, bf16[2,320,1024]{2,1,0:T(8,128)(2,1)}, bf16[2,320,1024]{2,1,0:T(8,128)(2,1)}) custom-call(bf16[320,1024]{1,0:T(8,128)(2,1)} %copy-done.49, bf16[320,1024]{1,0:T(8,128)(2,1)} %copy-done.52, bf16[320,1024]{1,0:T(8,128)(2,1)} %collective-permute-done.9.refs_2_.refs_6_, ...), custom_call_target="tpu_custom_call" | custom-call | flops 8999999488 | bytes 27000000 | tf_op jit(solution)/shard_map/feed/pallas_call | solution.py:294
  156.7 17.5 %feed_grads.1 = (bf16[2,4,2,512,256]{4,3,2,1,0:T(8,128)(2,1)}, bf16[2,320,1024]{2,1,0:T(8,128)(2,1)}, bf16[2,320,1024]{2,1,0:T(8,128)(2,1)}) custom-call(bf16[320,1024]{1,0:T(8,128)(2,1)} %bitcast.106, bf16[320,1024]{1,0:T(8,128)(2,1)} %copy-done.48, bf16[320,1024]{1,0:T(8,128)(2,1)} %copy-done.49, bf16[320,1024]{1,0:T(8,128)(2,1)} %copy-done.52, ...), custom_call_target="tpu_custom_call" | custom-call | flops 16000000000 | bytes 48000000 | tf_op jit(solution)/shard_map/feed_grads/pallas_call | solution.py:294
  174.2 10.9 %all-gather.7.cloned.1.call-done = bf16[1024,768]{1,0:T(8,128)(2,1)} async-done(((bf16[128,768]{1,0:T(8,128)(2,1)}), bf16[1024,768]{1,0:T(8,128)(2,1)}) %all-gather.7.cloned.1.call-update) | async-done | bytes 1572880 | tf_op jit(solution)/shard_map/all_gather | solution.py:974
  186.7 6.2 %branch_back.1 = (f32[2,160,1024]{2,1,0:T(8,128)}, bf16[2,160,1024]{2,1,0:T(8,128)(2,1)}, bf16[2,160,256]{2,1,0:T(8,128)(2,1)}, bf16[2,160,256]{2,1,0:T(8,128)(2...) custom-call(s32[3]{0:T(128)S(1)} %pad_add_fusion.pos.pos_ref, ...), custom_call_target="tpu_custom_call" | custom-call | flops 4000000000 | bytes 12000000 | tf_op jit(solution)/shard_map/branch_back/pallas_call | solution.py:294
  203.1 7.8 %collective-permute-done.22 = bf16[320,1024]{1,0:T(8,128)(2,1)S(1)} collective-permute-done((bf16[320,1024]{1,0:T(8,128)(2,1)S(1)}, bf16[320,1024]{1,0:T(8,128)(2,1)S(1)}, u32[]{:S(2)}, u32[]{:S(2)}) %collective-permute-start.22) | collective-permute-done | bytes 655392 | tf_op jit(solution)/shard_map/ppermute | solution.py:775
  217.4 24.0 %attend_back.1 = (bf16[2,160,256]{2,1,0:T(8,128)(2,1)}, bf16[2,160,256]{2,1,0:T(8,128)(2,1)}, bf16[2,160,256]{2,1,0:T(8,128)(2,1)}, bf16[2,160,256]{2,1,0:T(8,12...) custom-call(s32[2,20]{1,0:T(2,128)S(1)} %copy-done.22, ...), custom_call_target="tpu_custom_call" | custom-call | flops 24000000000 | bytes 72000000 | tf_op jit(solution)/shard_map/attend_back/pallas_call | solution.py:294
  245.5 5.7 %collective-permute-done.30.got = bf16[2,2,2,768,256]{4,3,2,1,0:T(8,128)(2,1)} collective-permute-done((bf16[2,2,2,768,256]{4,3,2,1,0:T(8,128)(2,1)}, bf16[2,2,2,768,256]{4,3,2,1,0:T(8,128)(2,1)}, u32[]{:S(2)}, u32[]{:S(2)}) %collective-permute-start.30) | collective-permute-done | bytes 3145760 | tf_op jit(solution)/shard_map/ppermute | solution.py:775
  262.6 10.9 %collective-permute-done.32 = bf16[2,4,64,512]{3,2,1,0:T(8,128)(2,1)S(1)} collective-permute-done((bf16[2,4,64,512]{3,2,1,0:T(8,128)(2,1)S(1)}, bf16[2,4,64,512]{3,2,1,0:T(8,128)(2,1)S(1)}, u32[]{:S(2)}, u32[]{:S(2)}) %collective-permute-start.32) | collective-permute-done | bytes 524320 | tf_op jit(solution)/shard_map/ppermute | solution.py:772
  276.5 38.5 %collective-permute-done.36.refs_3_ = bf16[2,160,1024]{2,1,0:T(8,128)(2,1)S(1)} collective-permute-done((bf16[2,160,1024]{2,1,0:T(8,128)(2,1)S(1)}, bf16[2,160,1024]{2,1,0:T(8,128)(2,1)S(1)}, u32[]{:S(2)}, u32[]{:S(2)}) %collective-permute-start.36) | collective-permute-done | bytes 655392 | tf_op jit(solution)/shard_map/ppermute | solution.py:1131
  315.8 5.9 %combine.1 = (bf16[2,2,768,256]{3,2,1,0:T(8,128)(2,1)}, bf16[3,2,192,256]{3,2,1,0:T(8,128)(2,1)}, bf16[3,2,192,256]{3,2,1,0:T(8,128)(2,1)}, bf16[3,2,192,256]{3,2,1,0:T(8,128)(2,1)}, bf16[3,2,192,256]{3,2,1,0:T(8,128)(2,1)}) custom-call(s32[3]{0:T(128)S(1)} %pad_add_fusion.pos.pos_ref, bf16[2,2,2,768,256]{4,3,2,1,0:T(8,128)(2,1)} %get-tuple-element.232.own, ...), custom_call_target="tpu_custom_call" | custom-call | flops 4000000000 | bytes 12000000 | tf_op jit(solution)/shard_map/combine/pallas_call | solution.py:294
  327.7 5.0 %collective-permute-done.38.refs_4_ = bf16[2,160,1024]{2,1,0:T(8,128)(2,1)S(1)} collective-permute-done((bf16[2,160,1024]{2,1,0:T(8,128)(2,1)S(1)}, bf16[2,160,1024]{2,1,0:T(8,128)(2,1)S(1)}, u32[]{:S(2)}, u32[]{:S(2)}) %collective-permute-start.38) | collective-permute-done | bytes 655392 | tf_op jit(solution)/shard_map/ppermute | solution.py:1157
  336.3 8.3 %qkv_grads.1 = (bf16[2,2,128,768]{3,2,1,0:T(8,128)(2,1)}, f32[2,128,768]{2,1,0:T(8,128)}, f32[2,128,768]{2,1,0:T(8,128)}) custom-call(s32[3]{0:T(128)S(1)} %pad_add_fusion.pos.pos_ref, bf16[2,768,1024]{2,1,0:T(8,128)(2,1)} %copy-done.25, bf16[2,640,256]{2,1,0:T(8,128)(2,1)} %get-tuple-element.226.gq, bf16[2,2,768,256]{3,2,1,0:T(8,128)(2,1)} %get-tuple-element.250.gkv), custom_call_target="tpu_custom_call" | custom-call | flops 8000000000 | bytes 24000000 | tf_op jit(solution)/shard_map/qkv_grads/pallas_call | solution.py:294
  344.6 36.9 %reduce-scatter.8.cloned.1.call-done = bf16[1,64,512]{2,1,0:T(8,128)(2,1)} async-done(((bf16[4,64,512]{2,1,0:T(8,128)(2,1)}), bf16[1,64,512]{2,1,0:T(8,128)(2,1)}) %reduce-scatter.8.cloned.1.call-update) | async-done | bytes 65552 | tf_op jit(solution)/shard_map/reduce_scatter | solution.py:1171
  386.7 10.8 %input_back.1 = (bf16[2,192,1024]{2,1,0:T(8,128)(2,1)}, f32[8,1024]{1,0:T(8,128)}) custom-call(s32[3]{0:T(128)S(1)} %pad_add_fusion.pos.pos_ref, bf16[3,2,192,256]{3,2,1,0:T(8,128)(2,1)} %get-tuple-element.268.refs_0_, bf16[3,2,192,256]{3,2,1,0:T(8,128)(2,1)} %collective-permute-done.39.refs_1_, bf16[3,2,192,256]{3,2,1,0:T(8,128)(2,1)} %collective-permute-done.40.refs_2_, ...), custom_call_target="tpu_custom_call" | custom-call | flops 4000000000 | bytes 12000000 | tf_op jit(solution)/shard_map/input_back/pallas_call | solution.py:294
  406.9 11.0 %collective-permute-done.45.refs_0_ = bf16[2,192,1024]{2,1,0:T(8,128)(2,1)S(1)} collective-permute-done((bf16[2,192,1024]{2,1,0:T(8,128)(2,1)}, bf16[2,192,1024]{2,1,0:T(8,128)(2,1)S(1)}, u32[]{:S(2)}, u32[]{:S(2)}) %collective-permute-start.45) | collective-permute-done | bytes 786464 | tf_op jit(solution)/shard_map/ppermute | solution.py:1111
  434.0 18.4 %collective-permute-start.57 = (f32[6,1024]{1,0:T(8,128)S(1)}, f32[6,1024]{1,0:T(8,128)S(1)}, u32[]{:S(2)}, u32[]{:S(2)}) collective-permute-start(f32[6,1024]{1,0:T(8,128)S(1)} %add.134), channel_id=1, source_target_pairs={{0,1},{1,0},{2,3},{3,2},{4,5},{5,4},{6,7},{7,6},{8,9},{9,8},{10,11... | collective-permute-start | bytes 73736 | tf_op jit(solution)/shard_map/ppermute | solution.py:1279
  (303 shorter events, 157.5 us)
Async XLA Ops:
  7.2 115.9 %all-gather.5.cloned.1.call-start = ((), (), s32[]{:S(2)}) async-start(), calls=%async_computation.6 | async-start | bytes 4718592 | tf_op jit(solution)/shard_map/all_gather | solution.py:917
  11.8 173.3 %all-gather.7.cloned.1.call-start = ((), (), s32[]{:S(2)}) async-start(), calls=%async_computation.7 | async-start | bytes 1769472 | tf_op jit(solution)/shard_map/all_gather | solution.py:974
  33.3 37.6 %collective-permute-start.3 = (bf16[2,768,512]{2,1,0:T(8,128)(2,1)S(1)}, bf16[2,768,512]{2,1,0:T(8,128)(2,1)}, u32[]{:S(2)}, u32[]{:S(2)}) collective-permute-start(bf16[2,768,512]{2,1,0:T(8,128)(2,1)S(1)} %get-tuple-element.163.refs_0_.refs_4_), channel_id=1, source_target_pairs={{0,8},{4,12},{8,0},{12,4},{1,9},{5,13},{9,1},{13,5},{2,10},{6,14},... | collective-permute-start | bytes 4718600 | tf_op jit(solution)/shard_map/ppermute | solution.py:775
  38.7 32.2 %collective-permute-start.5 = (bf16[256,512]{1,0:T(8,128)(2,1)S(1)}, bf16[256,512]{1,0:T(8,128)(2,1)S(1)}, u32[]{:S(2)}, u32[]{:S(2)}) collective-permute-start(bf16[256,512]{1,0:T(8,128)(2,1)S(1)} %copy-done.40), channel_id=1, source_target_pairs={{0,2},{1,3},{2,0},{3,1},{4,6},{5,7},{6,4},{7,5},{8,10},{9,11},{10,... | collective-permute-start | bytes 786440 | tf_op jit(solution)/shard_map/ppermute | solution.py:778
  38.7 32.2 %collective-permute-start.6 = (bf16[256,512]{1,0:T(8,128)(2,1)S(1)}, bf16[256,512]{1,0:T(8,128)(2,1)S(1)}, u32[]{:S(2)}, u32[]{:S(2)}) collective-permute-start(bf16[256,512]{1,0:T(8,128)(2,1)S(1)} %copy-done.40), channel_id=1, source_target_pairs={{0,1},{1,2},{2,3},{3,0},{4,5},{5,6},{6,7},{7,4},{8,9},{9,10},{10,1... | collective-permute-start | bytes 786440 | tf_op jit(solution)/shard_map/ppermute | solution.py:778
  41.7 34.5 %collective-permute-start.2 = (bf16[2,768,512]{2,1,0:T(8,128)(2,1)S(1)}, bf16[2,768,512]{2,1,0:T(8,128)(2,1)}, u32[]{:S(2)}, u32[]{:S(2)}) collective-permute-start(bf16[2,768,512]{2,1,0:T(8,128)(2,1)S(1)} %get-tuple-element.163.refs_0_.refs_4_), channel_id=1, source_target_pairs={{0,4},{4,0},{8,12},{12,8},{1,5},{5,1},{9,13},{13,9},{2,6},{6,2},{1... | collective-permute-start | bytes 4718600 | tf_op jit(solution)/shard_map/ppermute | solution.py:775
  73.0 35.4 %collective-permute-start.10 = (bf16[4,256,512]{2,1,0:T(8,128)(2,1)S(1)}, bf16[4,256,512]{2,1,0:T(8,128)(2,1)}, u32[]{:S(2)}, u32[]{:S(2)}) collective-permute-start(bf16[4,256,512]{2,1,0:T(8,128)(2,1)S(1)} %pad_maximum_fusion), channel_id=1, source_target_pairs={{0,16},{16,0},{1,17},{17,1},{2,18},{18,2},{3,19},{19,3},{4,20},{20... | collective-permute-start | bytes 3145736 | tf_op jit(solution)/shard_map/ppermute | solution.py:772
  138.2 107.0 %reduce-scatter.4.cloned.1.call-start = ((), (), s32[]{:S(2)}) async-start(), calls=%async_computation.3 | async-start | bytes 6291456 | tf_op jit(solution)/shard_map/reduce_scatter | solution.py:1141
  155.6 29.5 %collective-permute-start.20 = (bf16[320,1024]{1,0:T(8,128)(2,1)S(1)}, bf16[320,1024]{1,0:T(8,128)(2,1)S(1)}, u32[]{:S(2)}, u32[]{:S(2)}) collective-permute-start(bf16[320,1024]{1,0:T(8,128)(2,1)S(1)} %add_convert_fusion.2), channel_id=1, source_target_pairs={{0,8},{4,12},{8,0},{12,4},{1,9},{5,13},{9,1},{13,5},{2,10},{6,14},... | collective-permute-start | bytes 1966088 | tf_op jit(solution)/shard_map/ppermute | solution.py:775
  185.9 148.9 %reduce-scatter.6.cloned.1.call-start = ((), (), s32[]{:S(2)}) async-start(), calls=%async_computation.4 | async-start | bytes 2621440 | tf_op jit(solution)/shard_map/reduce_scatter | solution.py:1148
  199.8 44.4 %collective-permute-start.27 = (bf16[8,128,768]{2,1,0:T(8,128)(2,1)}, bf16[8,128,768]{2,1,0:T(8,128)(2,1)}, u32[]{:S(2)}, u32[]{:S(2)}) collective-permute-start(bf16[8,128,768]{2,1,0:T(8,128)(2,1)} %bitcast.19.refs_4_), channel_id=1, source_target_pairs={{0,8},{4,12},{8,0},{12,4},{1,9},{5,13},{9,1},{13,5},{2,10},{6,14},... | collective-permute-start | bytes 4718600 | tf_op jit(solution)/shard_map/ppermute | solution.py:775
  212.0 29.4 %collective-permute-start.28 = (bf16[2,160,1024]{2,1,0:T(8,128)(2,1)S(1)}, bf16[2,160,1024]{2,1,0:T(8,128)(2,1)S(1)}, u32[]{:S(2)}, u32[]{:S(2)}) collective-permute-start(bf16[2,160,1024]{2,1,0:T(8,128)(2,1)S(1)} %bitcast.77), channel_id=1, source_target_pairs={{0,1},{1,2},{2,3},{4,5},{5,6},{6,7},{8,9},{9,10},{10,11},{12,13},{... | collective-permute-start | bytes 1966088 | tf_op jit(solution)/shard_map/ppermute | solution.py:1111
  245.2 136.3 %reduce-scatter.8.cloned.1.call-start = ((), (), s32[]{:S(2)}) async-start(), calls=%async_computation.5 | async-start | bytes 327680 | tf_op jit(solution)/shard_map/reduce_scatter | solution.py:1171
  254.6 60.5 %collective-permute-start.31 = (bf16[2,2,768,256]{3,2,1,0:T(8,128)(2,1)}, bf16[2,2,768,256]{3,2,1,0:T(8,128)(2,1)}, u32[]{:S(2)}, u32[]{:S(2)}) collective-permute-start(bf16[2,2,768,256]{3,2,1,0:T(8,128)(2,1)} %fusion), channel_id=1, source_target_pairs={{0,8},{4,12},{8,0},{12,4},{1,9},{5,13},{9,1},{13,5},{2,10},{6,14},... | collective-permute-start | bytes 4718600 | tf_op jit(solution)/shard_map/ppermute | solution.py:775
  256.1 59.0 %collective-permute-start.34 = (bf16[8,128,768]{2,1,0:T(8,128)(2,1)}, bf16[8,128,768]{2,1,0:T(8,128)(2,1)}, u32[]{:S(2)}, u32[]{:S(2)}) collective-permute-start(bf16[8,128,768]{2,1,0:T(8,128)(2,1)} %bitcast.19.refs_4_), channel_id=1, source_target_pairs={{0,4},{4,0},{8,12},{12,8},{1,5},{5,1},{9,13},{13,9},{2,6},{6,2},{1... | collective-permute-start | bytes 4718600 | tf_op jit(solution)/shard_map/ppermute | solution.py:775
  256.1 59.0 %collective-permute-start.35 = (bf16[8,128,768]{2,1,0:T(8,128)(2,1)}, bf16[8,128,768]{2,1,0:T(8,128)(2,1)}, u32[]{:S(2)}, u32[]{:S(2)}) collective-permute-start(bf16[8,128,768]{2,1,0:T(8,128)(2,1)} %collective-permute-done.27.refs_5_), channel_id=1, source_target_pairs={{0,4},{4,0},{8,12},{12,8},{1,5},{5,1},{9,13},{13,9},{2,6},{6,2},{1... | collective-permute-start | bytes 4718600 | tf_op jit(solution)/shard_map/ppermute | solution.py:775
  260.3 54.8 %collective-permute-start.36 = (bf16[2,160,1024]{2,1,0:T(8,128)(2,1)S(1)}, bf16[2,160,1024]{2,1,0:T(8,128)(2,1)S(1)}, u32[]{:S(2)}, u32[]{:S(2)}) collective-permute-start(bf16[2,160,1024]{2,1,0:T(8,128)(2,1)S(1)} %bitcast.79), channel_id=1, source_target_pairs={{0,2},{1,3},{2,0},{3,1},{4,6},{5,7},{6,4},{7,5},{8,10},{9,11},{10,... | collective-permute-start | bytes 1966088 | tf_op jit(solution)/shard_map/ppermute | solution.py:1131
  275.9 39.2 %collective-permute-start.33 = (bf16[4,64,512]{2,1,0:T(8,128)(2,1)S(1)}, bf16[4,64,512]{2,1,0:T(8,128)(2,1)S(1)}, u32[]{:S(2)}, u32[]{:S(2)}) collective-permute-start(bf16[4,64,512]{2,1,0:T(8,128)(2,1)S(1)} %fusion.7), channel_id=1, source_target_pairs={{0,8},{4,12},{8,0},{12,4},{1,9},{5,13},{9,1},{13,5},{2,10},{6,14},... | collective-permute-start | bytes 786440 | tf_op jit(solution)/shard_map/ppermute | solution.py:775
  321.7 59.8 %collective-permute-start.39 = (bf16[3,2,192,256]{3,2,1,0:T(8,128)(2,1)}, bf16[3,2,192,256]{3,2,1,0:T(8,128)(2,1)}, u32[]{:S(2)}, u32[]{:S(2)}) collective-permute-start(bf16[3,2,192,256]{3,2,1,0:T(8,128)(2,1)} %get-tuple-element.261), channel_id=1, source_target_pairs={{0,3},{1,0},{2,1},{3,2},{4,7},{5,4},{6,5},{7,6},{8,11},{9,8},{10,9... | collective-permute-start | bytes 1769480 | tf_op jit(solution)/shard_map/ppermute | solution.py:778
  323.2 58.3 %collective-permute-start.40 = (bf16[3,2,192,256]{3,2,1,0:T(8,128)(2,1)}, bf16[3,2,192,256]{3,2,1,0:T(8,128)(2,1)}, u32[]{:S(2)}, u32[]{:S(2)}) collective-permute-start(bf16[3,2,192,256]{3,2,1,0:T(8,128)(2,1)} %get-tuple-element.262), channel_id=1, source_target_pairs={{0,2},{1,3},{2,0},{3,1},{4,6},{5,7},{6,4},{7,5},{8,10},{9,11},{10,... | collective-permute-start | bytes 1769480 | tf_op jit(solution)/shard_map/ppermute | solution.py:778
  325.2 56.3 %collective-permute-start.41 = (bf16[3,2,192,256]{3,2,1,0:T(8,128)(2,1)}, bf16[3,2,192,256]{3,2,1,0:T(8,128)(2,1)}, u32[]{:S(2)}, u32[]{:S(2)}) collective-permute-start(bf16[3,2,192,256]{3,2,1,0:T(8,128)(2,1)} %get-tuple-element.263), channel_id=1, source_target_pairs={{0,1},{1,2},{2,3},{3,0},{4,5},{5,6},{6,7},{7,4},{8,9},{9,10},{10,1... | collective-permute-start | bytes 1769480 | tf_op jit(solution)/shard_map/ppermute | solution.py:778
  334.9 46.6 %collective-permute-start.37 = (bf16[1024,256]{1,0:T(8,128)(2,1)}, bf16[1024,256]{1,0:T(8,128)(2,1)S(1)}, u32[]{:S(2)}, u32[]{:S(2)}) collective-permute-start(bf16[1024,256]{1,0:T(8,128)(2,1)} %bitcast.83), channel_id=1, source_target_pairs={{0,8},{4,12},{8,0},{12,4},{1,9},{5,13},{9,1},{13,5},{2,10},{6,14},... | collective-permute-start | bytes 1572872 | tf_op jit(solution)/shard_map/ppermute | solution.py:775
  401.0 56.0 %collective-permute-start.47 = (bf16[2,192,1024]{2,1,0:T(8,128)(2,1)}, bf16[2,192,1024]{2,1,0:T(8,128)(2,1)}, u32[]{:S(2)}, u32[]{:S(2)}) collective-permute-start(bf16[2,192,1024]{2,1,0:T(8,128)(2,1)} %get-tuple-element.281.refs_2_), channel_id=1, source_target_pairs={{0,2},{1,3},{2,0},{3,1},{4,6},{5,7},{6,4},{7,5},{8,10},{9,11},{10,... | collective-permute-start | bytes 2359304 | tf_op jit(solution)/shard_map/ppermute | solution.py:1131
  422.5 39.3 %collective-permute-start.49 = (bf16[2,128,768]{2,1,0:T(8,128)(2,1)}, bf16[2,128,768]{2,1,0:T(8,128)(2,1)}, u32[]{:S(2)}, u32[]{:S(2)}) collective-permute-start(bf16[2,128,768]{2,1,0:T(8,128)(2,1)} %fusion.2), channel_id=1, source_target_pairs={{0,8},{4,12},{8,0},{12,4},{1,9},{5,13},{9,1},{13,5},{2,10},{6,14},... | collective-permute-start | bytes 1179656 | tf_op jit(solution)/shard_map/ppermute | solution.py:775
  (101 other events, 1137.8 us)
Sparse Core Ops, SparseCore 0:
  11.9 106.4 all-gather.4
  138.3 46.7 all-gather.6
  187.4 53.1 reduce-scatter.3
  245.3 61.0 reduce-scatter.5
  327.8 53.6 reduce-scatter.7

commit v6 on v5

--- a/solution.py
+++ b/solution.py
@@ -1213,8 +1213,8 @@
             places = [zi, (zi + 1) % nt, (zi - 1) % nt] + [(zi + j) % nt for j in range(2, nt - 1)]
         (output,) = ordered(blocks, places, (zr,))
         own_y = pc(own, 2)
-        qkv_mid, qkv_own, qkv_far, own_y, output, attn_own, *dqkv = gate(
-            qkv_mid, qkv_own, qkv_far, own_y, output, attn_own, *dqkv
+        qkv_mid, qkv_own, qkv_far, own_y, output, *dqkv = gate(
+            qkv_mid, qkv_own, qkv_far, own_y, output, *dqkv
         )
         qkv_got = pc(qkv_far, 1)
         own_blocks = (own, own_y, pc(own, 1), pc(own_y, 1))

time: 491 us -> 499 us (1.016)
  waiting for transfers between devices: 221 us -> 227 us
    ppermute x9, waiting for transfers between devices: 36 us -> 73.5 us  [pz(): return lax.ppermute(x, 'tensor', [(a, (a - j) % nt) for a in range(nt)])]
    reduce_scatter x1, waiting for transfers between devices: 36.9 us -> 16.7 us  [on_device(): lax.psum_scatter(attn_sum, 'tensor', scatter_dimension=0, tiled=True)[0]]
    ppermute x2, waiting for transfers between devices: 11 us -> 0.01 us  [spread_near(): lax.ppermute(x, 'tensor', [(0, 1), (1, 2), (2, 3)])]
    ppermute x32, waiting for transfers between devices: 32.7 us -> 41.1 us  [pc(): return lax.ppermute(x, 'context', [(a, a ^ k) for a in range(nc)])]
    ppermute x1, waiting for transfers between devices: 5.04 us -> 0.01 us  [on_device(): lax.ppermute(out_far[0], 'tensor', [(2, 3), (1, 0), (3, 2), (0, 1)])]
    unnamed x124 -> x128, local copies, waits for them, and re-layouts: 12.8 us -> 12.9 us
  transfers between devices with their start and end apart: 64 -> 64, of which waited for: 27 -> 24; matrix products, arithmetic and copies ran while one was open for 6% -> 6% of each run, Pallas kernels for 27% -> 26%
where the time goes in v6:
time: 499 us; the launch traced here: 498 us
  waiting for transfers between devices  227 us (45%)
  Pallas kernels  133 us (27%)
  starting transfers between devices  76.6 us (15%)
  local copies, waits for them, and re-layouts  24.8 us (5%)
  other arithmetic  21.7 us (4%)
  between operations  14.6 us (3%)
    pallas_call x10, Pallas kernels, run(): return kernel(*args[:prefetch], *rest)  113 us
    ppermute x9, waiting for transfers between devices, pz(): return lax.ppermute(x, 'tensor', [(a, (a - j) % nt) for a in range(nt)])  73.5 us
    ppermute x32, waiting for transfers between devices, pc(): return lax.ppermute(x, 'context', [(a, a ^ k) for a in range(nc)])  41.1 us
    ppermute x5, waiting for transfers between devices, px(): return lax.ppermute(x, 'fsdp', [(0, 1), (1, 0)])  40.9 us
    ppermute x2, waiting for transfers between devices, swap(): return lax.ppermute(x, 'tensor', pairs + [(b, a) for a, b in pairs])  40.2 us
    ppermute x2, starting transfers between devices, on_device(): sums = sums + lax.ppermute(sums, 'tensor', [(a, a ^ k) for a in range(nt)])  18.6 us
    reduce_scatter x1, waiting for transfers between devices, on_device(): lax.psum_scatter(attn_sum, 'tensor', scatter_dimension=0, tiled=True)[0]  16.7 us
    ppermute x32, starting transfers between devices, pc(): return lax.ppermute(x, 'context', [(a, a ^ k) for a in range(nc)])  16.5 us
  transfers between devices with their start and end apart: 64, of which 24 were waited for; matrix products, arithmetic and copies ran while one was open for 6% of the time, Pallas kernels for 26%

profile of v6, /device:TPU:0, one launch (start us, length us, event | category | flops | bytes accessed | tf_op | source)
XLA Modules:
  0.0 497.8 jit_solution(3859852233767628586)
XLA Ops:
  14.9 9.0 %collective-permute-done.refs_3_ = bf16[256,768]{1,0:T(8,128)(2,1)S(1)} collective-permute-done((bf16[256,768]{1,0:T(8,128)(2,1)S(1)}, bf16[256,768]{1,0:T(8,128)(2,1)S(1)}, u32[]{:S(2)}, u32[]{:S(2)}) %collective-permute-start) | collective-permute-done | bytes 393248 | tf_op jit(solution)/shard_map/ppermute | solution.py:772
  41.6 6.6 %collective-permute-done.4.refs_5_.refs_1_ = bf16[256,512]{1,0:T(8,128)(2,1)S(1)} collective-permute-done((bf16[256,512]{1,0:T(8,128)(2,1)S(1)}, bf16[256,512]{1,0:T(8,128)(2,1)S(1)}, u32[]{:S(2)}, u32[]{:S(2)}) %collective-permute-start.4) | collective-permute-done | bytes 262176 | tf_op jit(solution)/shard_map/ppermute | solution.py:778
  48.2 22.6 %collective-permute-done.5.refs_6_.refs_2_ = bf16[256,512]{1,0:T(8,128)(2,1)S(1)} collective-permute-done((bf16[256,512]{1,0:T(8,128)(2,1)S(1)}, bf16[256,512]{1,0:T(8,128)(2,1)S(1)}, u32[]{:S(2)}, u32[]{:S(2)}) %collective-permute-start.5) | collective-permute-done | bytes 262176 | tf_op jit(solution)/shard_map/ppermute | solution.py:778
  76.1 13.8 %attend.1 = (bf16[2,160,256]{2,1,0:T(8,128)(2,1)}, bf16[2,160,256]{2,1,0:T(8,128)(2,1)}, bf16[2,160,256]{2,1,0:T(8,128)(2,1)}, bf16[2,160,256]{2,1,0:T(8,128)(2,1)}, f32[2,2,8,640]{3,2,1,0:T(8,128)}) custom-call(s32[2,20]{1,0:T(2,128)S(1)} %copy-done.24, s32[2,5]{1,0:T(2,128)S(1)} %copy-done.25, s32[3]{0:T(128)S(1)} %pad_add_fusion.pos.pos_ref, ...), custom_call_target="tpu_custom_call" | custom-call | flops 16000000000 | bytes 48000000 | tf_op jit(solution)/shard_map/attend/pallas_call | solution.py:294
  94.0 14.4 %collective-permute-done.10.refs_8_.refs_4_ = bf16[4,256,512]{2,1,0:T(8,128)(2,1)} collective-permute-done((bf16[4,256,512]{2,1,0:T(8,128)(2,1)S(1)}, bf16[4,256,512]{2,1,0:T(8,128)(2,1)}, u32[]{:S(2)}, u32[]{:S(2)}) %collective-permute-start.10) | collective-permute-done | bytes 1048608 | tf_op jit(solution)/shard_map/ppermute | solution.py:772
  108.4 6.7 %collective-permute-done.11.refs_2_ = bf16[2,160,256]{2,1,0:T(8,128)(2,1)S(1)} collective-permute-done((bf16[2,160,256]{2,1,0:T(8,128)(2,1)}, bf16[2,160,256]{2,1,0:T(8,128)(2,1)S(1)}, u32[]{:S(2)}, u32[]{:S(2)}) %collective-permute-start.11) | collective-permute-done | bytes 163872 | tf_op jit(solution)/shard_map/ppermute | solution.py:778
  123.9 10.8 %feed.2 = (bf16[320,1024]{1,0:T(8,128)(2,1)}, bf16[320,1024]{1,0:T(8,128)(2,1)}, bf16[2,320,1024]{2,1,0:T(8,128)(2,1)}, bf16[2,320,1024]{2,1,0:T(8,128)(2,1)}) custom-call(bf16[320,1024]{1,0:T(8,128)(2,1)} %bitcast.105, bf16[320,1024]{1,0:T(8,128)(2,1)} %copy-done.49, bf16[320,1024]{1,0:T(8,128)(2,1)} %bitcast.5.refs_2_.refs_4_, ...), custom_call_target="tpu_custom_call" | custom-call | flops 8999999488 | bytes 27000000 | tf_op jit(solution)/shard_map/feed/pallas_call | solution.py:294
  141.0 10.9 %feed.3 = (bf16[320,1024]{1,0:T(8,128)(2,1)}, bf16[320,1024]{1,0:T(8,128)(2,1)}, bf16[2,320,1024]{2,1,0:T(8,128)(2,1)}, bf16[2,320,1024]{2,1,0:T(8,128)(2,1)}) custom-call(bf16[320,1024]{1,0:T(8,128)(2,1)} %copy-done.50, bf16[320,1024]{1,0:T(8,128)(2,1)} %copy-done.53, bf16[320,1024]{1,0:T(8,128)(2,1)} %collective-permute-done.9.refs_2_.refs_6_, ...), custom_call_target="tpu_custom_call" | custom-call | flops 8999999488 | bytes 27000000 | tf_op jit(solution)/shard_map/feed/pallas_call | solution.py:294
  156.6 17.6 %feed_grads.1 = (bf16[2,4,2,512,256]{4,3,2,1,0:T(8,128)(2,1)}, bf16[2,320,1024]{2,1,0:T(8,128)(2,1)}, bf16[2,320,1024]{2,1,0:T(8,128)(2,1)}) custom-call(bf16[320,1024]{1,0:T(8,128)(2,1)} %bitcast.106, bf16[320,1024]{1,0:T(8,128)(2,1)} %copy-done.49, bf16[320,1024]{1,0:T(8,128)(2,1)} %copy-done.50, bf16[320,1024]{1,0:T(8,128)(2,1)} %copy-done.53, ...), custom_call_target="tpu_custom_call" | custom-call | flops 16000000000 | bytes 48000000 | tf_op jit(solution)/shard_map/feed_grads/pallas_call | solution.py:294
  174.2 10.9 %all-gather.7.cloned.1.call-done = bf16[1024,768]{1,0:T(8,128)(2,1)} async-done(((bf16[128,768]{1,0:T(8,128)(2,1)}), bf16[1024,768]{1,0:T(8,128)(2,1)}) %all-gather.7.cloned.1.call-update) | async-done | bytes 1572880 | tf_op jit(solution)/shard_map/all_gather | solution.py:974
  186.6 6.2 %branch_back.1 = (f32[2,160,1024]{2,1,0:T(8,128)}, bf16[2,160,1024]{2,1,0:T(8,128)(2,1)}, bf16[2,160,256]{2,1,0:T(8,128)(2,1)}, bf16[2,160,256]{2,1,0:T(8,128)(2...) custom-call(s32[3]{0:T(128)S(1)} %pad_add_fusion.pos.pos_ref, ...), custom_call_target="tpu_custom_call" | custom-call | flops 4000000000 | bytes 12000000 | tf_op jit(solution)/shard_map/branch_back/pallas_call | solution.py:294
  203.1 7.7 %collective-permute-done.22 = bf16[320,1024]{1,0:T(8,128)(2,1)S(1)} collective-permute-done((bf16[320,1024]{1,0:T(8,128)(2,1)S(1)}, bf16[320,1024]{1,0:T(8,128)(2,1)S(1)}, u32[]{:S(2)}, u32[]{:S(2)}) %collective-permute-start.22) | collective-permute-done | bytes 655392 | tf_op jit(solution)/shard_map/ppermute | solution.py:775
  217.4 24.0 %attend_back.1 = (bf16[2,160,256]{2,1,0:T(8,128)(2,1)}, bf16[2,160,256]{2,1,0:T(8,128)(2,1)}, bf16[2,160,256]{2,1,0:T(8,128)(2,1)}, bf16[2,160,256]{2,1,0:T(8,12...) custom-call(s32[2,20]{1,0:T(2,128)S(1)} %copy-done.24, ...), custom_call_target="tpu_custom_call" | custom-call | flops 24000000000 | bytes 72000000 | tf_op jit(solution)/shard_map/attend_back/pallas_call | solution.py:294
  245.5 5.7 %collective-permute-done.30.got = bf16[2,2,2,768,256]{4,3,2,1,0:T(8,128)(2,1)} collective-permute-done((bf16[2,2,2,768,256]{4,3,2,1,0:T(8,128)(2,1)}, bf16[2,2,2,768,256]{4,3,2,1,0:T(8,128)(2,1)}, u32[]{:S(2)}, u32[]{:S(2)}) %collective-permute-start.30) | collective-permute-done | bytes 3145760 | tf_op jit(solution)/shard_map/ppermute | solution.py:775
  262.6 10.9 %collective-permute-done.32 = bf16[2,4,64,512]{3,2,1,0:T(8,128)(2,1)S(1)} collective-permute-done((bf16[2,4,64,512]{3,2,1,0:T(8,128)(2,1)S(1)}, bf16[2,4,64,512]{3,2,1,0:T(8,128)(2,1)S(1)}, u32[]{:S(2)}, u32[]{:S(2)}) %collective-permute-start.32) | collective-permute-done | bytes 524320 | tf_op jit(solution)/shard_map/ppermute | solution.py:772
  274.9 40.2 %collective-permute-done.36.refs_3_ = bf16[2,160,1024]{2,1,0:T(8,128)(2,1)S(1)} collective-permute-done((bf16[2,160,1024]{2,1,0:T(8,128)(2,1)S(1)}, bf16[2,160,1024]{2,1,0:T(8,128)(2,1)S(1)}, u32[]{:S(2)}, u32[]{:S(2)}) %collective-permute-start.36) | collective-permute-done | bytes 655392 | tf_op jit(solution)/shard_map/ppermute | solution.py:1131
  316.7 6.6 %collective-permute-done.33 = bf16[4,64,512]{2,1,0:T(8,128)(2,1)S(1)} collective-permute-done((bf16[4,64,512]{2,1,0:T(8,128)(2,1)S(1)}, bf16[4,64,512]{2,1,0:T(8,128)(2,1)S(1)}, u32[]{:S(2)}, u32[]{:S(2)}) %collective-permute-start.33) | collective-permute-done | bytes 262176 | tf_op jit(solution)/shard_map/ppermute | solution.py:775
  323.4 5.9 %combine.1 = (bf16[2,2,768,256]{3,2,1,0:T(8,128)(2,1)}, bf16[3,2,192,256]{3,2,1,0:T(8,128)(2,1)}, bf16[3,2,192,256]{3,2,1,0:T(8,128)(2,1)}, bf16[3,2,192,256]{3,2,1,0:T(8,128)(2,1)}, bf16[3,2,192,256]{3,2,1,0:T(8,128)(2,1)}) custom-call(s32[3]{0:T(128)S(1)} %pad_add_fusion.pos.pos_ref, bf16[2,2,2,768,256]{4,3,2,1,0:T(8,128)(2,1)} %get-tuple-element.231.own, ...), custom_call_target="tpu_custom_call" | custom-call | flops 4000000000 | bytes 12000000 | tf_op jit(solution)/shard_map/combine/pallas_call | solution.py:294
  336.9 8.3 %qkv_grads.1 = (bf16[2,2,128,768]{3,2,1,0:T(8,128)(2,1)}, f32[2,128,768]{2,1,0:T(8,128)}, f32[2,128,768]{2,1,0:T(8,128)}) custom-call(s32[3]{0:T(128)S(1)} %pad_add_fusion.pos.pos_ref, bf16[2,768,1024]{2,1,0:T(8,128)(2,1)} %copy-done.27, bf16[2,640,256]{2,1,0:T(8,128)(2,1)} %get-tuple-element.225.gq, bf16[2,2,768,256]{3,2,1,0:T(8,128)(2,1)} %get-tuple-element.249.gkv), custom_call_target="tpu_custom_call" | custom-call | flops 8000000000 | bytes 24000000 | tf_op jit(solution)/shard_map/qkv_grads/pallas_call | solution.py:294
  345.2 37.6 %collective-permute-done.40.refs_2_ = bf16[3,2,192,256]{3,2,1,0:T(8,128)(2,1)} collective-permute-done((bf16[3,2,192,256]{3,2,1,0:T(8,128)(2,1)}, bf16[3,2,192,256]{3,2,1,0:T(8,128)(2,1)}, u32[]{:S(2)}, u32[]{:S(2)}) %collective-permute-start.40) | collective-permute-done | bytes 589856 | tf_op jit(solution)/shard_map/ppermute | solution.py:778
  387.8 10.8 %input_back.1 = (bf16[2,192,1024]{2,1,0:T(8,128)(2,1)}, f32[8,1024]{1,0:T(8,128)}) custom-call(s32[3]{0:T(128)S(1)} %pad_add_fusion.pos.pos_ref, bf16[3,2,192,256]{3,2,1,0:T(8,128)(2,1)} %get-tuple-element.265.refs_0_, bf16[3,2,192,256]{3,2,1,0:T(8,128)(2,1)} %copy-done.56, bf16[3,2,192,256]{3,2,1,0:T(8,128)(2,1)} %collective-permute-done.40.refs_2_, ...), custom_call_target="tpu_custom_call" | custom-call | flops 4000000000 | bytes 12000000 | tf_op jit(solution)/shard_map/input_back/pallas_call | solution.py:294
  411.5 16.7 %reduce-scatter.8.cloned.1.call-done = bf16[1,64,512]{2,1,0:T(8,128)(2,1)} async-done(((bf16[4,64,512]{2,1,0:T(8,128)(2,1)}), bf16[1,64,512]{2,1,0:T(8,128)(2,1)}) %reduce-scatter.8.cloned.1.call-update) | async-done | bytes 65552 | tf_op jit(solution)/shard_map/reduce_scatter | solution.py:1171
  442.2 18.6 %collective-permute-start.57 = (f32[6,1024]{1,0:T(8,128)S(1)}, f32[6,1024]{1,0:T(8,128)S(1)}, u32[]{:S(2)}, u32[]{:S(2)}) collective-permute-start(f32[6,1024]{1,0:T(8,128)S(1)} %add.134), channel_id=1, source_target_pairs={{0,1},{1,0},{2,3},{3,2},{4,5},{5,4},{6,7},{7,6},{8,9},{9,8},{10,11... | collective-permute-start | bytes 73736 | tf_op jit(solution)/shard_map/ppermute | solution.py:1279
  480.2 5.2 %collective-permute-done.51.refs_1_ = bf16[128,1024]{1,0:T(8,128)(2,1)S(1)} collective-permute-done((bf16[128,1024]{1,0:T(8,128)(2,1)S(1)}, bf16[128,1024]{1,0:T(8,128)(2,1)S(1)}, u32[]{:S(2)}, u32[]{:S(2)}) %collective-permute-start.51) | collective-permute-done | bytes 262176 | tf_op jit(solution)/shard_map/ppermute | solution.py:775
  (307 shorter events, 155.6 us)
Async XLA Ops:
  7.2 115.8 %all-gather.5.cloned.1.call-start = ((), (), s32[]{:S(2)}) async-start(), calls=%async_computation.6 | async-start | bytes 4718592 | tf_op jit(solution)/shard_map/all_gather | solution.py:917
  11.8 173.3 %all-gather.7.cloned.1.call-start = ((), (), s32[]{:S(2)}) async-start(), calls=%async_computation.7 | async-start | bytes 1769472 | tf_op jit(solution)/shard_map/all_gather | solution.py:974
  33.2 37.6 %collective-permute-start.3 = (bf16[2,768,512]{2,1,0:T(8,128)(2,1)S(1)}, bf16[2,768,512]{2,1,0:T(8,128)(2,1)}, u32[]{:S(2)}, u32[]{:S(2)}) collective-permute-start(bf16[2,768,512]{2,1,0:T(8,128)(2,1)S(1)} %get-tuple-element.162.refs_0_.refs_4_), channel_id=1, source_target_pairs={{0,8},{4,12},{8,0},{12,4},{1,9},{5,13},{9,1},{13,5},{2,10},{6,14},... | collective-permute-start | bytes 4718600 | tf_op jit(solution)/shard_map/ppermute | solution.py:775
  38.6 32.2 %collective-permute-start.5 = (bf16[256,512]{1,0:T(8,128)(2,1)S(1)}, bf16[256,512]{1,0:T(8,128)(2,1)S(1)}, u32[]{:S(2)}, u32[]{:S(2)}) collective-permute-start(bf16[256,512]{1,0:T(8,128)(2,1)S(1)} %copy-done.41), channel_id=1, source_target_pairs={{0,2},{1,3},{2,0},{3,1},{4,6},{5,7},{6,4},{7,5},{8,10},{9,11},{10,... | collective-permute-start | bytes 786440 | tf_op jit(solution)/shard_map/ppermute | solution.py:778
  38.6 32.2 %collective-permute-start.6 = (bf16[256,512]{1,0:T(8,128)(2,1)S(1)}, bf16[256,512]{1,0:T(8,128)(2,1)S(1)}, u32[]{:S(2)}, u32[]{:S(2)}) collective-permute-start(bf16[256,512]{1,0:T(8,128)(2,1)S(1)} %copy-done.41), channel_id=1, source_target_pairs={{0,1},{1,2},{2,3},{3,0},{4,5},{5,6},{6,7},{7,4},{8,9},{9,10},{10,1... | collective-permute-start | bytes 786440 | tf_op jit(solution)/shard_map/ppermute | solution.py:778
  41.6 34.5 %collective-permute-start.2 = (bf16[2,768,512]{2,1,0:T(8,128)(2,1)S(1)}, bf16[2,768,512]{2,1,0:T(8,128)(2,1)}, u32[]{:S(2)}, u32[]{:S(2)}) collective-permute-start(bf16[2,768,512]{2,1,0:T(8,128)(2,1)S(1)} %get-tuple-element.162.refs_0_.refs_4_), channel_id=1, source_target_pairs={{0,4},{4,0},{8,12},{12,8},{1,5},{5,1},{9,13},{13,9},{2,6},{6,2},{1... | collective-permute-start | bytes 4718600 | tf_op jit(solution)/shard_map/ppermute | solution.py:775
  72.9 35.5 %collective-permute-start.10 = (bf16[4,256,512]{2,1,0:T(8,128)(2,1)S(1)}, bf16[4,256,512]{2,1,0:T(8,128)(2,1)}, u32[]{:S(2)}, u32[]{:S(2)}) collective-permute-start(bf16[4,256,512]{2,1,0:T(8,128)(2,1)S(1)} %pad_maximum_fusion), channel_id=1, source_target_pairs={{0,16},{16,0},{1,17},{17,1},{2,18},{18,2},{3,19},{19,3},{4,20},{20... | collective-permute-start | bytes 3145736 | tf_op jit(solution)/shard_map/ppermute | solution.py:772
  94.0 27.9 %collective-permute-start.15 = (bf16[320,1024]{1,0:T(8,128)(2,1)}, bf16[320,1024]{1,0:T(8,128)(2,1)S(1)}, u32[]{:S(2)}, u32[]{:S(2)}) collective-permute-start(bf16[320,1024]{1,0:T(8,128)(2,1)} %bitcast.5.refs_2_.refs_4_), channel_id=1, source_target_pairs={{0,4},{4,0},{8,12},{12,8},{1,5},{5,1},{9,13},{13,9},{2,6},{6,2},{1... | collective-permute-start | bytes 1966088 | tf_op jit(solution)/shard_map/ppermute | solution.py:775
  138.1 107.1 %reduce-scatter.4.cloned.1.call-start = ((), (), s32[]{:S(2)}) async-start(), calls=%async_computation.3 | async-start | bytes 6291456 | tf_op jit(solution)/shard_map/reduce_scatter | solution.py:1141
  155.5 29.6 %collective-permute-start.20 = (bf16[320,1024]{1,0:T(8,128)(2,1)S(1)}, bf16[320,1024]{1,0:T(8,128)(2,1)S(1)}, u32[]{:S(2)}, u32[]{:S(2)}) collective-permute-start(bf16[320,1024]{1,0:T(8,128)(2,1)S(1)} %add_convert_fusion.2), channel_id=1, source_target_pairs={{0,8},{4,12},{8,0},{12,4},{1,9},{5,13},{9,1},{13,5},{2,10},{6,14},... | collective-permute-start | bytes 1966088 | tf_op jit(solution)/shard_map/ppermute | solution.py:775
  185.9 149.2 %reduce-scatter.6.cloned.1.call-start = ((), (), s32[]{:S(2)}) async-start(), calls=%async_computation.4 | async-start | bytes 2621440 | tf_op jit(solution)/shard_map/reduce_scatter | solution.py:1148
  199.8 44.4 %collective-permute-start.27 = (bf16[8,128,768]{2,1,0:T(8,128)(2,1)}, bf16[8,128,768]{2,1,0:T(8,128)(2,1)}, u32[]{:S(2)}, u32[]{:S(2)}) collective-permute-start(bf16[8,128,768]{2,1,0:T(8,128)(2,1)} %bitcast.19.refs_4_), channel_id=1, source_target_pairs={{0,8},{4,12},{8,0},{12,4},{1,9},{5,13},{9,1},{13,5},{2,10},{6,14},... | collective-permute-start | bytes 4718600 | tf_op jit(solution)/shard_map/ppermute | solution.py:775
  211.9 29.4 %collective-permute-start.28 = (bf16[2,160,1024]{2,1,0:T(8,128)(2,1)S(1)}, bf16[2,160,1024]{2,1,0:T(8,128)(2,1)S(1)}, u32[]{:S(2)}, u32[]{:S(2)}) collective-permute-start(bf16[2,160,1024]{2,1,0:T(8,128)(2,1)S(1)} %bitcast.77), channel_id=1, source_target_pairs={{0,1},{1,2},{2,3},{4,5},{5,6},{6,7},{8,9},{9,10},{10,11},{12,13},{... | collective-permute-start | bytes 1966088 | tf_op jit(solution)/shard_map/ppermute | solution.py:1111
  245.2 183.0 %reduce-scatter.8.cloned.1.call-start = ((), (), s32[]{:S(2)}) async-start(), calls=%async_computation.5 | async-start | bytes 327680 | tf_op jit(solution)/shard_map/reduce_scatter | solution.py:1171
  254.6 68.7 %collective-permute-start.31 = (bf16[2,2,768,256]{3,2,1,0:T(8,128)(2,1)}, bf16[2,2,768,256]{3,2,1,0:T(8,128)(2,1)}, u32[]{:S(2)}, u32[]{:S(2)}) collective-permute-start(bf16[2,2,768,256]{3,2,1,0:T(8,128)(2,1)} %fusion), channel_id=1, source_target_pairs={{0,8},{4,12},{8,0},{12,4},{1,9},{5,13},{9,1},{13,5},{2,10},{6,14},... | collective-permute-start | bytes 4718600 | tf_op jit(solution)/shard_map/ppermute | solution.py:775
  256.1 67.2 %collective-permute-start.34 = (bf16[8,128,768]{2,1,0:T(8,128)(2,1)}, bf16[8,128,768]{2,1,0:T(8,128)(2,1)}, u32[]{:S(2)}, u32[]{:S(2)}) collective-permute-start(bf16[8,128,768]{2,1,0:T(8,128)(2,1)} %bitcast.19.refs_4_), channel_id=1, source_target_pairs={{0,4},{4,0},{8,12},{12,8},{1,5},{5,1},{9,13},{13,9},{2,6},{6,2},{1... | collective-permute-start | bytes 4718600 | tf_op jit(solution)/shard_map/ppermute | solution.py:775
  256.1 67.2 %collective-permute-start.35 = (bf16[8,128,768]{2,1,0:T(8,128)(2,1)}, bf16[8,128,768]{2,1,0:T(8,128)(2,1)}, u32[]{:S(2)}, u32[]{:S(2)}) collective-permute-start(bf16[8,128,768]{2,1,0:T(8,128)(2,1)} %collective-permute-done.27.refs_5_), channel_id=1, source_target_pairs={{0,4},{4,0},{8,12},{12,8},{1,5},{5,1},{9,13},{13,9},{2,6},{6,2},{1... | collective-permute-start | bytes 4718600 | tf_op jit(solution)/shard_map/ppermute | solution.py:775
  260.3 54.7 %collective-permute-start.36 = (bf16[2,160,1024]{2,1,0:T(8,128)(2,1)S(1)}, bf16[2,160,1024]{2,1,0:T(8,128)(2,1)S(1)}, u32[]{:S(2)}, u32[]{:S(2)}) collective-permute-start(bf16[2,160,1024]{2,1,0:T(8,128)(2,1)S(1)} %bitcast.79), channel_id=1, source_target_pairs={{0,2},{1,3},{2,0},{3,1},{4,6},{5,7},{6,4},{7,5},{8,10},{9,11},{10,... | collective-permute-start | bytes 1966088 | tf_op jit(solution)/shard_map/ppermute | solution.py:1131
  330.6 52.1 %collective-permute-start.40 = (bf16[3,2,192,256]{3,2,1,0:T(8,128)(2,1)}, bf16[3,2,192,256]{3,2,1,0:T(8,128)(2,1)}, u32[]{:S(2)}, u32[]{:S(2)}) collective-permute-start(bf16[3,2,192,256]{3,2,1,0:T(8,128)(2,1)} %get-tuple-element.259), channel_id=1, source_target_pairs={{0,2},{1,3},{2,0},{3,1},{4,6},{5,7},{6,4},{7,5},{8,10},{9,11},{10,... | collective-permute-start | bytes 1769480 | tf_op jit(solution)/shard_map/ppermute | solution.py:778
  332.5 50.2 %collective-permute-start.41 = (bf16[3,2,192,256]{3,2,1,0:T(8,128)(2,1)}, bf16[3,2,192,256]{3,2,1,0:T(8,128)(2,1)}, u32[]{:S(2)}, u32[]{:S(2)}) collective-permute-start(bf16[3,2,192,256]{3,2,1,0:T(8,128)(2,1)} %get-tuple-element.260), channel_id=1, source_target_pairs={{0,1},{1,2},{2,3},{3,0},{4,5},{5,6},{6,7},{7,4},{8,9},{9,10},{10,1... | collective-permute-start | bytes 1769480 | tf_op jit(solution)/shard_map/ppermute | solution.py:778
  335.1 47.6 %collective-permute-start.37 = (bf16[1024,256]{1,0:T(8,128)(2,1)}, bf16[1024,256]{1,0:T(8,128)(2,1)S(1)}, u32[]{:S(2)}, u32[]{:S(2)}) collective-permute-start(bf16[1024,256]{1,0:T(8,128)(2,1)} %bitcast.83), channel_id=1, source_target_pairs={{0,8},{4,12},{8,0},{12,4},{1,9},{5,13},{9,1},{13,5},{2,10},{6,14},... | collective-permute-start | bytes 1572872 | tf_op jit(solution)/shard_map/ppermute | solution.py:775
  400.2 28.0 %collective-permute-start.45 = (bf16[2,192,1024]{2,1,0:T(8,128)(2,1)}, bf16[2,192,1024]{2,1,0:T(8,128)(2,1)S(1)}, u32[]{:S(2)}, u32[]{:S(2)}) collective-permute-start(bf16[2,192,1024]{2,1,0:T(8,128)(2,1)} %get-tuple-element.278.refs_2_), channel_id=1, source_target_pairs={{0,1},{1,2},{2,3},{4,5},{5,6},{6,7},{8,9},{9,10},{10,11},{12,13},{... | collective-permute-start | bytes 2359304 | tf_op jit(solution)/shard_map/ppermute | solution.py:1111
  403.8 62.1 %collective-permute-start.47 = (bf16[2,192,1024]{2,1,0:T(8,128)(2,1)S(1)}, bf16[2,192,1024]{2,1,0:T(8,128)(2,1)}, u32[]{:S(2)}, u32[]{:S(2)}) collective-permute-start(bf16[2,192,1024]{2,1,0:T(8,128)(2,1)S(1)} %copy-done.2), channel_id=1, source_target_pairs={{0,2},{1,3},{2,0},{3,1},{4,6},{5,7},{6,4},{7,5},{8,10},{9,11},{10,... | collective-permute-start | bytes 2359304 | tf_op jit(solution)/shard_map/ppermute | solution.py:1131
  430.4 40.4 %collective-permute-start.49 = (bf16[2,128,768]{2,1,0:T(8,128)(2,1)}, bf16[2,128,768]{2,1,0:T(8,128)(2,1)}, u32[]{:S(2)}, u32[]{:S(2)}) collective-permute-start(bf16[2,128,768]{2,1,0:T(8,128)(2,1)} %fusion.2), channel_id=1, source_target_pairs={{0,8},{4,12},{8,0},{12,4},{1,9},{5,13},{9,1},{13,5},{2,10},{6,14},... | collective-permute-start | bytes 1179656 | tf_op jit(solution)/shard_map/ppermute | solution.py:775
  (103 other events, 1179.1 us)
Sparse Core Ops, SparseCore 0:
  11.9 106.3 all-gather.4
  138.2 46.8 all-gather.6
  187.4 53.1 reduce-scatter.3
  245.4 60.9 reduce-scatter.5
  403.9 24.2 reduce-scatter.7
